TPU v7x, 256 devices: a whole 4x4x8 slice. The times are simulated.
256 devices in a mesh: cluster: 64 (over x, z, y_lo), camera: 4 (over y_hi, core).
Axes of the slice: x: 4, y: 4 (y_hi: 2, y_lo: 2; y = y_hi * 2 + y_lo), z: 8, core: 2. Of those that a mesh axis runs over, the one named last changes fastest.
Arguments:
- counts: int32 [64], replicated, may hold values from 1 to 16, as said below
- tiles: int32 [1024, 4], replicated, may hold values from 0 to 3
- cam_jac: float32 [1024, 128, 512], P('cluster', None, 'camera'), may hold values from -0.6 to 0.6
- point_jac: float32 [1024, 128, 3, 512], P('cluster', None, None, 'camera'), may hold values from -0.15625 to 0.15625
- point_inv: float32 [1024, 3, 3, 512], P('cluster', None, None, 'camera'), may hold values from -1 to 1, as said below
Outputs:
- reduced: float32 [4, 512, 2048], P('camera', 'cluster')
Inputs may be any that keep to these rules, and one draw needn't show every extreme that they name: For every device i below 32, exactly one of the devices i and i + 32 holds 13 to 16 live clusters and the other 1 to 8; at least 4 devices hold exactly 16. The live clusters of a device are its first counts slots. Every 3x3 block point_inv[c, :, :, p] is symmetric and positive definite.
All inputs are finite; a program needn't handle non-finite values.
Results may differ from a plain program's by a relative error of at most 0.0003.
Values sent between devices are 32-bit elements; how exact they have to be, the bound alone decides.
No kernel may reach another device: no remote copies, remote signals or barrier semaphores. Data moves between devices by JAX's collectives and lax.ppermute only.
A program may use at most 64 MiB of HBM per device.

v0:
```python
import jax
import jax.numpy as jnp
from jax import lax
from jax.sharding import PartitionSpec as P

GT = 4


HIGHEST_PRECISION = lax.Precision.HIGHEST


def contract_rows(left, right):
    return lax.dot_general(
        left,
        right,
        (((0,), (0,)), ((), ())),
        precision=HIGHEST_PRECISION,
        preferred_element_type=jnp.float32,
    )


def on_device(counts, tiles, cam_jac, point_jac, point_inv):
    device = lax.axis_index("cluster")
    camera = lax.axis_index("camera")
    cameras = lax.axis_size("camera")
    slot_count = cam_jac.shape[0]
    tile_width = cam_jac.shape[2]
    slot_ids = jnp.arange(slot_count, dtype=jnp.int32)
    local_live = slot_ids < counts[device]
    local_ids = device * slot_count + slot_ids
    masked = cam_jac * local_live.astype(jnp.float32)[:, None, None]
    full_jac = lax.all_gather(masked, "camera", axis=2, tiled=True)
    item_count = masked.shape[0]
    row_count = masked.shape[1]
    flat_points = point_jac.reshape(item_count, row_count, -1)
    item_tiles = tiles[local_ids]
    group_width = GT * tile_width
    accumulator = jnp.zeros((group_width, group_width * cameras), jnp.float32)
    weighted = jnp.einsum("nrjp,njkp->nrkp", point_jac, point_inv, precision=HIGHEST_PRECISION)
    coupled_local = lax.dot_general(
        weighted.reshape(item_count, row_count, -1),
        flat_points,
        (((2,), (2,)), ((0,), (0,))),
        precision=HIGHEST_PRECISION,
        preferred_element_type=jnp.float32,
    )
    coupled = lax.psum(coupled_local, "camera")

    def schur_rows(item_index):
        full_panel = full_jac[item_index]
        reduced_panel = full_panel - jnp.dot(
            coupled[item_index],
            full_panel,
            precision=HIGHEST_PRECISION,
            preferred_element_type=jnp.float32,
        )
        return contract_rows(masked[item_index], reduced_panel)

    def accumulate(item_index, accumulator):
        rows_block = schur_rows(item_index)
        row_start = item_tiles[item_index, camera] * tile_width
        for group_index in range(cameras):
            col_start = (group_index * GT + item_tiles[item_index, group_index]) * tile_width
            current = lax.dynamic_slice(
                accumulator, (row_start, col_start), (tile_width, tile_width)
            )
            updated = (
                current + rows_block[:, group_index * tile_width : (group_index + 1) * tile_width]
            )
            accumulator = lax.dynamic_update_slice(accumulator, updated, (row_start, col_start))
        return accumulator

    accumulator = lax.fori_loop(0, item_count, accumulate, accumulator)
    summed = lax.psum_scatter(accumulator, "cluster", scatter_dimension=0, tiled=True)
    return summed[None]


def solution(mesh):
    in_specs = (
        P(),
        P(),
        P("cluster", None, "camera"),
        P("cluster", None, None, "camera"),
        P("cluster", None, None, "camera"),
    )
    out_specs = P("camera", "cluster", None)
    return jax.shard_map(
        on_device, mesh=mesh, in_specs=in_specs, out_specs=out_specs, check_vma=False
    )
```

profile of v0, /device:TPU:16, one launch (start us, length us, event | category | flops | bytes accessed | tf_op | source)
XLA Modules:
  0.0 674.7 jit_solution(5375076101356940540)
XLA Ops:
  6.5 5.1 copy.12
  11.7 2.4 copy.14
  14.1 2.6 copy.11
  16.7 16.0 %convolution_bitcast_fusion = f32[16,128,3,128]{1,2,3,0:T(4,128)S(1)} fusion(f32[16,3,3,128]{1,2,3,0:T(4,128)} %copy.11, f32[16,128,3,128]{1,2,3,0:T(4,128)} %copy.12), kind=kOutput, calls=%fused_computation.23 | convolution fusion | flops 28311552 | bytes 6365184 | tf_op jit(solution)/shard_map/nrjp,njkp->nrkp/dot_general | solution.py:39
  34.7 6.2 fusion.14
  44.3 48.5 %all-reduce.2.cloned.1.call-done = f32[16,128,128]{2,1,0:T(8,128)} async-done(((f32[16,128,128]{2,1,0:T(8,128)}), f32[16,128,128]{2,1,0:T(8,128)}) %all-reduce.2.cloned.1.call-update) | async-done | bytes 1048592 | tf_op jit(solution)/shard_map/psum | solution.py:47
  92.8 42.0 %all-gather.2.cloned.1.call-done = f32[16,128,512]{2,1,0:T(8,128)} async-done(((f32[16,128,128]{2,1,0:T(8,128)}), f32[16,128,512]{2,1,0:T(8,128)}) %all-gather.2.cloned.1.call-update) | async-done | bytes 4194320 | tf_op jit(solution)/shard_map/all_gather | solution.py:32
  134.8 2.5 broadcast_in_dim.8
  137.3 202.6 %while.15 = (s32[]{:T(128)}, f32[512,2048]{1,0:T(8,128)}, s32[16,4]{0,1:T(4,128)S(1)}, s32[]{:T(128)}, f32[16,128,128]{2,1,0:T(8,128)}, /*index=5*/f32[16,128,51...) while((s32[]{:T(128)}, f32[512,2048]{1,0:T(8,128)}, ...), condition=%wide.region_2.0_spmd, body=%wide.region_1.0_spmd.sunk | while | flops 201457664 | bytes 1968103 | solution.py:73
  139.3 1.6 convolution_subtract_fusion.2
  142.1 1.5 fusion.34
  144.3 1.5 fusion.35
  152.0 1.6 convolution_subtract_fusion.2
  157.0 1.5 fusion.35
  161.2 1.5 fusion.37
  164.7 1.6 convolution_subtract_fusion.2
  167.5 1.5 fusion.34
  169.6 1.5 fusion.35
  177.3 1.5 convolution_subtract_fusion.2
  180.1 1.5 fusion.34
  189.9 1.6 convolution_subtract_fusion.2
  192.8 1.5 fusion.34
  194.9 1.5 fusion.35
  199.1 1.5 fusion.37
  202.6 1.6 convolution_subtract_fusion.2
  205.4 1.5 fusion.34
  215.2 1.5 convolution_subtract_fusion.2
  227.8 1.5 convolution_subtract_fusion.2
  232.8 1.5 fusion.35
  240.5 1.5 convolution_subtract_fusion.2
  245.4 1.5 fusion.35
  253.1 1.5 convolution_subtract_fusion.2
  262.2 1.5 fusion.37
  265.7 1.6 convolution_subtract_fusion.2
  268.6 1.5 fusion.34
  278.4 1.6 convolution_subtract_fusion.2
  281.3 1.5 fusion.34
  283.5 1.5 fusion.35
  291.1 1.6 convolution_subtract_fusion.2
  296.1 1.5 fusion.35
  303.8 1.5 convolution_subtract_fusion.2
  312.9 1.5 fusion.37
  316.4 1.6 convolution_subtract_fusion.2
  321.4 1.5 fusion.35
  329.1 1.7 convolution_subtract_fusion.2
  332.1 1.5 fusion.34
  338.4 1.5 fusion.37
  339.9 328.2 %reduce-scatter.2.cloned.1.call-done = f32[8,2048]{1,0:T(8,128)} async-done(((f32[512,2048]{1,0:T(8,128)}), f32[8,2048]{1,0:T(8,128)}) %reduce-scatter.2.cloned.1.call-update) | async-done | bytes 65552 | tf_op jit(solution)/shard_map/reduce_scatter | solution.py:74
  (101 shorter events, 98.6 us)
Async XLA Ops:
  6.5 5.1 copy-start
  6.5 86.2 %all-reduce.2.cloned.1.call-start = ((), (), s32[]{:S(2)}) async-start(), calls=%async_computation.2 | async-start | bytes 2097152 | tf_op jit(solution)/shard_map/psum | solution.py:47
  11.7 2.4 copy-start.3
  32.8 1.9 copy-start.1
  34.7 6.2 copy-start.5
  34.7 7.5 %copy-start.2 = (f32[16,128,128]{2,1,0:T(8,128)S(1)}, f32[16,128,128]{2,1,0:T(8,128)}, u32[]{:S(2)}) copy-start(f32[16,128,128]{2,1,0:T(8,128)} %param.9) | copy-start | bytes 3145732
  34.7 8.7 %copy-start.4 = (s32[1024,4]{0,1:T(4,128)S(1)}, s32[1024,4]{0,1:T(4,128)}, u32[]{:S(2)}) copy-start(s32[1024,4]{0,1:T(4,128)} %param.8) | copy-start | bytes 49156
  40.9 94.0 %all-gather.2.cloned.1.call-start = ((), (), s32[]{:S(2)}) async-start(), calls=%async_computation.1 | async-start | bytes 5242880 | tf_op jit(solution)/shard_map/all_gather | solution.py:32
  43.3 624.9 %reduce-scatter.2.cloned.1.call-start = ((), (), s32[]{:S(2)}) async-start(), calls=%async_computation.3 | async-start | bytes 4259840 | tf_op jit(solution)/shard_map/reduce_scatter | solution.py:74
Sparse Core Ops, SparseCore 0:
  41.0 51.7 all-reduce.1
  94.6 40.1 all-gather.1
  340.1 328.0 reduce-scatter.1
where the time goes:
time: 679 us; the launch traced here: 675 us
  waiting for transfers between devices  419 us (62%)
  other arithmetic  97.4 us (14%)
  matrix products  67.5 us (10%)
  loops' own time  51.1 us (8%)
  local copies, waits for them, and re-layouts  26.7 us (4%)
  between operations  13.2 us (2%)
    reduce_scatter x1, waiting for transfers between devices, on_device(): lax.psum_scatter(accumulator, 'cluster', scatter_dimension=0, tiled=True)  328 us
    dynamic_update_slice x64, other arithmetic, accumulate(): lax.dynamic_update_slice(accumulator, updated, (row_start, col_start))  95.6 us
    another operation x1, loops' own time, on_device(): accumulator = lax.fori_loop(0, item_count, accumulate, accumulator)  51.1 us
    psum x1, waiting for transfers between devices, on_device(): coupled = lax.psum(coupled_local, 'camera')  48.5 us
    all_gather x1, waiting for transfers between devices, on_device(): full_jac = lax.all_gather(masked, 'camera', axis=2, tiled=True)  42 us
    dot_general x16, matrix products, schur_rows(): jnp.dot(coupled[item_index], full_panel, precision=HIGHEST_PRECISION, pre...  25 us
    dot_general x16, matrix products, contract_rows(): lax.dot_general(left, right, (((0,), (0,)), ((), ())), precision=HIGHEST_...  20.2 us
    dot_general x1, matrix products, on_device(): jnp.einsum('nrjp,njkp->nrkp', point_jac, point_inv, precision=HIGHEST_PRE...  16 us
  transfers between devices with their start and end apart: 3, of which 3 were waited for; matrix products, arithmetic and copies ran while one was open for 0% of the time, Pallas kernels for 0%

commit v1 on v0

v1 whole, which is shorter than its diff:
```python
import jax
import jax.numpy as jnp
from jax import lax
from jax.experimental import pallas as pl
from jax.experimental.pallas import tpu as pltpu
from jax.sharding import Mesh, PartitionSpec as P

W = 128
SLOTS = 16
HALF = SLOTS // 2
GT = 4
NX, NZ, NYL = 4, 8, 2
TILES = 3 * GT + 1
F32 = jnp.float32
BF16 = jnp.bfloat16


def split(value):
    high = value.astype(BF16)
    return high, (value - high.astype(F32)).astype(BF16)


def coupling_kernel(idx_ref, pts_ref, inv_ref, out_ref):
    slot = idx_ref[0] * HALF + pl.program_id(0)
    lane_row = lax.rem(slot, 8)
    pts = [pts_ref[0, j] for j in range(3)]
    pairs = []
    for k in range(3):
        weighted = None
        for j in range(3):
            scale = inv_ref[j, k, pl.ds(lane_row, 1), :]
            term = pts[j] * scale
            weighted = term if weighted is None else weighted + term
        pairs.append((split(weighted), split(pts[k])))
    left = jnp.concatenate([w[0] for w, _ in pairs] + [w[0] for w, _ in pairs] + [w[1] for w, _ in pairs], axis=1)
    right = jnp.concatenate([p[0] for _, p in pairs] + [p[1] for _, p in pairs] + [p[0] for _, p in pairs], axis=1)
    out_ref[0] = lax.dot_general(left, right, (((1,), (1,)), ((), ())), preferred_element_type=F32)


def coupling(which, pts, inv):
    return pl.pallas_call(
        coupling_kernel,
        out_shape=jax.ShapeDtypeStruct((HALF, W, W), F32),
        grid_spec=pltpu.PrefetchScalarGridSpec(
            num_scalar_prefetch=1,
            grid=(HALF,),
            in_specs=[
                pl.BlockSpec((1, 3, W, W), lambda i, idx: (idx[0] * HALF + i, 0, 0, 0)),
                pl.BlockSpec((3, 3, 8, W), lambda i, idx: (0, 0, idx[0], 0)),
            ],
            out_specs=pl.BlockSpec((1, W, W), lambda i, idx: (i, 0, 0)),
        ),
        cost_estimate=pl.CostEstimate(flops=HALF * 2 * 9 * W * W * W, bytes_accessed=HALF * 4 * W * W * 4, transcendentals=0),
        name="coupling",
    )(which, pts, inv)


def schur_kernel(meta_ref, tiles_ref, own_ref, oth_ref, c0_ref, c1_ref, c2_ref, c3_ref, acc_ref):
    phase = pl.program_id(0)
    step = pl.program_id(1)
    core = meta_ref[0]
    live = meta_ref[1]
    cam = meta_ref[2]
    half = lax.rem(core + phase, 2)
    slot = half * HALF + step

    @pl.when((phase == 0) & (step == 0))
    def _():
        acc_ref[...] = jnp.zeros_like(acc_ref)

    @pl.when(slot < live)
    def _():
        m_high, m_low = split(jnp.where(phase == 0, own_ref[0], oth_ref[0]))
        panel_t = c0_ref[0].T
        t_high, t_low = split(panel_t)
        prod = jnp.dot(
            jnp.concatenate([t_high, t_high, t_low], axis=1),
            jnp.concatenate([m_high, m_low, m_high], axis=0),
            preferred_element_type=F32,
        )
        r_high, r_low = split(panel_t - prod)
        left = jnp.concatenate([r_high, r_high, r_low], axis=1)
        parts = [split(ref[0]) for ref in (c0_ref, c1_ref, c2_ref, c3_ref)]
        right = jnp.concatenate(
            [
                jnp.concatenate([h for h, _ in parts], axis=1),
                jnp.concatenate([l for _, l in parts], axis=1),
                jnp.concatenate([h for h, _ in parts], axis=1),
            ],
            axis=0,
        )
        rows = jnp.dot(left, right, preferred_element_type=F32)
        row_tile = tiles_ref[slot * 4 + cam]
        for rel in range(4):
            block = rows[:, rel * W : (rel + 1) * W].reshape(NZ, NYL, 8, W)
            if rel == 0:
                tile = 3 * GT
            else:
                tile = (rel - 1) * GT + tiles_ref[slot * 4 + lax.bitwise_xor(cam, rel)]
            for yl in range(NYL):
                acc_ref[row_tile * NYL + yl, :, tile] += block[:, yl]


def schur(meta, tiles, own, oth, panels):
    def panel_map(p, j, meta_ref, tiles_ref):
        return (lax.rem(meta_ref[0] + p, 2) * HALF + j, 0, 0)

    panel = pl.BlockSpec((1, W, W), panel_map)
    shape = (NX * NYL, NZ, TILES, 8, W)
    return pl.pallas_call(
        schur_kernel,
        out_shape=jax.ShapeDtypeStruct(shape, F32),
        grid_spec=pltpu.PrefetchScalarGridSpec(
            num_scalar_prefetch=2,
            grid=(2, HALF),
            in_specs=[
                pl.BlockSpec((1, W, W), lambda p, j, m, t: (jnp.where(p == 0, j, HALF - 1), 0, 0)),
                pl.BlockSpec((1, W, W), lambda p, j, m, t: (jnp.where(p == 0, 0, j), 0, 0)),
                panel,
                panel,
                panel,
                panel,
            ],
            out_specs=pl.BlockSpec(shape, lambda p, j, m, t: (0, 0, 0, 0, 0)),
        ),
        cost_estimate=pl.CostEstimate(flops=SLOTS * 6 * 5 * W * W * W, bytes_accessed=SLOTS * 5 * W * W * 4, transcendentals=0),
        name="schur",
    )(meta, tiles, own, oth, *panels)


def place_kernel(meta_ref, in_ref, out_ref):
    cam = meta_ref[0]
    row_tile = meta_ref[1]
    out_ref[...] = jnp.zeros_like(out_ref)

    def total(tile):
        value = in_ref[0, tile]
        for z in range(1, NZ):
            value = value + in_ref[z, tile]
        return value

    for rel in range(1, 4):
        base = lax.bitwise_xor(cam, rel) * GT
        for t in range(GT):
            out_ref[0, :, pl.ds(pl.multiple_of((base + t) * W, W), W)] = total((rel - 1) * GT + t)
    out_ref[0, :, pl.ds(pl.multiple_of((cam * GT + row_tile) * W, W), W)] = total(3 * GT)


def place(meta, pieces):
    return pl.pallas_call(
        place_kernel,
        out_shape=jax.ShapeDtypeStruct((1, 8, 4 * GT * W), F32),
        grid_spec=pltpu.PrefetchScalarGridSpec(
            num_scalar_prefetch=1,
            grid=(1,),
            in_specs=[pl.BlockSpec((NZ, TILES, 8, W), lambda i, m: (0, 0, 0, 0))],
            out_specs=pl.BlockSpec((1, 8, 4 * GT * W), lambda i, m: (0, 0, 0)),
        ),
        name="place",
    )(meta, pieces)


def swap(value, axis):
    return lax.ppermute(value, axis, [(0, 1), (1, 0)])


def on_device(counts, tiles, cam_jac, point_jac, point_inv):
    x = lax.axis_index("x")
    z = lax.axis_index("z")
    yl = lax.axis_index("yl")
    yh = lax.axis_index("yh")
    core = lax.axis_index("c")
    device = (x * NZ + z) * NYL + yl
    cam = yh * 2 + core
    live = lax.dynamic_index_in_dim(counts, device, keepdims=False)
    local_tiles = lax.dynamic_slice_in_dim(tiles, device * SLOTS, SLOTS, 0).reshape(-1)

    pts = point_jac.transpose(0, 2, 1, 3)
    inv = point_inv.transpose(1, 2, 0, 3)

    c0 = cam_jac
    c2 = swap(c0, "yh")
    c1 = swap(c0, "c")

    m_send = coupling((1 - core)[None], pts, inv)
    m_recv = swap(m_send, "c")
    m_keep = coupling(core[None], pts, inv)
    m_chip = m_keep + m_recv
    m_own = m_chip + swap(m_chip, "yh")
    m_oth = swap(m_own, "c")
    c3 = swap(c2, "c")

    acc = schur(jnp.stack([core, live, cam]), local_tiles, m_own, m_oth, (c0, c1, c2, c3))
    got = lax.all_to_all(acc, ("x", "yl"), 0, 0, tiled=True)
    part = got.sum(axis=0)
    got = lax.all_to_all(part, "z", 0, 0, tiled=True)
    return place(jnp.stack([cam, x]), got)


def solution(mesh):
    fine = Mesh(mesh.devices.reshape(NX, NZ, NYL, 2, 2), ("x", "z", "yl", "yh", "c"))
    rows = ("x", "z", "yl")
    cams = ("yh", "c")
    in_specs = (
        P(),
        P(),
        P(rows, None, cams),
        P(rows, None, None, cams),
        P(rows, None, None, cams),
    )
    return jax.shard_map(
        on_device, mesh=fine, in_specs=in_specs, out_specs=P(cams, rows, None), check_vma=False
    )
```

time: 679 us -> 131 us (0.19)
  waiting for transfers between devices: 419 us -> 34.8 us
  other arithmetic: 97.4 us -> 3.91 us
  matrix products: 67.5 us -> 0 us
  loops' own time: 51.1 us -> 0 us
  blocking collectives: 0 us -> 47.3 us
  Pallas kernels: 0 us -> 27.1 us
  local copies, waits for them, and re-layouts: 26.7 us -> 2.93 us
  starting transfers between devices: 0.09 us -> 13.5 us
  between operations: 13.2 us -> 0.1 us
    reduce_scatter x1 -> x0, waiting for transfers between devices: 328 us -> none  [on_device(): lax.psum_scatter(accumulator, 'cluster', scatter_dimension=0, tiled=True)]
    dynamic_update_slice x64 -> x0, other arithmetic: 95.6 us -> none  [accumulate(): lax.dynamic_update_slice(accumulator, updated, (row_start, col_start))]
    dot_general x34 -> x0, matrix products: 67.5 us -> none  [the longest x16 25 us: schur_rows(): jnp.dot(coupled[item_index], full_panel, precision=HIGHEST_PRECISION, pre...]
    another operation x1 -> x0, loops' own time: 51.1 us -> none  [on_device(): accumulator = lax.fori_loop(0, item_count, accumulate, accumulator)]
    psum x1 -> x0, waiting for transfers between devices: 48.5 us -> none  [on_device(): coupled = lax.psum(coupled_local, 'camera')]
    all_to_all x0 -> x1, blocking collectives: none -> 47.3 us  [on_device(): got = lax.all_to_all(acc, ('x', 'yl'), 0, 0, tiled=True)]
    all_gather x1 -> x0, waiting for transfers between devices: 42 us -> none  [on_device(): full_jac = lax.all_gather(masked, 'camera', axis=2, tiled=True)]
    pallas_call x0 -> x4, Pallas kernels: none -> 27.1 us  [the longest x1 12.4 us: schur(): pl.pallas_call(schur_kernel, out_shape=jax.ShapeDtypeStruct(shape, F32),...]
  transfers between devices with their start and end apart: 3 -> 7, of which waited for: 3 -> 3; matrix products, arithmetic and copies ran while one was open for 0% -> 3% of each run, Pallas kernels for 0% -> 10%
where the time goes in v1:
time: 131 us; the launch traced here: 130 us
  blocking collectives  47.3 us (36%)
  waiting for transfers between devices  34.8 us (27%)
  Pallas kernels  27.1 us (21%)
  starting transfers between devices  13.5 us (10%)
  other arithmetic  3.91 us (3%)
  local copies, waits for them, and re-layouts  2.93 us (2%)
    all_to_all x1, blocking collectives, on_device(): got = lax.all_to_all(acc, ('x', 'yl'), 0, 0, tiled=True)  47.3 us
    ppermute x6, waiting for transfers between devices, swap(): return lax.ppermute(value, axis, [(0, 1), (1, 0)])  20.6 us
    all_to_all x1, waiting for transfers between devices, on_device(): got = lax.all_to_all(part, 'z', 0, 0, tiled=True)  14.2 us
    pallas_call x1, Pallas kernels, schur(): pl.pallas_call(schur_kernel, out_shape=jax.ShapeDtypeStruct(shape, F32),...  12.4 us
    pallas_call x2, Pallas kernels, coupling(): pl.pallas_call(coupling_kernel, out_shape=jax.ShapeDtypeStruct((HALF, W,...  12.4 us
    all_to_all x1, starting transfers between devices, on_device(): got = lax.all_to_all(part, 'z', 0, 0, tiled=True)  9.62 us
    ppermute x6, starting transfers between devices, swap(): return lax.ppermute(value, axis, [(0, 1), (1, 0)])  3.84 us
  transfers between devices with their start and end apart: 7, of which 3 were waited for; matrix products, arithmetic and copies ran while one was open for 3% of the time, Pallas kernels for 10%

profile of v1, /device:TPU:16, one launch (start us, length us, event | category | flops | bytes accessed | tf_op | source)
XLA Modules:
  0.0 129.6 jit_solution(10546834921181635756)
XLA Ops:
  0.0 0.0 copy-start
  0.0 2.0 %collective-permute-start.4 = (f32[16,128,128]{2,1,0:T(8,128)}, f32[16,128,128]{2,1,0:T(8,128)S(1)}, u32[]{:S(2)}, u32[]{:S(2)}) collective-permute-start(f32[16,128,128]{2,1,0:T(8,128)} %c0_ref.1), channel_id=1, source_target_pairs={{0,2},{2,0},{1,3},{3,1},{4,6},{6,4},{5,7},{7,5},{8,10},{10,8},{9,1... | collective-permute-start | bytes 3145736 | tf_op jit(solution)/shard_map/ppermute | solution.py:164
  2.0 6.1 %coupling.3 = f32[8,128,128]{2,1,0:T(8,128)} custom-call(s32[1]{0:T(128)} %bitcast.5.idx_ref, f32[16,3,128,128]{3,2,1,0:T(8,128)} %bitcast.6, f32[3,3,16,128]{3,2,1,0:T(8,128)} %bitcast.8), custom_call_target="tpu_custom_call" | custom-call | flops 301989888 | bytes 2097152 | tf_op jit(solution)/shard_map/coupling/pallas_call | solution.py:41
  8.2 0.0 copy-start.3
  8.2 0.0 collective-permute-start
  8.2 0.0 copy-start.6
  8.2 6.2 %coupling.2 = f32[8,128,128]{2,1,0:T(8,128)} custom-call(s32[1]{0:T(128)} %bitcast.2.idx_ref, f32[16,3,128,128]{3,2,1,0:T(8,128)} %bitcast.7, f32[3,3,16,128]{3,2,1,0:T(8,128)} %bitcast.9), custom_call_target="tpu_custom_call" | custom-call | flops 301989888 | bytes 2097152 | tf_op jit(solution)/shard_map/coupling/pallas_call | solution.py:41
  14.4 0.0 collective-permute-done
  14.4 1.1 add.27
  15.5 1.6 %collective-permute-start.1 = (f32[8,128,128]{2,1,0:T(8,128)S(1)}, f32[8,128,128]{2,1,0:T(8,128)S(1)}, u32[]{:S(2)}, u32[]{:S(2)}) collective-permute-start(f32[8,128,128]{2,1,0:T(8,128)S(1)} %add.27), channel_id=1, source_target_pairs={{0,2},{2,0},{1,3},{3,1},{4,6},{6,4},{5,7},{7,5},{8,10},{10,8},{9,1... | collective-permute-start | bytes 1572872 | tf_op jit(solution)/shard_map/ppermute | solution.py:164
  17.1 0.0 copy-done.3
  17.1 0.1 collective-permute-start.3
  17.2 10.5 %collective-permute-done.4.c2_ref = f32[16,128,128]{2,1,0:T(8,128)S(1)} collective-permute-done((f32[16,128,128]{2,1,0:T(8,128)}, f32[16,128,128]{2,1,0:T(8,128)S(1)}, u32[]{:S(2)}, u32[]{:S(2)}) %collective-permute-start.4) | collective-permute-done | bytes 1048608 | tf_op jit(solution)/shard_map/ppermute | solution.py:164
  27.7 0.0 copy-start.4
  27.7 0.0 collective-permute-start.5
  27.8 10.1 %collective-permute-done.1 = f32[8,128,128]{2,1,0:T(8,128)S(1)} collective-permute-done((f32[8,128,128]{2,1,0:T(8,128)S(1)}, f32[8,128,128]{2,1,0:T(8,128)S(1)}, u32[]{:S(2)}, u32[]{:S(2)}) %collective-permute-start.1) | collective-permute-done | bytes 524320 | tf_op jit(solution)/shard_map/ppermute | solution.py:164
  37.9 0.1 add.28.own_ref
  37.9 0.0 copy-start.1
  37.9 0.1 collective-permute-start.2
  38.0 0.0 copy-done
  38.0 0.1 constant_dynamic-slice_fusion
  38.1 0.1 copy.7
  38.2 0.6 reshape.3.tiles_ref
  38.8 0.0 copy-done.6
  38.8 0.6 dynamic_slice.7
  39.4 1.2 pad_add_fusion.1.meta_ref
  40.7 0.0 collective-permute-done.3.c1_ref
  40.7 0.0 collective-permute-done.2.oth_ref
  40.7 0.0 copy-start.5
  40.7 0.0 collective-permute-done.5.c3_ref
  40.7 0.0 copy-done.4
  40.7 0.0 copy-done.1
  40.7 0.8 copy-done.5
  41.5 12.4 %schur.1 = f32[8,8,13,8,128]{4,3,2,1,0:T(8,128)} custom-call(s32[3]{0:T(128)} %pad_add_fusion.1.meta_ref, s32[64]{0:T(128)} %reshape.3.tiles_ref, f32[8,128,128]{2,1,0:T(8,128)} %copy-done.1, f32[8,128,128]{2,1,0:T(8,128)} %copy-done.5, f32[16,128,128]{2,1,0:T(8,128)} %c0_ref.1, f32[16,128,128]{2,1,0:T(8,128)} %collective-permute-done.3.c1_ref, ...), custom_call_target="tpu_custom_call" | custom-call | flops 1006632960 | bytes 5242880 | tf_op jit(solution)/shard_map/schur/pallas_call | solution.py:110
  53.9 47.3 %all_to_all.10 = f32[8,8,13,8,128]{4,3,2,1,0:T(8,128)S(1)} all-to-all(f32[8,8,13,8,128]{4,3,2,1,0:T(8,128)} %schur.1), channel_id=1, replica_groups=mesh['x'=4,'z'=8,'yl'=2,'yh'=2,'c'=2] {'x','yl'}, dimensions={0} | all-to-all | bytes 6815744 | tf_op jit(solution)/shard_map/all_to_all | solution.py:194
  101.2 0.9 reduce_sum.9
  102.1 9.6 %all-to-all-start.1 = ((f32[8,13,8,128]{3,2,1,0:T(8,128)}), f32[8,13,8,128]{3,2,1,0:T(8,128)S(1)}, u32[]{:S(2)}, u32[]{:S(2)}) async-start(f32[8,13,8,128]{3,2,1,0:T(8,128)} %reduce_sum.9), calls=%async_computation.1 | async-start | bytes 851968 | tf_op jit(solution)/shard_map/all_to_all | solution.py:196
  111.8 0.6 pad_add_fusion.meta_ref
  112.3 14.2 %all-to-all-done.1.in_ref = f32[8,13,8,128]{3,2,1,0:T(8,128)S(1)} async-done(((f32[8,13,8,128]{3,2,1,0:T(8,128)}), f32[8,13,8,128]{3,2,1,0:T(8,128)S(1)}, u32[]{:S(2)}, u32[]{:S(2)}) %all-to-all-start.1) | async-done | bytes 426016 | tf_op jit(solution)/shard_map/all_to_all | solution.py:196
  126.5 0.0 copy-start.2
  126.5 0.8 copy-done.2
  127.3 2.3 %place.1 = f32[1,8,2048]{2,1,0:T(8,128)} custom-call(s32[2]{0:T(128)} %pad_add_fusion.meta_ref, f32[8,13,8,128]{3,2,1,0:T(8,128)} %copy-done.2), custom_call_target="tpu_custom_call" | custom-call | tf_op jit(solution)/shard_map/place/pallas_call | solution.py:150
Async XLA Ops:
  0.0 38.0 %copy-start = (s32[1024,4]{0,1:T(4,128)S(1)}, s32[1024,4]{0,1:T(4,128)}, u32[]{:S(2)}) copy-start(s32[1024,4]{0,1:T(4,128)} %param.6) | copy-start | bytes 49156
  0.0 27.7 %collective-permute-start.4 = (f32[16,128,128]{2,1,0:T(8,128)}, f32[16,128,128]{2,1,0:T(8,128)S(1)}, u32[]{:S(2)}, u32[]{:S(2)}) collective-permute-start(f32[16,128,128]{2,1,0:T(8,128)} %c0_ref.1), channel_id=1, source_target_pairs={{0,2},{2,0},{1,3},{3,1},{4,6},{6,4},{5,7},{7,5},{8,10},{10,8},{9,1... | collective-permute-start | bytes 3145736 | tf_op jit(solution)/shard_map/ppermute | solution.py:164
  8.2 8.9 %copy-start.3 = (f32[16,128,128]{2,1,0:T(8,128)S(1)}, f32[16,128,128]{2,1,0:T(8,128)}, u32[]{:S(2)}) copy-start(f32[16,128,128]{2,1,0:T(8,128)} %c0_ref.1) | copy-start | bytes 3145732
  8.2 6.3 %collective-permute-start = (f32[8,128,128]{2,1,0:T(8,128)}, f32[8,128,128]{2,1,0:T(8,128)S(1)}, u32[]{:S(2)}, u32[]{:S(2)}) collective-permute-start(f32[8,128,128]{2,1,0:T(8,128)} %coupling.3), channel_id=1, source_target_pairs={{0,1},{1,0},{2,3},{3,2},{4,5},{5,4},{6,7},{7,6},{8,9},{9,8},{10,11... | collective-permute-start | bytes 1572872 | tf_op jit(solution)/shard_map/ppermute | solution.py:164
  8.2 30.7 %copy-start.6 = (s32[64]{0:T(128)S(1)}, s32[64]{0:T(128)}, u32[]{:S(2)}) copy-start(s32[64]{0:T(128)} %param.5) | copy-start | bytes 772
  15.5 22.3 %collective-permute-start.1 = (f32[8,128,128]{2,1,0:T(8,128)S(1)}, f32[8,128,128]{2,1,0:T(8,128)S(1)}, u32[]{:S(2)}, u32[]{:S(2)}) collective-permute-start(f32[8,128,128]{2,1,0:T(8,128)S(1)} %add.27), channel_id=1, source_target_pairs={{0,2},{2,0},{1,3},{3,1},{4,6},{6,4},{5,7},{7,5},{8,10},{10,8},{9,1... | collective-permute-start | bytes 1572872 | tf_op jit(solution)/shard_map/ppermute | solution.py:164
  17.1 23.6 %collective-permute-start.3 = (f32[16,128,128]{2,1,0:T(8,128)S(1)}, f32[16,128,128]{2,1,0:T(8,128)}, u32[]{:S(2)}, u32[]{:S(2)}) collective-permute-start(f32[16,128,128]{2,1,0:T(8,128)S(1)} %copy-done.3), channel_id=1, source_target_pairs={{0,1},{1,0},{2,3},{3,2},{4,5},{5,4},{6,7},{7,6},{8,9},{9,8},{10,11... | collective-permute-start | bytes 3145736 | tf_op jit(solution)/shard_map/ppermute | solution.py:164
  27.7 12.9 %copy-start.4 = (f32[16,128,128]{2,1,0:T(8,128)}, f32[16,128,128]{2,1,0:T(8,128)S(1)}, u32[]{:S(2)}) copy-start(f32[16,128,128]{2,1,0:T(8,128)S(1)} %collective-permute-done.4.c2_ref) | copy-start | bytes 3145732
  27.7 12.9 %collective-permute-start.5 = (f32[16,128,128]{2,1,0:T(8,128)S(1)}, f32[16,128,128]{2,1,0:T(8,128)}, u32[]{:S(2)}, u32[]{:S(2)}) collective-permute-start(f32[16,128,128]{2,1,0:T(8,128)S(1)} %collective-permute-done.4.c2_ref), channel_id=1, source_target_pairs={{0,1},{1,0},{2,3},{3,2},{4,5},{5,4},{6,7},{7,6},{8,9},{9,8},{10,11... | collective-permute-start | bytes 3145736 | tf_op jit(solution)/shard_map/ppermute | solution.py:164
  37.9 2.8 %copy-start.1 = (f32[8,128,128]{2,1,0:T(8,128)}, f32[8,128,128]{2,1,0:T(8,128)S(1)}, u32[]{:S(2)}) copy-start(f32[8,128,128]{2,1,0:T(8,128)S(1)} %add.28.own_ref) | copy-start | bytes 1572868
  37.9 2.8 %collective-permute-start.2 = (f32[8,128,128]{2,1,0:T(8,128)S(1)}, f32[8,128,128]{2,1,0:T(8,128)S(1)}, u32[]{:S(2)}, u32[]{:S(2)}) collective-permute-start(f32[8,128,128]{2,1,0:T(8,128)S(1)} %add.28.own_ref), channel_id=1, source_target_pairs={{0,1},{1,0},{2,3},{3,2},{4,5},{5,4},{6,7},{7,6},{8,9},{9,8},{10,11... | collective-permute-start | bytes 1572872 | tf_op jit(solution)/shard_map/ppermute | solution.py:164
  40.7 0.8 copy-start.5
  102.1 24.4 %all-to-all-start.1 = ((f32[8,13,8,128]{3,2,1,0:T(8,128)}), f32[8,13,8,128]{3,2,1,0:T(8,128)S(1)}, u32[]{:S(2)}, u32[]{:S(2)}) async-start(f32[8,13,8,128]{3,2,1,0:T(8,128)} %reduce_sum.9), calls=%async_computation.1 | async-start | bytes 851968 | tf_op jit(solution)/shard_map/all_to_all | solution.py:196
  126.5 0.8 copy-start.2

commit v2 on v0

v2 whole, which is shorter than its diff:
```python
import jax
import jax.numpy as jnp
from jax import lax
from jax.experimental import pallas as pl
from jax.experimental.pallas import tpu as pltpu
from jax.sharding import Mesh, PartitionSpec as P

W = 128
SLOTS = 16
HALF = SLOTS // 2
CHUNK = 4
GT = 4
NX, NZH, NZL, NYL = 4, 4, 2, 2
FIRST = NX * NZL * NYL
TILES = 3 * GT + 1
F32 = jnp.float32
BF16 = jnp.bfloat16
ANY = pl.BlockSpec(memory_space=pl.ANY)
SMEM = pl.BlockSpec(memory_space=pltpu.SMEM)
VMEM = pl.BlockSpec(memory_space=pltpu.VMEM)


def split(value):
    high = value.astype(BF16)
    return high, (value - high.astype(F32)).astype(BF16)


def camera_index():
    return lax.axis_index("yh") * 2 + lax.axis_index("c")


def cluster_device():
    x, zh, zl, yl = (lax.axis_index(name) for name in ("x", "zh", "zl", "yl"))
    return ((x * NZH + zh) * NZL + zl) * NYL + yl


def coupling_kernel(mine, pts_hbm, inv_ref, out_ref, pts_buf, sems):
    core = lax.axis_index("c")
    base = (core if mine else 1 - core) * HALF

    def fetch(i):
        return pltpu.make_async_copy(pts_hbm.at[base + i], pts_buf.at[i], sems.at[i])

    for i in range(HALF):
        fetch(i).start()
    for i in range(HALF):
        fetch(i).wait()
        pts = [pts_buf[i, j] for j in range(3)]
        pairs = []
        for k in range(3):
            weighted = None
            for j in range(3):
                term = pts[j] * inv_ref[j, k, pl.ds(base + i, 1), :]
                weighted = term if weighted is None else weighted + term
            pairs.append((split(weighted), split(pts[k])))
        left = jnp.concatenate([w[0] for w, _ in pairs] + [w[0] for w, _ in pairs] + [w[1] for w, _ in pairs], axis=1)
        right = jnp.concatenate([p[0] for _, p in pairs] + [p[1] for _, p in pairs] + [p[0] for _, p in pairs], axis=1)
        out_ref[i] = lax.dot_general(left, right, (((1,), (1,)), ((), ())), preferred_element_type=F32)


def coupling(mine, pts, inv):
    def kernel(*refs):
        coupling_kernel(mine, *refs)

    return pl.pallas_call(
        kernel,
        out_shape=jax.ShapeDtypeStruct((HALF, W, W), F32),
        in_specs=[ANY, VMEM],
        out_specs=VMEM,
        scratch_shapes=[pltpu.VMEM((HALF, 3, W, W), F32), pltpu.SemaphoreType.DMA((HALF,))],
        cost_estimate=pl.CostEstimate(flops=HALF * 2 * 9 * W * W * W, bytes_accessed=HALF * 4 * W * W * 4, transcendentals=0),
        name="coupling",
    )(pts, inv)


def schur_kernel(counts_ref, tiles_ref, own_hbm, oth_hbm, c0_hbm, c1_hbm, c2_hbm, c3_hbm, acc_ref, m_buf, c_buf, m_sems, c_sems):
    core = lax.axis_index("c")
    cam = camera_index()
    device = cluster_device()
    live = counts_ref[device]
    panels = (c0_hbm, c1_hbm, c2_hbm, c3_hbm)

    def fetch_m(which):
        source, half = (own_hbm, core) if which == 0 else (oth_hbm, 1 - core)
        return pltpu.make_async_copy(source, m_buf.at[pl.ds(half * HALF, HALF)], m_sems.at[which])

    def fetch_c(rel, k):
        part = pl.ds(k * CHUNK, CHUNK)
        return pltpu.make_async_copy(panels[rel].at[part], c_buf.at[rel, part], c_sems.at[rel, k])

    steps = SLOTS // CHUNK
    for which in range(2):
        fetch_m(which).start()
    for k in range(steps):
        for rel in range(4):
            fetch_c(rel, k).start()
    acc_ref[...] = jnp.zeros_like(acc_ref)
    for which in range(2):
        fetch_m(which).wait()

    for k in range(steps):
        for rel in range(4):
            fetch_c(rel, k).wait()

        @pl.when(k * CHUNK < live)
        def _():
            for i in range(CHUNK):
                slot = k * CHUNK + i
                m_high, m_low = split(m_buf[slot])
                panel_t = c_buf[0, slot].T
                t_high, t_low = split(panel_t)
                prod = jnp.dot(
                    jnp.concatenate([t_high, t_high, t_low], axis=1),
                    jnp.concatenate([m_high, m_low, m_high], axis=0),
                    preferred_element_type=F32,
                )
                rest = panel_t - prod
                if i:
                    rest = jnp.where(slot < live, rest, 0.0)
                r_high, r_low = split(rest)
                left = jnp.concatenate([r_high, r_high, r_low], axis=1)
                parts = [split(c_buf[rel, slot]) for rel in range(4)]
                highs = jnp.concatenate([h for h, _ in parts], axis=1)
                lows = jnp.concatenate([l for _, l in parts], axis=1)
                right = jnp.concatenate([highs, lows, highs], axis=0)
                rows = jnp.dot(left, right, preferred_element_type=F32)
                row_tile = tiles_ref[cam, device * SLOTS + slot]
                for rel in range(4):
                    block = rows[:, rel * W : (rel + 1) * W].reshape(NZH, NZL, NYL, 8, W)
                    if rel == 0:
                        tile = 3 * GT
                    else:
                        tile = (rel - 1) * GT + tiles_ref[lax.bitwise_xor(cam, rel), device * SLOTS + slot]
                    for zl in range(NZL):
                        for yl in range(NYL):
                            acc_ref[row_tile * (NZL * NYL) + zl * NYL + yl, :, tile] += block[:, zl, yl]


def schur(counts, tiles, own, oth, panels):
    return pl.pallas_call(
        schur_kernel,
        out_shape=jax.ShapeDtypeStruct((FIRST, NZH, TILES, 8, W), F32),
        in_specs=[SMEM, SMEM] + [ANY] * 6,
        out_specs=VMEM,
        scratch_shapes=[
            pltpu.VMEM((SLOTS, W, W), F32),
            pltpu.VMEM((4, SLOTS, W, W), F32),
            pltpu.SemaphoreType.DMA((2,)),
            pltpu.SemaphoreType.DMA((4, SLOTS // CHUNK)),
        ],
        cost_estimate=pl.CostEstimate(flops=SLOTS * 6 * 5 * W * W * W, bytes_accessed=SLOTS * 5 * W * W * 4, transcendentals=0),
        name="schur",
    )(counts, tiles, own, oth, *panels)


def place_kernel(in_ref, out_ref):
    cam = camera_index()
    x = lax.axis_index("x")
    out_ref[...] = jnp.zeros_like(out_ref)

    def total(tile):
        value = in_ref[0, tile]
        for source in range(1, NZH):
            value = value + in_ref[source, tile]
        return value

    for rel in range(1, 4):
        base = lax.bitwise_xor(cam, rel) * GT
        for t in range(GT):
            out_ref[0, :, pl.ds(pl.multiple_of((base + t) * W, W), W)] = total((rel - 1) * GT + t)
    out_ref[0, :, pl.ds(pl.multiple_of((cam * GT + x) * W, W), W)] = total(3 * GT)


def place(pieces):
    return pl.pallas_call(
        place_kernel,
        out_shape=jax.ShapeDtypeStruct((1, 8, 4 * GT * W), F32),
        in_specs=[VMEM],
        out_specs=VMEM,
        name="place",
    )(pieces)


def swap(value, axis):
    return lax.ppermute(value, axis, [(0, 1), (1, 0)])


def on_device(counts, tiles, cam_jac, point_jac, point_inv):
    pts = point_jac.transpose(0, 2, 1, 3)
    inv = point_inv.transpose(1, 2, 0, 3)

    c0 = cam_jac
    c2 = swap(c0, "yh")
    c1 = swap(c0, "c")

    m_send = coupling(False, pts, inv)
    m_recv = swap(m_send, "c")
    m_keep = coupling(True, pts, inv)
    m_chip = m_keep + m_recv
    m_own = m_chip + swap(m_chip, "yh")
    m_oth = swap(m_own, "c")
    c3 = swap(c2, "c")

    acc = schur(counts, tiles.T, m_own, m_oth, (c0, c1, c2, c3))
    got = lax.all_to_all(acc, ("x", "zl", "yl"), 0, 0, tiled=True)
    part = got.sum(axis=0)
    return place(lax.all_to_all(part, "zh", 0, 0, tiled=True))


def solution(mesh):
    fine = Mesh(mesh.devices.reshape(NX, NZH, NZL, NYL, 2, 2), ("x", "zh", "zl", "yl", "yh", "c"))
    rows = ("x", "zh", "zl", "yl")
    cams = ("yh", "c")
    in_specs = (
        P(),
        P(),
        P(rows, None, cams),
        P(rows, None, None, cams),
        P(rows, None, None, cams),
    )
    return jax.shard_map(
        on_device, mesh=fine, in_specs=in_specs, out_specs=P(cams, rows, None), check_vma=False
    )
```

time: 679 us -> 119 us (0.18)
  waiting for transfers between devices: 419 us -> 24.7 us
  other arithmetic: 97.4 us -> 2 us
  blocking collectives: 0 us -> 68.4 us
  matrix products: 67.5 us -> 0 us
  loops' own time: 51.1 us -> 0 us
  local copies, waits for them, and re-layouts: 26.7 us -> 1.18 us
  Pallas kernels: 0 us -> 17.9 us
  between operations: 13.2 us -> 0.11 us
    reduce_scatter x1 -> x0, waiting for transfers between devices: 328 us -> none  [on_device(): lax.psum_scatter(accumulator, 'cluster', scatter_dimension=0, tiled=True)]
    dynamic_update_slice x64 -> x0, other arithmetic: 95.6 us -> none  [accumulate(): lax.dynamic_update_slice(accumulator, updated, (row_start, col_start))]
    all_to_all x0 -> x2, blocking collectives: none -> 68.4 us  [the longest x1 51.5 us: on_device(): got = lax.all_to_all(acc, ('x', 'zl', 'yl'), 0, 0, tiled=True)]
    dot_general x34 -> x0, matrix products: 67.5 us -> none  [the longest x16 25 us: schur_rows(): jnp.dot(coupled[item_index], full_panel, precision=HIGHEST_PRECISION, pre...]
    another operation x1 -> x0, loops' own time: 51.1 us -> none  [on_device(): accumulator = lax.fori_loop(0, item_count, accumulate, accumulator)]
    psum x1 -> x0, waiting for transfers between devices: 48.5 us -> none  [on_device(): coupled = lax.psum(coupled_local, 'camera')]
    all_gather x1 -> x0, waiting for transfers between devices: 42 us -> none  [on_device(): full_jac = lax.all_gather(masked, 'camera', axis=2, tiled=True)]
    ppermute x0 -> x6, waiting for transfers between devices: none -> 24.7 us  [swap(): return lax.ppermute(value, axis, [(0, 1), (1, 0)])]
  transfers between devices with their start and end apart: 3 -> 6, of which waited for: 3 -> 3; matrix products, arithmetic and copies ran while one was open for 0% -> 1% of each run, Pallas kernels for 0% -> 8%
where the time goes in v2:
time: 119 us; the launch traced here: 118 us
  blocking collectives  68.4 us (57%)
  waiting for transfers between devices  24.7 us (21%)
  Pallas kernels  17.9 us (15%)
  starting transfers between devices  3.97 us (3%)
  other arithmetic  2 us (2%)
    all_to_all x1, blocking collectives, on_device(): got = lax.all_to_all(acc, ('x', 'zl', 'yl'), 0, 0, tiled=True)  51.5 us
    ppermute x6, waiting for transfers between devices, swap(): return lax.ppermute(value, axis, [(0, 1), (1, 0)])  24.7 us
    all_to_all x1, blocking collectives, on_device(): return place(lax.all_to_all(part, 'zh', 0, 0, tiled=True))  16.9 us
    pallas_call x2, Pallas kernels, coupling(): pl.pallas_call(kernel, out_shape=jax.ShapeDtypeStruct((HALF, W, W), F32),...  10 us
    pallas_call x1, Pallas kernels, schur(): pl.pallas_call(schur_kernel, out_shape=jax.ShapeDtypeStruct((FIRST, NZH,...  6.28 us
    ppermute x6, starting transfers between devices, swap(): return lax.ppermute(value, axis, [(0, 1), (1, 0)])  3.97 us
  transfers between devices with their start and end apart: 6, of which 3 were waited for; matrix products, arithmetic and copies ran while one was open for 1% of the time, Pallas kernels for 8%

profile of v2, /device:TPU:16, one launch (start us, length us, event | category | flops | bytes accessed | tf_op | source)
XLA Modules:
  0.0 118.2 jit_solution(15935071203375415874)
XLA Ops:
  0.0 2.0 %collective-permute-start.4 = (f32[16,128,128]{2,1,0:T(8,128)}, f32[16,128,128]{2,1,0:T(8,128)S(1)}, u32[]{:S(2)}, u32[]{:S(2)}) collective-permute-start(f32[16,128,128]{2,1,0:T(8,128)} %c0_hbm.1), channel_id=1, source_target_pairs={{0,2},{2,0},{1,3},{3,1},{4,6},{6,4},{5,7},{7,5},{8,10},{10,8},{9,1... | collective-permute-start | bytes 3145736 | tf_op jit(solution)/shard_map/ppermute | solution.py:185
  2.0 5.0 %coupling.3 = f32[8,128,128]{2,1,0:T(8,128)} custom-call(f32[16,3,128,128]{3,2,1,0:T(8,128)} %bitcast.3, f32[3,3,16,128]{3,2,1,0:T(8,128)} %bitcast.5), custom_call_target="tpu_custom_call" | custom-call | flops 301989888 | bytes 2097152 | tf_op jit(solution)/shard_map/coupling/pallas_call | solution.py:65
  7.0 0.0 copy-start.1
  7.0 0.1 collective-permute-start
  7.1 5.0 %coupling.2 = f32[8,128,128]{2,1,0:T(8,128)} custom-call(f32[16,3,128,128]{3,2,1,0:T(8,128)} %bitcast.4, f32[3,3,16,128]{3,2,1,0:T(8,128)} %bitcast.6), custom_call_target="tpu_custom_call" | custom-call | flops 301989888 | bytes 2097152 | tf_op jit(solution)/shard_map/coupling/pallas_call | solution.py:65
  12.2 0.0 collective-permute-done
  12.2 1.1 add.6
  13.3 1.6 %collective-permute-start.1 = (f32[8,128,128]{2,1,0:T(8,128)S(1)}, f32[8,128,128]{2,1,0:T(8,128)S(1)}, u32[]{:S(2)}, u32[]{:S(2)}) collective-permute-start(f32[8,128,128]{2,1,0:T(8,128)S(1)} %add.6), channel_id=1, source_target_pairs={{0,2},{2,0},{1,3},{3,1},{4,6},{6,4},{5,7},{7,5},{8,10},{10,8},{9,1... | collective-permute-start | bytes 1572872 | tf_op jit(solution)/shard_map/ppermute | solution.py:185
  14.9 0.0 copy-done.1
  14.9 0.2 collective-permute-start.3
  15.0 12.7 %collective-permute-done.4.c2_hbm = f32[16,128,128]{2,1,0:T(8,128)S(1)} collective-permute-done((f32[16,128,128]{2,1,0:T(8,128)}, f32[16,128,128]{2,1,0:T(8,128)S(1)}, u32[]{:S(2)}, u32[]{:S(2)}) %collective-permute-start.4) | collective-permute-done | bytes 1048608 | tf_op jit(solution)/shard_map/ppermute | solution.py:185
  27.7 0.0 copy-start.2
  27.7 0.0 collective-permute-start.5
  27.8 10.1 %collective-permute-done.1 = f32[8,128,128]{2,1,0:T(8,128)S(1)} collective-permute-done((f32[8,128,128]{2,1,0:T(8,128)S(1)}, f32[8,128,128]{2,1,0:T(8,128)S(1)}, u32[]{:S(2)}, u32[]{:S(2)}) %collective-permute-start.1) | collective-permute-done | bytes 524320 | tf_op jit(solution)/shard_map/ppermute | solution.py:185
  37.9 0.1 add.7.own_hbm
  37.9 0.0 copy-start
  37.9 0.1 collective-permute-start.2
  38.0 0.0 collective-permute-done.3.c1_hbm
  38.0 0.0 copy-start.3
  38.0 1.9 %collective-permute-done.2.oth_hbm = f32[8,128,128]{2,1,0:T(8,128)S(1)} collective-permute-done((f32[8,128,128]{2,1,0:T(8,128)S(1)}, f32[8,128,128]{2,1,0:T(8,128)S(1)}, u32[]{:S(2)}, u32[]{:S(2)}) %collective-permute-start.2) | collective-permute-done | bytes 524320 | tf_op jit(solution)/shard_map/ppermute | solution.py:185
  39.9 0.0 copy-start.5
  39.9 0.0 collective-permute-done.5.c3_hbm
  39.9 0.0 copy-done.3
  39.9 0.0 copy-start.4
  39.9 1.0 copy-done.4
  41.0 0.0 copy-done.2
  41.0 0.0 copy-done
  41.0 0.1 copy-done.5
  41.1 6.3 %schur.1 = f32[16,4,13,8,128]{4,3,2,1,0:T(8,128)} custom-call(s32[64]{0:T(128)} %counts_ref.1, s32[4,1024]{1,0:T(4,128)} %bitcast.7, f32[8,128,128]{2,1,0:T(8,128)} %copy-done, f32[8,128,128]{2,1,0:T(8,128)} %copy-done.5, f32[16,128,128]{2,1,0:T(8,128)} %c0_hbm.1, f32[16,128,128]{2,1,0:T(8,128)} %copy-done.3, f32[16,128,128]{2,1,0:T(8,128)} %copy-done.2, ...), custom_call_target="tpu_custom_call" | custom-call | flops 1006632960 | bytes 5242880 | tf_op jit(solution)/shard_map/schur/pallas_call | solution.py:140
  47.4 51.5 %all_to_all.10 = f32[16,4,13,8,128]{4,3,2,1,0:T(8,128)S(1)} all-to-all(f32[16,4,13,8,128]{4,3,2,1,0:T(8,128)} %schur.1), channel_id=1, replica_groups=mesh['x'=4,'zh'=4,'zl'=2,'yl'=2,'yh'=2,'c'=2] {'x','zl','yl'}, dimensions={0} | all-to-all | bytes 6815744 | tf_op jit(solution)/shard_map/all_to_all | solution.py:205
  98.9 0.8 reduce_sum.9
  99.7 16.9 %all_to_all.11.in_ref = f32[4,13,8,128]{3,2,1,0:T(8,128)} all-to-all(f32[4,13,8,128]{3,2,1,0:T(8,128)} %reduce_sum.9), channel_id=1, replica_groups=mesh['x'=4,'zh'=4,'zl'=2,'yl'=2,'yh'=2,'c'=2] {'zh'}, dimensions={0} | all-to-all | bytes 425984 | tf_op jit(solution)/shard_map/all_to_all | solution.py:207
  116.6 1.6 %place.1 = f32[1,8,2048]{2,1,0:T(8,128)} custom-call(f32[4,13,8,128]{3,2,1,0:T(8,128)} %all_to_all.11.in_ref), custom_call_target="tpu_custom_call" | custom-call | tf_op jit(solution)/shard_map/place/pallas_call | solution.py:175
Async XLA Ops:
  0.0 27.7 %collective-permute-start.4 = (f32[16,128,128]{2,1,0:T(8,128)}, f32[16,128,128]{2,1,0:T(8,128)S(1)}, u32[]{:S(2)}, u32[]{:S(2)}) collective-permute-start(f32[16,128,128]{2,1,0:T(8,128)} %c0_hbm.1), channel_id=1, source_target_pairs={{0,2},{2,0},{1,3},{3,1},{4,6},{6,4},{5,7},{7,5},{8,10},{10,8},{9,1... | collective-permute-start | bytes 3145736 | tf_op jit(solution)/shard_map/ppermute | solution.py:185
  7.0 7.8 %copy-start.1 = (f32[16,128,128]{2,1,0:T(8,128)S(1)}, f32[16,128,128]{2,1,0:T(8,128)}, u32[]{:S(2)}) copy-start(f32[16,128,128]{2,1,0:T(8,128)} %c0_hbm.1) | copy-start | bytes 3145732
  7.0 5.1 %collective-permute-start = (f32[8,128,128]{2,1,0:T(8,128)}, f32[8,128,128]{2,1,0:T(8,128)S(1)}, u32[]{:S(2)}, u32[]{:S(2)}) collective-permute-start(f32[8,128,128]{2,1,0:T(8,128)} %coupling.3), channel_id=1, source_target_pairs={{0,1},{1,0},{2,3},{3,2},{4,5},{5,4},{6,7},{7,6},{8,9},{9,8},{10,11... | collective-permute-start | bytes 1572872 | tf_op jit(solution)/shard_map/ppermute | solution.py:185
  13.3 24.6 %collective-permute-start.1 = (f32[8,128,128]{2,1,0:T(8,128)S(1)}, f32[8,128,128]{2,1,0:T(8,128)S(1)}, u32[]{:S(2)}, u32[]{:S(2)}) collective-permute-start(f32[8,128,128]{2,1,0:T(8,128)S(1)} %add.6), channel_id=1, source_target_pairs={{0,2},{2,0},{1,3},{3,1},{4,6},{6,4},{5,7},{7,5},{8,10},{10,8},{9,1... | collective-permute-start | bytes 1572872 | tf_op jit(solution)/shard_map/ppermute | solution.py:185
  14.9 23.2 %collective-permute-start.3 = (f32[16,128,128]{2,1,0:T(8,128)S(1)}, f32[16,128,128]{2,1,0:T(8,128)S(1)}, u32[]{:S(2)}, u32[]{:S(2)}) collective-permute-start(f32[16,128,128]{2,1,0:T(8,128)S(1)} %copy-done.1), channel_id=1, source_target_pairs={{0,1},{1,0},{2,3},{3,2},{4,5},{5,4},{6,7},{7,6},{8,9},{9,8},{10,11... | collective-permute-start | bytes 3145736 | tf_op jit(solution)/shard_map/ppermute | solution.py:185
  27.7 13.2 %copy-start.2 = (f32[16,128,128]{2,1,0:T(8,128)}, f32[16,128,128]{2,1,0:T(8,128)S(1)}, u32[]{:S(2)}) copy-start(f32[16,128,128]{2,1,0:T(8,128)S(1)} %collective-permute-done.4.c2_hbm) | copy-start | bytes 3145732
  27.7 12.2 %collective-permute-start.5 = (f32[16,128,128]{2,1,0:T(8,128)S(1)}, f32[16,128,128]{2,1,0:T(8,128)S(1)}, u32[]{:S(2)}, u32[]{:S(2)}) collective-permute-start(f32[16,128,128]{2,1,0:T(8,128)S(1)} %collective-permute-done.4.c2_hbm), channel_id=1, source_target_pairs={{0,1},{1,0},{2,3},{3,2},{4,5},{5,4},{6,7},{7,6},{8,9},{9,8},{10,11... | collective-permute-start | bytes 3145736 | tf_op jit(solution)/shard_map/ppermute | solution.py:185
  37.9 3.1 %copy-start = (f32[8,128,128]{2,1,0:T(8,128)}, f32[8,128,128]{2,1,0:T(8,128)S(1)}, u32[]{:S(2)}) copy-start(f32[8,128,128]{2,1,0:T(8,128)S(1)} %add.7.own_hbm) | copy-start | bytes 1572868
  37.9 2.0 %collective-permute-start.2 = (f32[8,128,128]{2,1,0:T(8,128)S(1)}, f32[8,128,128]{2,1,0:T(8,128)S(1)}, u32[]{:S(2)}, u32[]{:S(2)}) collective-permute-start(f32[8,128,128]{2,1,0:T(8,128)S(1)} %add.7.own_hbm), channel_id=1, source_target_pairs={{0,1},{1,0},{2,3},{3,2},{4,5},{5,4},{6,7},{7,6},{8,9},{9,8},{10,11... | collective-permute-start | bytes 1572872 | tf_op jit(solution)/shard_map/ppermute | solution.py:185
  38.0 1.9 %copy-start.3 = (f32[16,128,128]{2,1,0:T(8,128)}, f32[16,128,128]{2,1,0:T(8,128)S(1)}, u32[]{:S(2)}) copy-start(f32[16,128,128]{2,1,0:T(8,128)S(1)} %collective-permute-done.3.c1_hbm) | copy-start | bytes 3145732
  39.9 1.2 copy-start.5
  39.9 1.0 copy-start.4

commit v3 on v2

--- a/solution.py
+++ b/solution.py
@@ -5,14 +5,14 @@
 from jax.experimental.pallas import tpu as pltpu
 from jax.sharding import Mesh, PartitionSpec as P
 
+
 W = 128
 SLOTS = 16
 HALF = SLOTS // 2
 CHUNK = 4
 GT = 4
-NX, NZH, NZL, NYL = 4, 4, 2, 2
-FIRST = NX * NZL * NYL
-TILES = 3 * GT + 1
+NXH, NXL, NZH, NZL, NYL = 2, 2, 4, 2, 2
+GROUPS = (("xl", "zl", "yl", GT), ("zl", "yl", "xl", GT), ("yl", "xl", "zl", GT + 1))
 F32 = jnp.float32
 BF16 = jnp.bfloat16
 ANY = pl.BlockSpec(memory_space=pl.ANY)
@@ -30,8 +30,8 @@
 
 
 def cluster_device():
-    x, zh, zl, yl = (lax.axis_index(name) for name in ("x", "zh", "zl", "yl"))
-    return ((x * NZH + zh) * NZL + zl) * NYL + yl
+    xh, xl, zh, zl, yl = (lax.axis_index(name) for name in ("xh", "xl", "zh", "zl", "yl"))
+    return (((xh * NXL + xl) * NZH + zh) * NZL + zl) * NYL + yl
 
 
 def coupling_kernel(mine, pts_hbm, inv_ref, out_ref, pts_buf, sems):
@@ -73,7 +73,8 @@
     )(pts, inv)
 
 
-def schur_kernel(counts_ref, tiles_ref, own_hbm, oth_hbm, c0_hbm, c1_hbm, c2_hbm, c3_hbm, acc_ref, m_buf, c_buf, m_sems, c_sems):
+def schur_kernel(counts_ref, tiles_ref, own_hbm, oth_hbm, c0_hbm, c1_hbm, c2_hbm, c3_hbm, *refs):
+    outs, (m_buf, c_buf, m_sems, c_sems, o_sems), accs = refs[:6], refs[6:11], refs[11:]
     core = lax.axis_index("c")
     cam = camera_index()
     device = cluster_device()
@@ -94,7 +95,8 @@
     for k in range(steps):
         for rel in range(4):
             fetch_c(rel, k).start()
-    acc_ref[...] = jnp.zeros_like(acc_ref)
+    for acc in accs:
+        acc[...] = jnp.zeros_like(acc)
     for which in range(2):
         fetch_m(which).wait()
 
@@ -128,26 +130,41 @@
                 for rel in range(4):
                     block = rows[:, rel * W : (rel + 1) * W].reshape(NZH, NZL, NYL, 8, W)
                     if rel == 0:
-                        tile = 3 * GT
+                        group, tile = 2, GT
                     else:
-                        tile = (rel - 1) * GT + tiles_ref[lax.bitwise_xor(cam, rel), device * SLOTS + slot]
+                        group, tile = rel - 1, tiles_ref[lax.bitwise_xor(cam, rel), device * SLOTS + slot]
                     for zl in range(NZL):
                         for yl in range(NYL):
-                            acc_ref[row_tile * (NZL * NYL) + zl * NYL + yl, :, tile] += block[:, zl, yl]
+                            place_at = {"xl": lax.rem(row_tile, NXL), "zl": zl, "yl": yl}
+                            lead = tuple(place_at[name] for name in GROUPS[group][:3])
+                            accs[group][lead + (row_tile // NXL, slice(None), tile)] += block[:, zl, yl]
+
+    copies = []
+    for group, names in enumerate(GROUPS):
+        bit = lax.axis_index(names[0])
+        for which, source in enumerate((1 - bit, bit)):
+            k = group * 2 + which
+            copies.append(pltpu.make_async_copy(accs[group].at[source], outs[k], o_sems.at[k]))
+    for copy in copies:
+        copy.start()
+    for copy in copies:
+        copy.wait()
 
 
 def schur(counts, tiles, own, oth, panels):
     return pl.pallas_call(
         schur_kernel,
-        out_shape=jax.ShapeDtypeStruct((FIRST, NZH, TILES, 8, W), F32),
+        out_shape=[jax.ShapeDtypeStruct((2, 2, NXH, NZH, names[3], 8, W), F32) for names in GROUPS for _ in range(2)],
         in_specs=[SMEM, SMEM] + [ANY] * 6,
-        out_specs=VMEM,
+        out_specs=[ANY] * 6,
         scratch_shapes=[
             pltpu.VMEM((SLOTS, W, W), F32),
             pltpu.VMEM((4, SLOTS, W, W), F32),
             pltpu.SemaphoreType.DMA((2,)),
             pltpu.SemaphoreType.DMA((4, SLOTS // CHUNK)),
-        ],
+            pltpu.SemaphoreType.DMA((6,)),
+        ]
+        + [pltpu.VMEM((2, 2, 2, NXH, NZH, names[3], 8, W), F32) for names in GROUPS],
         cost_estimate=pl.CostEstimate(flops=SLOTS * 6 * 5 * W * W * W, bytes_accessed=SLOTS * 5 * W * W * 4, transcendentals=0),
         name="schur",
     )(counts, tiles, own, oth, *panels)
@@ -155,12 +172,12 @@
 
 def place_kernel(in_ref, out_ref):
     cam = camera_index()
-    x = lax.axis_index("x")
+    x = lax.axis_index("xh") * NXL + lax.axis_index("xl")
     out_ref[...] = jnp.zeros_like(out_ref)
 
     def total(tile):
         value = in_ref[0, tile]
-        for source in range(1, NZH):
+        for source in range(1, NXH * NZH):
             value = value + in_ref[source, tile]
         return value
 
@@ -201,15 +218,33 @@
     m_oth = swap(m_own, "c")
     c3 = swap(c2, "c")
 
-    acc = schur(counts, tiles.T, m_own, m_oth, (c0, c1, c2, c3))
-    got = lax.all_to_all(acc, ("x", "zl", "yl"), 0, 0, tiled=True)
-    part = got.sum(axis=0)
-    return place(lax.all_to_all(part, "zh", 0, 0, tiled=True))
+    outs = schur(counts, tiles.T, m_own, m_oth, (c0, c1, c2, c3))
+    groups = [(outs[2 * k], outs[2 * k + 1]) for k in range(3)]
+    for phase in range(3):
+        received = []
+        for k, (send, _) in enumerate(groups):
+            received.append(swap(send, GROUPS[k][phase]))
+        if phase == 2:
+            break
+        split_groups = []
+        for k, (_, keep) in enumerate(groups):
+            bit = lax.axis_index(GROUPS[k][phase + 1])
+            halves = [
+                lax.dynamic_index_in_dim(keep, at, keepdims=False)
+                + lax.dynamic_index_in_dim(received[k], at, keepdims=False)
+                for at in (1 - bit, bit)
+            ]
+            split_groups.append(tuple(halves))
+        groups = split_groups
+    part = jnp.concatenate(
+        [(keep + got).reshape(NXH * NZH, -1, 8, W) for (_, keep), got in zip(groups, received)], axis=1
+    )
+    return place(lax.all_to_all(part, ("xh", "zh"), 0, 0, tiled=True))
 
 
 def solution(mesh):
-    fine = Mesh(mesh.devices.reshape(NX, NZH, NZL, NYL, 2, 2), ("x", "zh", "zl", "yl", "yh", "c"))
-    rows = ("x", "zh", "zl", "yl")
+    fine = Mesh(mesh.devices.reshape(NXH, NXL, NZH, NZL, NYL, 2, 2), ("xh", "xl", "zh", "zl", "yl", "yh", "c"))
+    rows = ("xh", "xl", "zh", "zl", "yl")
     cams = ("yh", "c")
     in_specs = (
         P(),

time: 119 us -> 116 us (0.975)
  blocking collectives: 68.4 us -> 23.2 us
  waiting for transfers between devices: 24.7 us -> 45.5 us
  starting transfers between devices: 3.97 us -> 23.4 us
  other arithmetic: 2 us -> 3.62 us
    all_to_all x2 -> x1, blocking collectives: 68.4 us -> 23.2 us  [on_device(): return place(lax.all_to_all(part, ('xh', 'zh'), 0, 0, tiled=True))]
    ppermute x6 -> x15, waiting for transfers between devices: 24.7 us -> 45.5 us  [swap(): return lax.ppermute(value, axis, [(0, 1), (1, 0)])]
    ppermute x6 -> x15, starting transfers between devices: 3.97 us -> 23.4 us  [swap(): return lax.ppermute(value, axis, [(0, 1), (1, 0)])]
    add x0 -> x9, other arithmetic: none -> 2.44 us  [the longest x6 2.35 us: on_device(): lax.dynamic_index_in_dim(keep, at, keepdims=False)]
  transfers between devices with their start and end apart: 6 -> 15, of which waited for: 3 -> 9; matrix products, arithmetic and copies ran while one was open for 1% -> 3% of each run, Pallas kernels for 8% -> 9%
where the time goes in v3:
time: 116 us; the launch traced here: 115 us
  waiting for transfers between devices  45.5 us (39%)
  starting transfers between devices  23.4 us (20%)
  blocking collectives  23.2 us (20%)
  Pallas kernels  18.1 us (16%)
  other arithmetic  3.62 us (3%)
  local copies, waits for them, and re-layouts  1.23 us (1%)
    ppermute x15, waiting for transfers between devices, swap(): return lax.ppermute(value, axis, [(0, 1), (1, 0)])  45.5 us
    ppermute x15, starting transfers between devices, swap(): return lax.ppermute(value, axis, [(0, 1), (1, 0)])  23.4 us
    all_to_all x1, blocking collectives, on_device(): return place(lax.all_to_all(part, ('xh', 'zh'), 0, 0, tiled=True))  23.2 us
    pallas_call x2, Pallas kernels, coupling(): pl.pallas_call(kernel, out_shape=jax.ShapeDtypeStruct((HALF, W, W), F32),...  10 us
    pallas_call x1, Pallas kernels, schur(): pl.pallas_call(schur_kernel, out_shape=[jax.ShapeDtypeStruct((2, 2, NXH,...  6.36 us
    add x6, other arithmetic, on_device(): lax.dynamic_index_in_dim(keep, at, keepdims=False)  2.35 us
  transfers between devices with their start and end apart: 15, of which 9 were waited for; matrix products, arithmetic and copies ran while one was open for 3% of the time, Pallas kernels for 9%

profile of v3, /device:TPU:16, one launch (start us, length us, event | category | flops | bytes accessed | tf_op | source)
XLA Modules:
  0.0 115.2 jit_solution(13420507511674637244)
XLA Ops:
  0.0 2.0 %collective-permute-start.4 = (f32[16,128,128]{2,1,0:T(8,128)}, f32[16,128,128]{2,1,0:T(8,128)S(1)}, u32[]{:S(2)}, u32[]{:S(2)}) collective-permute-start(f32[16,128,128]{2,1,0:T(8,128)} %c0_hbm.1), channel_id=1, source_target_pairs={{0,2},{2,0},{1,3},{3,1},{4,6},{6,4},{5,7},{7,5},{8,10},{10,8},{9,1... | collective-permute-start | bytes 3145736 | tf_op jit(solution)/shard_map/ppermute | solution.py:202
  2.0 5.0 %coupling.3 = f32[8,128,128]{2,1,0:T(8,128)} custom-call(f32[16,3,128,128]{3,2,1,0:T(8,128)} %bitcast.48, f32[3,3,16,128]{3,2,1,0:T(8,128)} %bitcast.53), custom_call_target="tpu_custom_call" | custom-call | flops 301989888 | bytes 2097152 | tf_op jit(solution)/shard_map/coupling/pallas_call | solution.py:65
  7.0 0.0 copy-start.1
  7.1 0.1 collective-permute-start
  7.2 5.0 %coupling.2 = f32[8,128,128]{2,1,0:T(8,128)} custom-call(f32[16,3,128,128]{3,2,1,0:T(8,128)} %bitcast.49, f32[3,3,16,128]{3,2,1,0:T(8,128)} %bitcast.54), custom_call_target="tpu_custom_call" | custom-call | flops 301989888 | bytes 2097152 | tf_op jit(solution)/shard_map/coupling/pallas_call | solution.py:65
  12.2 0.0 collective-permute-done
  12.2 1.1 add.124
  13.3 1.6 %collective-permute-start.1 = (f32[8,128,128]{2,1,0:T(8,128)S(1)}, f32[8,128,128]{2,1,0:T(8,128)S(1)}, u32[]{:S(2)}, u32[]{:S(2)}) collective-permute-start(f32[8,128,128]{2,1,0:T(8,128)S(1)} %add.124), channel_id=1, source_target_pairs={{0,2},{2,0},{1,3},{3,1},{4,6},{6,4},{5,7},{7,5},{8,10},{10,8},{9,1... | collective-permute-start | bytes 1572872 | tf_op jit(solution)/shard_map/ppermute | solution.py:202
  14.9 0.0 copy-done.1
  14.9 0.2 collective-permute-start.3
  15.1 12.7 %collective-permute-done.4.c2_hbm = f32[16,128,128]{2,1,0:T(8,128)S(1)} collective-permute-done((f32[16,128,128]{2,1,0:T(8,128)}, f32[16,128,128]{2,1,0:T(8,128)S(1)}, u32[]{:S(2)}, u32[]{:S(2)}) %collective-permute-start.4) | collective-permute-done | bytes 1048608 | tf_op jit(solution)/shard_map/ppermute | solution.py:202
  27.7 0.0 collective-permute-start.5
  27.8 10.1 %collective-permute-done.1 = f32[8,128,128]{2,1,0:T(8,128)S(1)} collective-permute-done((f32[8,128,128]{2,1,0:T(8,128)S(1)}, f32[8,128,128]{2,1,0:T(8,128)S(1)}, u32[]{:S(2)}, u32[]{:S(2)}) %collective-permute-start.1) | collective-permute-done | bytes 524320 | tf_op jit(solution)/shard_map/ppermute | solution.py:202
  37.9 0.1 add.125.own_hbm
  37.9 0.0 copy-start
  37.9 0.1 collective-permute-start.2
  38.0 0.0 collective-permute-done.3.c1_hbm
  38.0 0.0 copy-start.3
  38.0 1.9 %collective-permute-done.2.oth_hbm = f32[8,128,128]{2,1,0:T(8,128)S(1)} collective-permute-done((f32[8,128,128]{2,1,0:T(8,128)S(1)}, f32[8,128,128]{2,1,0:T(8,128)S(1)}, u32[]{:S(2)}, u32[]{:S(2)}) %collective-permute-start.2) | collective-permute-done | bytes 524320 | tf_op jit(solution)/shard_map/ppermute | solution.py:202
  39.9 0.0 collective-permute-done.5.c3_hbm
  39.9 0.0 copy-done.3
  39.9 0.0 copy-start.4
  39.9 1.0 copy-done.4
  41.0 0.2 copy-done.6
  41.2 6.4 %schur.1 = (f32[2,2,2,4,4,8,128]{6,5,4,3,2,1,0:T(8,128)}, f32[2,2,2,4,4,8,128]{6,5,4,3,2,1,0:T(8,128)}, f32[2,2,2,4,4,8,128]{6,5,4,3,2,1,0:T(8,128)}, f32[2,2,2,...) custom-call(s32[64]{0:T(128)} %counts_ref.1, ...), custom_call_target="tpu_custom_call" | custom-call | flops 1006632960 | bytes 5242880 | tf_op jit(solution)/shard_map/schur/pallas_call | solution.py:155
  47.5 1.6 %collective-permute-start.6 = (f32[2,2,2,4,4,8,128]{6,5,4,3,2,1,0:T(8,128)}, f32[2,2,2,4,4,8,128]{6,5,4,3,2,1,0:T(8,128)S(1)}, u32[]{:S(2)}, u32[]{:S(2)}) collective-permute-start(f32[2,2,2,4,4,8,128]{6,5,4,3,2,1,0:T(8,128)} %get-tuple-element.12), channel_id=1, source_target_pairs={{0,64},{64,0},{1,65},{65,1},{2,66},{66,2},{3,67},{67,3},{4,68},{68... | collective-permute-start | bytes 1572872 | tf_op jit(solution)/shard_map/ppermute | solution.py:202
  49.1 3.0 %collective-permute-start.9 = (f32[2,2,2,4,4,8,128]{6,5,4,3,2,1,0:T(8,128)}, f32[2,2,2,4,4,8,128]{6,5,4,3,2,1,0:T(8,128)S(1)}, u32[]{:S(2)}, u32[]{:S(2)}) collective-permute-start(f32[2,2,2,4,4,8,128]{6,5,4,3,2,1,0:T(8,128)} %get-tuple-element.14), channel_id=1, source_target_pairs={{0,8},{8,0},{1,9},{9,1},{2,10},{10,2},{3,11},{11,3},{4,12},{12,4},... | collective-permute-start | bytes 1572872 | tf_op jit(solution)/shard_map/ppermute | solution.py:202
  52.1 2.0 %collective-permute-start.12 = (f32[2,2,2,4,5,8,128]{6,5,4,3,2,1,0:T(8,128)}, f32[2,2,2,4,5,8,128]{6,5,4,3,2,1,0:T(8,128)S(1)}, u32[]{:S(2)}, u32[]{:S(2)}) collective-permute-start(f32[2,2,2,4,5,8,128]{6,5,4,3,2,1,0:T(8,128)} %get-tuple-element.16), channel_id=1, source_target_pairs={{0,4},{4,0},{1,5},{5,1},{2,6},{6,2},{3,7},{7,3},{8,12},{12,8},{9,1... | collective-permute-start | bytes 1966088 | tf_op jit(solution)/shard_map/ppermute | solution.py:202
  54.0 7.7 %collective-permute-done.6 = f32[2,2,2,4,4,8,128]{6,5,4,3,2,1,0:T(8,128)S(1)} collective-permute-done((f32[2,2,2,4,4,8,128]{6,5,4,3,2,1,0:T(8,128)}, f32[2,2,2,4,4,8,128]{6,5,4,3,2,1,0:T(8,128)S(1)}, u32[]{:S(2)}, u32[]{:S(2)}) %collective-permute-start.6) | collective-permute-done | bytes 524320 | tf_op jit(solution)/shard_map/ppermute | solution.py:202
  61.8 1.1 dynamic-slice_add_fusion.2
  62.9 2.8 %collective-permute-start.7 = (f32[2,2,4,4,8,128]{5,4,3,2,1,0:T(8,128)S(1)}, f32[2,2,4,4,8,128]{5,4,3,2,1,0:T(8,128)S(1)}, u32[]{:S(2)}, u32[]{:S(2)}) collective-permute-start(f32[2,2,4,4,8,128]{5,4,3,2,1,0:T(8,128)S(1)} %get-tuple-element.20), channel_id=1, source_target_pairs={{0,8},{8,0},{1,9},{9,1},{2,10},{10,2},{3,11},{11,3},{4,12},{12,4},... | collective-permute-start | bytes 786440 | tf_op jit(solution)/shard_map/ppermute | solution.py:202
  65.7 0.0 collective-permute-done.9
  65.7 1.1 dynamic-slice_add_fusion.1
  66.8 3.9 %collective-permute-start.10 = (f32[2,2,4,4,8,128]{5,4,3,2,1,0:T(8,128)S(1)}, f32[2,2,4,4,8,128]{5,4,3,2,1,0:T(8,128)S(1)}, u32[]{:S(2)}, u32[]{:S(2)}) collective-permute-start(f32[2,2,4,4,8,128]{5,4,3,2,1,0:T(8,128)S(1)} %get-tuple-element.22), channel_id=1, source_target_pairs={{0,4},{4,0},{1,5},{5,1},{2,6},{6,2},{3,7},{7,3},{8,12},{12,8},{9,1... | collective-permute-start | bytes 786440 | tf_op jit(solution)/shard_map/ppermute | solution.py:202
  70.7 1.0 collective-permute-done.7
  71.7 3.5 %collective-permute-start.8 = (f32[2,4,4,8,128]{4,3,2,1,0:T(8,128)S(1)}, f32[2,4,4,8,128]{4,3,2,1,0:T(8,128)S(1)}, u32[]{:S(2)}, u32[]{:S(2)}) collective-permute-start(f32[2,4,4,8,128]{4,3,2,1,0:T(8,128)S(1)} %fusion.2), channel_id=1, source_target_pairs={{0,4},{4,0},{1,5},{5,1},{2,6},{6,2},{3,7},{7,3},{8,12},{12,8},{9,1... | collective-permute-start | bytes 393224 | tf_op jit(solution)/shard_map/ppermute | solution.py:202
  75.2 0.0 collective-permute-done.12
  75.2 0.1 dynamic-slice_add_fusion
  75.3 0.7 collective-permute-start.13
  76.0 1.7 %collective-permute-done.10 = f32[2,2,4,4,8,128]{5,4,3,2,1,0:T(8,128)S(1)} collective-permute-done((f32[2,2,4,4,8,128]{5,4,3,2,1,0:T(8,128)S(1)}, f32[2,2,4,4,8,128]{5,4,3,2,1,0:T(8,128)S(1)}, u32[]{:S(2)}, u32[]{:S(2)}) %collective-permute-start.10) | collective-permute-done | bytes 262176 | tf_op jit(solution)/shard_map/ppermute | solution.py:202
  77.6 0.5 collective-permute-start.11
  78.1 0.9 collective-permute-done.8
  79.1 5.7 %collective-permute-done.13 = f32[2,2,4,5,8,128]{5,4,3,2,1,0:T(8,128)S(1)} collective-permute-done((f32[2,2,4,5,8,128]{5,4,3,2,1,0:T(8,128)S(1)}, f32[2,2,4,5,8,128]{5,4,3,2,1,0:T(8,128)S(1)}, u32[]{:S(2)}, u32[]{:S(2)}) %collective-permute-start.13) | collective-permute-done | bytes 327712 | tf_op jit(solution)/shard_map/ppermute | solution.py:202
  84.8 1.6 %collective-permute-start.14 = (f32[2,4,5,8,128]{4,3,2,1,0:T(8,128)S(1)}, f32[2,4,5,8,128]{4,3,2,1,0:T(8,128)S(1)}, u32[]{:S(2)}, u32[]{:S(2)}) collective-permute-start(f32[2,4,5,8,128]{4,3,2,1,0:T(8,128)S(1)} %fusion), channel_id=1, source_target_pairs={{0,8},{8,0},{1,9},{9,1},{2,10},{10,2},{3,11},{11,3},{4,12},{12,4},... | collective-permute-start | bytes 491528 | tf_op jit(solution)/shard_map/ppermute | solution.py:202
  86.4 0.0 collective-permute-done.11
  86.5 3.7 %collective-permute-done.14 = f32[2,4,5,8,128]{4,3,2,1,0:T(8,128)S(1)} collective-permute-done((f32[2,4,5,8,128]{4,3,2,1,0:T(8,128)S(1)}, f32[2,4,5,8,128]{4,3,2,1,0:T(8,128)S(1)}, u32[]{:S(2)}, u32[]{:S(2)}) %collective-permute-start.14) | collective-permute-done | bytes 163872 | tf_op jit(solution)/shard_map/ppermute | solution.py:202
  90.3 23.2 %all_to_all.5.in_ref = f32[8,13,8,128]{3,2,1,0:T(8,128)} all-to-all(f32[8,13,8,128]{3,2,1,0:T(8,128)S(1)} %pad_maximum_fusion), channel_id=1, replica_groups=mesh['xh'=2,'xl'=2,'zh'=4,'zl'=2,'yl'=2,'yh'=2,'c'=2] {'xh','zh'}, dimensions={0} | all-to-all | bytes 851968 | tf_op jit(solution)/shard_map/all_to_all | solution.py:242
  113.5 1.7 %place.1 = f32[1,8,2048]{2,1,0:T(8,128)} custom-call(f32[8,13,8,128]{3,2,1,0:T(8,128)} %all_to_all.5.in_ref), custom_call_target="tpu_custom_call" | custom-call | tf_op jit(solution)/shard_map/place/pallas_call | solution.py:192
  (13 shorter events, 0.2 us)
Async XLA Ops:
  0.0 27.7 %collective-permute-start.4 = (f32[16,128,128]{2,1,0:T(8,128)}, f32[16,128,128]{2,1,0:T(8,128)S(1)}, u32[]{:S(2)}, u32[]{:S(2)}) collective-permute-start(f32[16,128,128]{2,1,0:T(8,128)} %c0_hbm.1), channel_id=1, source_target_pairs={{0,2},{2,0},{1,3},{3,1},{4,6},{6,4},{5,7},{7,5},{8,10},{10,8},{9,1... | collective-permute-start | bytes 3145736 | tf_op jit(solution)/shard_map/ppermute | solution.py:202
  7.0 7.9 %copy-start.1 = (f32[16,128,128]{2,1,0:T(8,128)S(1)}, f32[16,128,128]{2,1,0:T(8,128)}, u32[]{:S(2)}) copy-start(f32[16,128,128]{2,1,0:T(8,128)} %c0_hbm.1) | copy-start | bytes 3145732
  7.1 5.2 %collective-permute-start = (f32[8,128,128]{2,1,0:T(8,128)}, f32[8,128,128]{2,1,0:T(8,128)S(1)}, u32[]{:S(2)}, u32[]{:S(2)}) collective-permute-start(f32[8,128,128]{2,1,0:T(8,128)} %coupling.3), channel_id=1, source_target_pairs={{0,1},{1,0},{2,3},{3,2},{4,5},{5,4},{6,7},{7,6},{8,9},{9,8},{10,11... | collective-permute-start | bytes 1572872 | tf_op jit(solution)/shard_map/ppermute | solution.py:202
  13.3 24.5 %collective-permute-start.1 = (f32[8,128,128]{2,1,0:T(8,128)S(1)}, f32[8,128,128]{2,1,0:T(8,128)S(1)}, u32[]{:S(2)}, u32[]{:S(2)}) collective-permute-start(f32[8,128,128]{2,1,0:T(8,128)S(1)} %add.124), channel_id=1, source_target_pairs={{0,2},{2,0},{1,3},{3,1},{4,6},{6,4},{5,7},{7,5},{8,10},{10,8},{9,1... | collective-permute-start | bytes 1572872 | tf_op jit(solution)/shard_map/ppermute | solution.py:202
  14.9 23.1 %collective-permute-start.3 = (f32[16,128,128]{2,1,0:T(8,128)S(1)}, f32[16,128,128]{2,1,0:T(8,128)S(1)}, u32[]{:S(2)}, u32[]{:S(2)}) collective-permute-start(f32[16,128,128]{2,1,0:T(8,128)S(1)} %copy-done.1), channel_id=1, source_target_pairs={{0,1},{1,0},{2,3},{3,2},{4,5},{5,4},{6,7},{7,6},{8,9},{9,8},{10,11... | collective-permute-start | bytes 3145736 | tf_op jit(solution)/shard_map/ppermute | solution.py:202
  27.7 13.2 %copy-start.2 = (f32[16,128,128]{2,1,0:T(8,128)}, f32[16,128,128]{2,1,0:T(8,128)S(1)}, u32[]{:S(2)}) copy-start(f32[16,128,128]{2,1,0:T(8,128)S(1)} %collective-permute-done.4.c2_hbm) | copy-start | bytes 3145732
  27.7 12.2 %collective-permute-start.5 = (f32[16,128,128]{2,1,0:T(8,128)S(1)}, f32[16,128,128]{2,1,0:T(8,128)S(1)}, u32[]{:S(2)}, u32[]{:S(2)}) collective-permute-start(f32[16,128,128]{2,1,0:T(8,128)S(1)} %collective-permute-done.4.c2_hbm), channel_id=1, source_target_pairs={{0,1},{1,0},{2,3},{3,2},{4,5},{5,4},{6,7},{7,6},{8,9},{9,8},{10,11... | collective-permute-start | bytes 3145736 | tf_op jit(solution)/shard_map/ppermute | solution.py:202
  37.9 3.0 %copy-start = (f32[8,128,128]{2,1,0:T(8,128)}, f32[8,128,128]{2,1,0:T(8,128)S(1)}, u32[]{:S(2)}) copy-start(f32[8,128,128]{2,1,0:T(8,128)S(1)} %add.125.own_hbm) | copy-start | bytes 1572868
  37.9 2.0 %collective-permute-start.2 = (f32[8,128,128]{2,1,0:T(8,128)S(1)}, f32[8,128,128]{2,1,0:T(8,128)S(1)}, u32[]{:S(2)}, u32[]{:S(2)}) collective-permute-start(f32[8,128,128]{2,1,0:T(8,128)S(1)} %add.125.own_hbm), channel_id=1, source_target_pairs={{0,1},{1,0},{2,3},{3,2},{4,5},{5,4},{6,7},{7,6},{8,9},{9,8},{10,11... | collective-permute-start | bytes 1572872 | tf_op jit(solution)/shard_map/ppermute | solution.py:202
  38.0 1.9 %copy-start.3 = (f32[16,128,128]{2,1,0:T(8,128)}, f32[16,128,128]{2,1,0:T(8,128)S(1)}, u32[]{:S(2)}) copy-start(f32[16,128,128]{2,1,0:T(8,128)S(1)} %collective-permute-done.3.c1_hbm) | copy-start | bytes 3145732
  39.9 1.2 %copy-start.6 = (f32[8,128,128]{2,1,0:T(8,128)}, f32[8,128,128]{2,1,0:T(8,128)S(1)}, u32[]{:S(2)}) copy-start(f32[8,128,128]{2,1,0:T(8,128)S(1)} %collective-permute-done.2.oth_hbm) | copy-start | bytes 1572868
  39.9 1.0 copy-start.4
  47.5 27.7 %copy-start.5 = (f32[2,2,2,4,5,8,128]{6,5,4,3,2,1,0:T(8,128)S(1)}, f32[2,2,2,4,5,8,128]{6,5,4,3,2,1,0:T(8,128)}, u32[]{:S(2)}) copy-start(f32[2,2,2,4,5,8,128]{6,5,4,3,2,1,0:T(8,128)} %get-tuple-element.15) | copy-start | bytes 1966084
  47.5 14.3 %collective-permute-start.6 = (f32[2,2,2,4,4,8,128]{6,5,4,3,2,1,0:T(8,128)}, f32[2,2,2,4,4,8,128]{6,5,4,3,2,1,0:T(8,128)S(1)}, u32[]{:S(2)}, u32[]{:S(2)}) collective-permute-start(f32[2,2,2,4,4,8,128]{6,5,4,3,2,1,0:T(8,128)} %get-tuple-element.12), channel_id=1, source_target_pairs={{0,64},{64,0},{1,65},{65,1},{2,66},{66,2},{3,67},{67,3},{4,68},{68... | collective-permute-start | bytes 1572872 | tf_op jit(solution)/shard_map/ppermute | solution.py:202
  49.1 16.6 %collective-permute-start.9 = (f32[2,2,2,4,4,8,128]{6,5,4,3,2,1,0:T(8,128)}, f32[2,2,2,4,4,8,128]{6,5,4,3,2,1,0:T(8,128)S(1)}, u32[]{:S(2)}, u32[]{:S(2)}) collective-permute-start(f32[2,2,2,4,4,8,128]{6,5,4,3,2,1,0:T(8,128)} %get-tuple-element.14), channel_id=1, source_target_pairs={{0,8},{8,0},{1,9},{9,1},{2,10},{10,2},{3,11},{11,3},{4,12},{12,4},... | collective-permute-start | bytes 1572872 | tf_op jit(solution)/shard_map/ppermute | solution.py:202
  52.1 23.2 %collective-permute-start.12 = (f32[2,2,2,4,5,8,128]{6,5,4,3,2,1,0:T(8,128)}, f32[2,2,2,4,5,8,128]{6,5,4,3,2,1,0:T(8,128)S(1)}, u32[]{:S(2)}, u32[]{:S(2)}) collective-permute-start(f32[2,2,2,4,5,8,128]{6,5,4,3,2,1,0:T(8,128)} %get-tuple-element.16), channel_id=1, source_target_pairs={{0,4},{4,0},{1,5},{5,1},{2,6},{6,2},{3,7},{7,3},{8,12},{12,8},{9,1... | collective-permute-start | bytes 1966088 | tf_op jit(solution)/shard_map/ppermute | solution.py:202
  62.9 8.8 %collective-permute-start.7 = (f32[2,2,4,4,8,128]{5,4,3,2,1,0:T(8,128)S(1)}, f32[2,2,4,4,8,128]{5,4,3,2,1,0:T(8,128)S(1)}, u32[]{:S(2)}, u32[]{:S(2)}) collective-permute-start(f32[2,2,4,4,8,128]{5,4,3,2,1,0:T(8,128)S(1)} %get-tuple-element.20), channel_id=1, source_target_pairs={{0,8},{8,0},{1,9},{9,1},{2,10},{10,2},{3,11},{11,3},{4,12},{12,4},... | collective-permute-start | bytes 786440 | tf_op jit(solution)/shard_map/ppermute | solution.py:202
  66.8 10.8 %collective-permute-start.10 = (f32[2,2,4,4,8,128]{5,4,3,2,1,0:T(8,128)S(1)}, f32[2,2,4,4,8,128]{5,4,3,2,1,0:T(8,128)S(1)}, u32[]{:S(2)}, u32[]{:S(2)}) collective-permute-start(f32[2,2,4,4,8,128]{5,4,3,2,1,0:T(8,128)S(1)} %get-tuple-element.22), channel_id=1, source_target_pairs={{0,4},{4,0},{1,5},{5,1},{2,6},{6,2},{3,7},{7,3},{8,12},{12,8},{9,1... | collective-permute-start | bytes 786440 | tf_op jit(solution)/shard_map/ppermute | solution.py:202
  71.7 7.3 %collective-permute-start.8 = (f32[2,4,4,8,128]{4,3,2,1,0:T(8,128)S(1)}, f32[2,4,4,8,128]{4,3,2,1,0:T(8,128)S(1)}, u32[]{:S(2)}, u32[]{:S(2)}) collective-permute-start(f32[2,4,4,8,128]{4,3,2,1,0:T(8,128)S(1)} %fusion.2), channel_id=1, source_target_pairs={{0,4},{4,0},{1,5},{5,1},{2,6},{6,2},{3,7},{7,3},{8,12},{12,8},{9,1... | collective-permute-start | bytes 393224 | tf_op jit(solution)/shard_map/ppermute | solution.py:202
  75.3 9.5 %collective-permute-start.13 = (f32[2,2,4,5,8,128]{5,4,3,2,1,0:T(8,128)S(1)}, f32[2,2,4,5,8,128]{5,4,3,2,1,0:T(8,128)S(1)}, u32[]{:S(2)}, u32[]{:S(2)}) collective-permute-start(f32[2,2,4,5,8,128]{5,4,3,2,1,0:T(8,128)S(1)} %get-tuple-element.18), channel_id=1, source_target_pairs={{0,64},{64,0},{1,65},{65,1},{2,66},{66,2},{3,67},{67,3},{4,68},{68... | collective-permute-start | bytes 983048 | tf_op jit(solution)/shard_map/ppermute | solution.py:202
  77.6 8.8 %collective-permute-start.11 = (f32[2,4,4,8,128]{4,3,2,1,0:T(8,128)S(1)}, f32[2,4,4,8,128]{4,3,2,1,0:T(8,128)S(1)}, u32[]{:S(2)}, u32[]{:S(2)}) collective-permute-start(f32[2,4,4,8,128]{4,3,2,1,0:T(8,128)S(1)} %fusion.1), channel_id=1, source_target_pairs={{0,64},{64,0},{1,65},{65,1},{2,66},{66,2},{3,67},{67,3},{4,68},{68... | collective-permute-start | bytes 393224 | tf_op jit(solution)/shard_map/ppermute | solution.py:202
  84.8 5.4 %collective-permute-start.14 = (f32[2,4,5,8,128]{4,3,2,1,0:T(8,128)S(1)}, f32[2,4,5,8,128]{4,3,2,1,0:T(8,128)S(1)}, u32[]{:S(2)}, u32[]{:S(2)}) collective-permute-start(f32[2,4,5,8,128]{4,3,2,1,0:T(8,128)S(1)} %fusion), channel_id=1, source_target_pairs={{0,8},{8,0},{1,9},{9,1},{2,10},{10,2},{3,11},{11,3},{4,12},{12,4},... | collective-permute-start | bytes 491528 | tf_op jit(solution)/shard_map/ppermute | solution.py:202

commit v4 on v3

v4 whole, which is shorter than its diff:
```python
import jax
import jax.numpy as jnp
from jax import lax
from jax.experimental import pallas as pl
from jax.experimental.pallas import tpu as pltpu
from jax.sharding import Mesh, PartitionSpec as P


W = 128
SLOTS = 16
HALF = SLOTS // 2
CHUNK = 4
GT = 4
NXH, NXL, NZH, NZL, NYL = 2, 2, 4, 2, 2
GROUPS = (("xl", "zl", "yl", GT + 1), ("zl", "yl", "xl", GT), ("yl", "xl", "zl", GT))
F32 = jnp.float32
BF16 = jnp.bfloat16
ANY = pl.BlockSpec(memory_space=pl.ANY)
SMEM = pl.BlockSpec(memory_space=pltpu.SMEM)
VMEM = pl.BlockSpec(memory_space=pltpu.VMEM)
HBM = pl.BlockSpec(memory_space=pltpu.HBM)


def split(value):
    high = value.astype(BF16)
    return high, (value - high.astype(F32)).astype(BF16)


def camera_index():
    return lax.axis_index("yh") * 2 + lax.axis_index("c")


def cluster_device():
    xh, xl, zh, zl, yl = (lax.axis_index(name) for name in ("xh", "xl", "zh", "zl", "yl"))
    return (((xh * NXL + xl) * NZH + zh) * NZL + zl) * NYL + yl


def coupling_kernel(mine, pts_hbm, inv_ref, out_ref, pts_buf, sems):
    core = lax.axis_index("c")
    base = (core if mine else 1 - core) * HALF

    def fetch(i):
        return pltpu.make_async_copy(pts_hbm.at[base + i], pts_buf.at[i], sems.at[i])

    for i in range(HALF):
        fetch(i).start()
    for i in range(HALF):
        fetch(i).wait()
        pts = [pts_buf[i, j] for j in range(3)]
        pairs = []
        for k in range(3):
            weighted = None
            for j in range(3):
                term = pts[j] * inv_ref[j, k, pl.ds(base + i, 1), :]
                weighted = term if weighted is None else weighted + term
            pairs.append((split(weighted), split(pts[k])))
        left = jnp.concatenate([w[0] for w, _ in pairs] + [w[0] for w, _ in pairs] + [w[1] for w, _ in pairs], axis=1)
        right = jnp.concatenate([p[0] for _, p in pairs] + [p[1] for _, p in pairs] + [p[0] for _, p in pairs], axis=1)
        out_ref[i] = lax.dot_general(left, right, (((1,), (1,)), ((), ())), preferred_element_type=F32)


def coupling(mine, pts, inv):
    def kernel(*refs):
        coupling_kernel(mine, *refs)

    return pl.pallas_call(
        kernel,
        out_shape=jax.ShapeDtypeStruct((HALF, W, W), F32),
        in_specs=[HBM, VMEM],
        out_specs=VMEM,
        scratch_shapes=[pltpu.VMEM((HALF, 3, W, W), F32), pltpu.SemaphoreType.DMA((HALF,))],
        cost_estimate=pl.CostEstimate(flops=HALF * 2 * 9 * W * W * W, bytes_accessed=HALF * 4 * W * W * 4, transcendentals=0),
        compiler_params=pltpu.CompilerParams(vmem_limit_bytes=8 << 20),
        name="coupling",
    )(pts, inv)


def schur_kernel(counts_ref, tiles_ref, own_ref, oth_ref, c0_ref, c1_ref, c2_ref, c3_ref, *refs):
    outs, o_sems, accs = refs[:7], refs[7], refs[8:]
    core = lax.axis_index("c")
    cam = camera_index()
    device = cluster_device()
    live = counts_ref[device]
    panels = (c0_ref, c1_ref, c2_ref, c3_ref)

    steps = SLOTS // CHUNK
    for acc in accs:
        acc[...] = jnp.zeros_like(acc)

    for k in range(steps):
        @pl.when(k * CHUNK < live)
        def _():
            for i in range(CHUNK):
                slot = k * CHUNK + i
                m_high, m_low = split(jnp.where(core == k // 2, own_ref[slot % HALF], oth_ref[slot % HALF]))
                panel_t = c0_ref[slot].T
                t_high, t_low = split(panel_t)
                prod = jnp.dot(
                    jnp.concatenate([t_high, t_high, t_low], axis=1),
                    jnp.concatenate([m_high, m_low, m_high], axis=0),
                    preferred_element_type=F32,
                )
                rest = panel_t - prod
                if i:
                    rest = jnp.where(slot < live, rest, 0.0)
                r_high, r_low = split(rest)
                left = jnp.concatenate([r_high, r_high, r_low], axis=1)
                parts = [split(panels[rel][slot]) for rel in range(4)]
                highs = jnp.concatenate([h for h, _ in parts], axis=1)
                lows = jnp.concatenate([l for _, l in parts], axis=1)
                right = jnp.concatenate([highs, lows, highs], axis=0)
                rows = jnp.dot(left, right, preferred_element_type=F32)
                row_tile = tiles_ref[cam, device * SLOTS + slot]
                for rel in range(4):
                    block = rows[:, rel * W : (rel + 1) * W].reshape(NZH, NZL, NYL, 8, W)

                    def add(group, tile, block=block):
                        for zl in range(NZL):
                            for yl in range(NYL):
                                at = {"xl": lax.rem(row_tile, NXL), "zl": zl, "yl": yl}
                                lead = tuple(at[name] for name in GROUPS[group][:3])
                                accs[group][lead + (row_tile // NXL, slice(None), tile)] += block[:, zl, yl]

                    if rel == 0:
                        add(0, GT)
                        continue
                    tile = tiles_ref[lax.bitwise_xor(cam, rel), device * SLOTS + slot]
                    add(rel - 1, tile)

    copies = []
    for group, names in enumerate(GROUPS):
        bit = lax.axis_index(names[0])
        away = accs[group].at[1 - bit]
        copies += [away.at[0], away.at[1]] if group == 0 else [away]
        copies.append(accs[group].at[bit])
    copies = [pltpu.make_async_copy(source, outs[k], o_sems.at[k]) for k, source in enumerate(copies)]
    for copy in copies:
        copy.start()
    for copy in copies:
        copy.wait()


def schur(counts, tiles, own, oth, panels):
    return pl.pallas_call(
        schur_kernel,
        out_shape=[
            jax.ShapeDtypeStruct(lead + (2, NXH, NZH, names[3], 8, W), F32) for k, names in enumerate(GROUPS)
            for lead in (((), (), (2,)) if k == 0 else ((2,), (2,)))
        ],
        in_specs=[SMEM, SMEM] + [VMEM] * 6,
        out_specs=[ANY] * 7,
        scratch_shapes=[
            pltpu.SemaphoreType.DMA((7,)),
        ]
        + [pltpu.VMEM((2, 2, 2, NXH, NZH, names[3], 8, W), F32) for names in GROUPS],
        cost_estimate=pl.CostEstimate(flops=SLOTS * 6 * 5 * W * W * W, bytes_accessed=SLOTS * 5 * W * W * 4, transcendentals=0),
        compiler_params=pltpu.CompilerParams(vmem_limit_bytes=12 << 20),
        name="schur",
    )(counts, tiles, *[pltpu.with_memory_space_constraint(v, pltpu.VMEM) for v in (own, oth, *panels)])


def place_kernel(in_ref, out_ref):
    cam = camera_index()
    x = lax.axis_index("xh") * NXL + lax.axis_index("xl")
    out_ref[...] = jnp.zeros_like(out_ref)

    def total(tile):
        value = in_ref[0, tile]
        for source in range(1, NXH * NZH):
            value = value + in_ref[source, tile]
        return value

    row = 0
    for rel, t in [(1, t) for t in range(GT)] + [(0, x)] + [(rel, t) for rel in (2, 3) for t in range(GT)]:
        column = lax.bitwise_xor(cam, rel) * GT + t
        out_ref[0, :, pl.ds(pl.multiple_of(column * W, W), W)] = total(row)
        row += 1


def place(pieces):
    return pl.pallas_call(
        place_kernel,
        out_shape=jax.ShapeDtypeStruct((1, 8, 4 * GT * W), F32),
        in_specs=[VMEM],
        out_specs=VMEM,
        compiler_params=pltpu.CompilerParams(vmem_limit_bytes=4 << 20),
        name="place",
    )(pieces)


def halve_kernel(axis, keep_ref, *refs):
    parts, send_ref, out_ref = refs[:-2], refs[-2], refs[-1]
    bit = lax.axis_index(axis)
    for at in range(2):
        value = keep_ref[at] + (parts[at][...] if len(parts) == 2 else parts[0][at])

        @pl.when(bit == at)
        def _():
            out_ref[...] = value

        @pl.when(bit != at)
        def _():
            send_ref[...] = value


def halve(axis, keep, parts):
    def kernel(*refs):
        halve_kernel(axis, *refs)

    return pl.pallas_call(
        kernel,
        out_shape=[jax.ShapeDtypeStruct(keep.shape[1:], F32)] * 2,
        in_specs=[VMEM] * (1 + len(parts)),
        out_specs=[VMEM] * 2,
        compiler_params=pltpu.CompilerParams(vmem_limit_bytes=4 << 20),
        name="halve",
    )(*[pltpu.with_memory_space_constraint(v, pltpu.VMEM) for v in (keep, *parts)])


def swap_x_other(value):
    size = NXH * NXL
    return lax.ppermute(value, ("xh", "xl"), [(i, (i + 1 if i % 2 else i - 1) % size) for i in range(size)])


def swap(value, axis):
    return lax.ppermute(value, axis, [(0, 1), (1, 0)])


def on_device(counts, tiles, cam_jac, point_jac, point_inv):
    pts = point_jac.transpose(0, 2, 1, 3)
    inv = point_inv.transpose(1, 2, 0, 3)

    c0 = cam_jac
    c2 = swap(c0, "yh")
    c1 = swap(c0, "c")

    m_send = coupling(False, pts, inv)
    m_recv = swap(m_send, "c")
    m_keep = coupling(True, pts, inv)
    m_chip = m_keep + m_recv
    m_own = m_chip + swap(m_chip, "yh")
    m_oth = swap(m_own, "c")
    c3 = swap(c2, "c")

    outs = schur(counts, tiles.T, m_own, m_oth, (c0, c1, c2, c3))
    near_z = swap(outs[3], "zl")
    near_y = swap(outs[5], "yl")
    low_x = swap(outs[0], "xl")
    high_x = swap_x_other(outs[1])
    groups = [(outs[2], (low_x, high_x)), (outs[4], (near_z,)), (outs[6], (near_y,))]
    for phase in (1, 2):
        halves = []
        for k, (keep, parts) in enumerate(groups):
            halves.append(halve(GROUPS[k][phase], keep, parts))
        groups = []
        for k, (send, keep) in enumerate(halves):
            groups.append((keep, (swap(send, GROUPS[k][phase]),)))
    groups = [(keep, parts[0]) for keep, parts in groups]
    received = [got for _, got in groups]
    part = jnp.concatenate(
        [(keep + got).reshape(NXH * NZH, -1, 8, W) for (keep, _), got in zip(groups, received)], axis=1
    )
    return place(lax.all_to_all(part, ("xh", "zh"), 0, 0, tiled=True))


def solution(mesh):
    fine = Mesh(mesh.devices.reshape(NXH, NXL, NZH, NZL, NYL, 2, 2), ("xh", "xl", "zh", "zl", "yl", "yh", "c"))
    rows = ("xh", "xl", "zh", "zl", "yl")
    cams = ("yh", "c")
    in_specs = (
        P(),
        P(),
        P(rows, None, cams),
        P(rows, None, None, cams),
        P(rows, None, None, cams),
    )
    return jax.shard_map(
        on_device, mesh=fine, in_specs=in_specs, out_specs=P(cams, rows, None), check_vma=False
    )
```

time: 116 us -> 99.5 us (0.86)
  Pallas kernels: 18.1 us -> 12.6 us
  starting transfers between devices: 23.4 us -> 18.2 us
  waiting for transfers between devices: 45.5 us -> 42 us
  other arithmetic: 3.62 us -> 0.2 us
  local copies, waits for them, and re-layouts: 1.23 us -> 2.79 us
    ppermute x15, starting transfers between devices: 23.4 us -> 15.5 us  [swap(): return lax.ppermute(value, axis, [(0, 1), (1, 0)])]
    ppermute x15, waiting for transfers between devices: 45.5 us -> 40.8 us  [swap(): return lax.ppermute(value, axis, [(0, 1), (1, 0)])]
    pallas_call x1 -> x7, Pallas kernels: 6.36 us -> 3.19 us  [the longest x1 2.8 us: schur(): pl.pallas_call(schur_kernel, out_shape=[jax.ShapeDtypeStruct(lead + (2, N...]
    ppermute x0 -> x1, starting transfers between devices: none -> 2.78 us  [swap_x_other(): lax.ppermute(value, ('xh', 'xl'), [(i, (i + 1 if i % 2 else i - 1) % size...]
    add x6 -> x0, other arithmetic: 2.35 us -> none  [on_device(): lax.dynamic_index_in_dim(keep, at, keepdims=False)]
    unnamed x14 -> x10, local copies, waits for them, and re-layouts: 1.23 us -> 2.79 us
    pallas_call x2, Pallas kernels: 10 us -> 8.77 us  [coupling(): pl.pallas_call(kernel, out_shape=jax.ShapeDtypeStruct((HALF, W, W), F32),...]
    ppermute x0 -> x1, waiting for transfers between devices: none -> 1.21 us  [swap_x_other(): lax.ppermute(value, ('xh', 'xl'), [(i, (i + 1 if i % 2 else i - 1) % size...]
  transfers between devices with their start and end apart: 15 -> 16, of which waited for: 9 -> 9; matrix products, arithmetic and copies ran while one was open for 3% -> 0% of each run, Pallas kernels for 9% -> 9%
where the time goes in v4:
time: 99.5 us; the launch traced here: 99.1 us
  waiting for transfers between devices  42 us (42%)
  blocking collectives  23.1 us (23%)
  starting transfers between devices  18.2 us (18%)
  Pallas kernels  12.6 us (13%)
  local copies, waits for them, and re-layouts  2.79 us (3%)
    ppermute x15, waiting for transfers between devices, swap(): return lax.ppermute(value, axis, [(0, 1), (1, 0)])  40.8 us
    all_to_all x1, blocking collectives, on_device(): return place(lax.all_to_all(part, ('xh', 'zh'), 0, 0, tiled=True))  23.1 us
    ppermute x15, starting transfers between devices, swap(): return lax.ppermute(value, axis, [(0, 1), (1, 0)])  15.5 us
    pallas_call x2, Pallas kernels, coupling(): pl.pallas_call(kernel, out_shape=jax.ShapeDtypeStruct((HALF, W, W), F32),...  8.77 us
    pallas_call x1, Pallas kernels, schur(): pl.pallas_call(schur_kernel, out_shape=[jax.ShapeDtypeStruct(lead + (2, N...  2.8 us
    unnamed x10, local copies, waits for them, and re-layouts  2.79 us
    ppermute x1, starting transfers between devices, swap_x_other(): lax.ppermute(value, ('xh', 'xl'), [(i, (i + 1 if i % 2 else i - 1) % size...  2.78 us
  transfers between devices with their start and end apart: 16, of which 9 were waited for; matrix products, arithmetic and copies ran while one was open for 0% of the time, Pallas kernels for 9%

profile of v4, /device:TPU:16, one launch (start us, length us, event | category | flops | bytes accessed | tf_op | source)
XLA Modules:
  0.0 99.1 jit_solution(12878508983001528364)
XLA Ops:
  0.0 2.0 %collective-permute-start.4 = (f32[16,128,128]{2,1,0:T(8,128)}, f32[16,128,128]{2,1,0:T(8,128)S(1)}, u32[]{:S(2)}, u32[]{:S(2)}) collective-permute-start(f32[16,128,128]{2,1,0:T(8,128)} %c0_ref.1), channel_id=1, source_target_pairs={{0,2},{2,0},{1,3},{3,1},{4,6},{6,4},{5,7},{7,5},{8,10},{10,8},{9,1... | collective-permute-start | bytes 3145736 | tf_op jit(solution)/shard_map/ppermute | solution.py:226
  2.0 1.9 %copy-done = f32[16,128,3,128]{3,1,2,0:T(8,128)S(1)} copy-done((f32[16,128,3,128]{3,1,2,0:T(8,128)S(1)}, f32[16,128,3,128]{3,1,2,0:T(8,128)}, u32[]{:S(2)}) %copy-start) | copy-done | bytes 3145752
  3.9 0.9 copy-done.2
  4.8 4.4 %coupling.3 = f32[8,128,128]{2,1,0:T(8,128)S(1)} custom-call(f32[16,3,128,128]{3,2,1,0:T(8,128)S(1)} %bitcast.6, f32[3,3,16,128]{3,2,1,0:T(8,128)S(1)} %bitcast.8), custom_call_target="tpu_custom_call" | custom-call | flops 301989888 | bytes 2097152 | tf_op jit(solution)/shard_map/coupling/pallas_call | solution.py:66
  9.2 0.0 copy-start.1
  9.2 0.0 copy-start.3
  9.2 0.0 copy-start.4
  9.2 0.1 collective-permute-start
  9.3 4.4 %coupling.2 = f32[8,128,128]{2,1,0:T(8,128)S(1)} custom-call(f32[16,3,128,128]{3,2,1,0:T(8,128)S(1)} %bitcast.7, f32[3,3,16,128]{3,2,1,0:T(8,128)S(1)} %bitcast.9), custom_call_target="tpu_custom_call" | custom-call | flops 301989888 | bytes 2097152 | tf_op jit(solution)/shard_map/coupling/pallas_call | solution.py:66
  13.7 0.0 collective-permute-done
  13.8 0.1 add.15
  13.8 1.6 %collective-permute-start.1 = (f32[8,128,128]{2,1,0:T(8,128)S(1)}, f32[8,128,128]{2,1,0:T(8,128)S(1)}, u32[]{:S(2)}, u32[]{:S(2)}) collective-permute-start(f32[8,128,128]{2,1,0:T(8,128)S(1)} %add.15), channel_id=1, source_target_pairs={{0,2},{2,0},{1,3},{3,1},{4,6},{6,4},{5,7},{7,5},{8,10},{10,8},{9,1... | collective-permute-start | bytes 1572872 | tf_op jit(solution)/shard_map/ppermute | solution.py:226
  15.4 0.0 copy-done.1
  15.4 0.2 collective-permute-start.3
  15.6 12.2 %collective-permute-done.4.c2_ref = f32[16,128,128]{2,1,0:T(8,128)S(1)} collective-permute-done((f32[16,128,128]{2,1,0:T(8,128)}, f32[16,128,128]{2,1,0:T(8,128)S(1)}, u32[]{:S(2)}, u32[]{:S(2)}) %collective-permute-start.4) | collective-permute-done | bytes 1048608 | tf_op jit(solution)/shard_map/ppermute | solution.py:226
  27.7 0.0 collective-permute-start.5
  27.7 10.1 %collective-permute-done.1 = f32[8,128,128]{2,1,0:T(8,128)S(1)} collective-permute-done((f32[8,128,128]{2,1,0:T(8,128)S(1)}, f32[8,128,128]{2,1,0:T(8,128)S(1)}, u32[]{:S(2)}, u32[]{:S(2)}) %collective-permute-start.1) | collective-permute-done | bytes 524320 | tf_op jit(solution)/shard_map/ppermute | solution.py:226
  37.9 0.1 add.16.own_ref
  37.9 0.1 collective-permute-start.2
  38.0 0.0 collective-permute-done.3.c1_ref
  38.0 1.9 %collective-permute-done.2.oth_ref = f32[8,128,128]{2,1,0:T(8,128)S(1)} collective-permute-done((f32[8,128,128]{2,1,0:T(8,128)S(1)}, f32[8,128,128]{2,1,0:T(8,128)S(1)}, u32[]{:S(2)}, u32[]{:S(2)}) %collective-permute-start.2) | collective-permute-done | bytes 524320 | tf_op jit(solution)/shard_map/ppermute | solution.py:226
  39.9 0.0 collective-permute-done.5.c3_ref
  39.9 2.8 %schur.1 = (f32[2,2,4,5,8,128]{5,4,3,2,1,0:T(8,128)S(1)}, f32[2,2,4,5,8,128]{5,4,3,2,1,0:T(8,128)S(1)}, f32[2,2,2,4,5,8,128]{6,5,4,3,2,1,0:T(8,128)S(1)}, f32[2,...) custom-call(s32[64]{0:T(128)S(1)} %copy-done.4, ...), custom_call_target="tpu_custom_call" | custom-call | flops 1006632960 | bytes 5242880 | tf_op jit(solution)/shard_map/schur/pallas_call | solution.py:144
  42.7 2.0 %collective-permute-start.10 = (f32[2,2,2,4,4,8,128]{6,5,4,3,2,1,0:T(8,128)S(1)}, f32[2,2,2,4,4,8,128]{6,5,4,3,2,1,0:T(8,128)S(1)}, u32[]{:S(2)}, u32[]{:S(2)}) collective-permute-start(f32[2,2,2,4,4,8,128]{6,5,4,3,2,1,0:T(8,128)S(1)} %get-tuple-element.32), channel_id=1, source_target_pairs={{0,8},{8,0},{1,9},{9,1},{2,10},{10,2},{3,11},{11,3},{4,12},{12,4},... | collective-permute-start | bytes 1572872 | tf_op jit(solution)/shard_map/ppermute | solution.py:226
  44.7 4.4 %collective-permute-start.13 = (f32[2,2,2,4,4,8,128]{6,5,4,3,2,1,0:T(8,128)S(1)}, f32[2,2,2,4,4,8,128]{6,5,4,3,2,1,0:T(8,128)S(1)}, u32[]{:S(2)}, u32[]{:S(2)}) collective-permute-start(f32[2,2,2,4,4,8,128]{6,5,4,3,2,1,0:T(8,128)S(1)} %get-tuple-element.38), channel_id=1, source_target_pairs={{0,4},{4,0},{1,5},{5,1},{2,6},{6,2},{3,7},{7,3},{8,12},{12,8},{9,1... | collective-permute-start | bytes 1572872 | tf_op jit(solution)/shard_map/ppermute | solution.py:226
  49.1 0.0 collective-permute-start.6
  49.1 2.8 %collective-permute-start.7 = (f32[2,2,4,5,8,128]{5,4,3,2,1,0:T(8,128)S(1)}, f32[2,2,4,5,8,128]{5,4,3,2,1,0:T(8,128)S(1)}, u32[]{:S(2)}, u32[]{:S(2)}) collective-permute-start(f32[2,2,4,5,8,128]{5,4,3,2,1,0:T(8,128)S(1)} %get-tuple-element.26), channel_id=1, source_target_pairs={{0,192},{64,128},{128,64},{192,0},{1,193},{65,129},{129,65},{193,1... | collective-permute-start | bytes 983048 | tf_op jit(solution)/shard_map/ppermute | solution.py:222
  51.9 6.4 %collective-permute-done.6.refs_1_ = f32[2,2,4,5,8,128]{5,4,3,2,1,0:T(8,128)S(1)} collective-permute-done((f32[2,2,4,5,8,128]{5,4,3,2,1,0:T(8,128)S(1)}, f32[2,2,4,5,8,128]{5,4,3,2,1,0:T(8,128)S(1)}, u32[]{:S(2)}, u32[]{:S(2)}) %collective-permute-start.6) | collective-permute-done | bytes 327712 | tf_op jit(solution)/shard_map/ppermute | solution.py:226
  58.3 1.2 %collective-permute-done.7.refs_2_ = f32[2,2,4,5,8,128]{5,4,3,2,1,0:T(8,128)S(1)} collective-permute-done((f32[2,2,4,5,8,128]{5,4,3,2,1,0:T(8,128)S(1)}, f32[2,2,4,5,8,128]{5,4,3,2,1,0:T(8,128)S(1)}, u32[]{:S(2)}, u32[]{:S(2)}) %collective-permute-start.7) | collective-permute-done | bytes 327712 | tf_op jit(solution)/shard_map/ppermute | solution.py:222
  59.5 0.1 halve.6
  59.6 0.6 collective-permute-start.8
  60.3 0.0 collective-permute-done.10.refs_1_
  60.3 0.1 halve.8
  60.4 1.2 %collective-permute-start.11 = (f32[2,2,4,4,8,128]{5,4,3,2,1,0:T(8,128)S(1)}, f32[2,2,4,4,8,128]{5,4,3,2,1,0:T(8,128)S(1)}, u32[]{:S(2)}, u32[]{:S(2)}) collective-permute-start(f32[2,2,4,4,8,128]{5,4,3,2,1,0:T(8,128)S(1)} %get-tuple-element.34), channel_id=1, source_target_pairs={{0,4},{4,0},{1,5},{5,1},{2,6},{6,2},{3,7},{7,3},{8,12},{12,8},{9,1... | collective-permute-start | bytes 786440 | tf_op jit(solution)/shard_map/ppermute | solution.py:226
  61.6 0.0 collective-permute-done.13.refs_1_
  61.6 0.1 halve.10
  61.7 0.7 collective-permute-start.14
  62.3 5.9 %collective-permute-done.8.refs_1_ = f32[2,2,4,5,8,128]{5,4,3,2,1,0:T(8,128)S(1)} collective-permute-done((f32[2,2,4,5,8,128]{5,4,3,2,1,0:T(8,128)S(1)}, f32[2,2,4,5,8,128]{5,4,3,2,1,0:T(8,128)S(1)}, u32[]{:S(2)}, u32[]{:S(2)}) %collective-permute-start.8) | collective-permute-done | bytes 327712 | tf_op jit(solution)/shard_map/ppermute | solution.py:226
  68.3 1.2 %collective-permute-start.9 = (f32[2,4,5,8,128]{4,3,2,1,0:T(8,128)S(1)}, f32[2,4,5,8,128]{4,3,2,1,0:T(8,128)S(1)}, u32[]{:S(2)}, u32[]{:S(2)}) collective-permute-start(f32[2,4,5,8,128]{4,3,2,1,0:T(8,128)S(1)} %get-tuple-element.30), channel_id=1, source_target_pairs={{0,4},{4,0},{1,5},{5,1},{2,6},{6,2},{3,7},{7,3},{8,12},{12,8},{9,1... | collective-permute-start | bytes 491528 | tf_op jit(solution)/shard_map/ppermute | solution.py:226
  69.5 0.0 collective-permute-done.11.refs_1_
  69.5 0.7 collective-permute-start.12
  70.2 0.0 collective-permute-done.14.refs_1_
  70.2 0.7 collective-permute-start.15
  71.0 2.7 %collective-permute-done.9 = f32[2,4,5,8,128]{4,3,2,1,0:T(8,128)S(1)} collective-permute-done((f32[2,4,5,8,128]{4,3,2,1,0:T(8,128)S(1)}, f32[2,4,5,8,128]{4,3,2,1,0:T(8,128)S(1)}, u32[]{:S(2)}, u32[]{:S(2)}) %collective-permute-start.9) | collective-permute-done | bytes 163872 | tf_op jit(solution)/shard_map/ppermute | solution.py:226
  73.7 0.8 collective-permute-done.12
  74.6 0.7 collective-permute-done.15
  75.4 23.1 %all_to_all.5.in_ref = f32[8,13,8,128]{3,2,1,0:T(8,128)S(1)} all-to-all(f32[8,13,8,128]{3,2,1,0:T(8,128)S(1)} %pad_maximum_fusion), channel_id=1, replica_groups=mesh['xh'=2,'xl'=2,'zh'=4,'zl'=2,'yl'=2,'yh'=2,'c'=2] {'xh','zh'}, dimensions={0} | all-to-all | bytes 851968 | tf_op jit(solution)/shard_map/all_to_all | solution.py:263
  98.5 0.7 place.1
  (11 shorter events, 0.2 us)
Async XLA Ops:
  0.0 27.7 %collective-permute-start.4 = (f32[16,128,128]{2,1,0:T(8,128)}, f32[16,128,128]{2,1,0:T(8,128)S(1)}, u32[]{:S(2)}, u32[]{:S(2)}) collective-permute-start(f32[16,128,128]{2,1,0:T(8,128)} %c0_ref.1), channel_id=1, source_target_pairs={{0,2},{2,0},{1,3},{3,1},{4,6},{6,4},{5,7},{7,5},{8,10},{10,8},{9,1... | collective-permute-start | bytes 3145736 | tf_op jit(solution)/shard_map/ppermute | solution.py:226
  2.0 1.9 %copy-start = (f32[16,128,3,128]{3,1,2,0:T(8,128)S(1)}, f32[16,128,3,128]{3,1,2,0:T(8,128)}, u32[]{:S(2)}) copy-start(f32[16,128,3,128]{3,1,2,0:T(8,128)} %param.8) | copy-start | bytes 9437188
  3.9 0.9 copy-start.2
  9.2 6.2 %copy-start.1 = (f32[16,128,128]{2,1,0:T(8,128)S(1)}, f32[16,128,128]{2,1,0:T(8,128)}, u32[]{:S(2)}) copy-start(f32[16,128,128]{2,1,0:T(8,128)} %c0_ref.1) | copy-start | bytes 3145732
  9.2 30.7 %copy-start.3 = (s32[1024,4]{0,1:T(4,128)S(1)}, s32[1024,4]{0,1:T(4,128)}, u32[]{:S(2)}) copy-start(s32[1024,4]{0,1:T(4,128)} %param.6) | copy-start | bytes 49156
  9.2 30.7 %copy-start.4 = (s32[64]{0:T(128)S(1)}, s32[64]{0:T(128)}, u32[]{:S(2)}) copy-start(s32[64]{0:T(128)} %counts_ref.1) | copy-start | bytes 772
  9.2 4.5 %collective-permute-start = (f32[8,128,128]{2,1,0:T(8,128)S(1)}, f32[8,128,128]{2,1,0:T(8,128)S(1)}, u32[]{:S(2)}, u32[]{:S(2)}) collective-permute-start(f32[8,128,128]{2,1,0:T(8,128)S(1)} %coupling.3), channel_id=1, source_target_pairs={{0,1},{1,0},{2,3},{3,2},{4,5},{5,4},{6,7},{7,6},{8,9},{9,8},{10,11... | collective-permute-start | bytes 1572872 | tf_op jit(solution)/shard_map/ppermute | solution.py:226
  13.8 24.0 %collective-permute-start.1 = (f32[8,128,128]{2,1,0:T(8,128)S(1)}, f32[8,128,128]{2,1,0:T(8,128)S(1)}, u32[]{:S(2)}, u32[]{:S(2)}) collective-permute-start(f32[8,128,128]{2,1,0:T(8,128)S(1)} %add.15), channel_id=1, source_target_pairs={{0,2},{2,0},{1,3},{3,1},{4,6},{6,4},{5,7},{7,5},{8,10},{10,8},{9,1... | collective-permute-start | bytes 1572872 | tf_op jit(solution)/shard_map/ppermute | solution.py:226
  15.4 22.6 %collective-permute-start.3 = (f32[16,128,128]{2,1,0:T(8,128)S(1)}, f32[16,128,128]{2,1,0:T(8,128)S(1)}, u32[]{:S(2)}, u32[]{:S(2)}) collective-permute-start(f32[16,128,128]{2,1,0:T(8,128)S(1)} %copy-done.1), channel_id=1, source_target_pairs={{0,1},{1,0},{2,3},{3,2},{4,5},{5,4},{6,7},{7,6},{8,9},{9,8},{10,11... | collective-permute-start | bytes 3145736 | tf_op jit(solution)/shard_map/ppermute | solution.py:226
  27.7 12.2 %collective-permute-start.5 = (f32[16,128,128]{2,1,0:T(8,128)S(1)}, f32[16,128,128]{2,1,0:T(8,128)S(1)}, u32[]{:S(2)}, u32[]{:S(2)}) collective-permute-start(f32[16,128,128]{2,1,0:T(8,128)S(1)} %collective-permute-done.4.c2_ref), channel_id=1, source_target_pairs={{0,1},{1,0},{2,3},{3,2},{4,5},{5,4},{6,7},{7,6},{8,9},{9,8},{10,11... | collective-permute-start | bytes 3145736 | tf_op jit(solution)/shard_map/ppermute | solution.py:226
  37.9 2.0 %collective-permute-start.2 = (f32[8,128,128]{2,1,0:T(8,128)S(1)}, f32[8,128,128]{2,1,0:T(8,128)S(1)}, u32[]{:S(2)}, u32[]{:S(2)}) collective-permute-start(f32[8,128,128]{2,1,0:T(8,128)S(1)} %add.16.own_ref), channel_id=1, source_target_pairs={{0,1},{1,0},{2,3},{3,2},{4,5},{5,4},{6,7},{7,6},{8,9},{9,8},{10,11... | collective-permute-start | bytes 1572872 | tf_op jit(solution)/shard_map/ppermute | solution.py:226
  42.7 17.6 %collective-permute-start.10 = (f32[2,2,2,4,4,8,128]{6,5,4,3,2,1,0:T(8,128)S(1)}, f32[2,2,2,4,4,8,128]{6,5,4,3,2,1,0:T(8,128)S(1)}, u32[]{:S(2)}, u32[]{:S(2)}) collective-permute-start(f32[2,2,2,4,4,8,128]{6,5,4,3,2,1,0:T(8,128)S(1)} %get-tuple-element.32), channel_id=1, source_target_pairs={{0,8},{8,0},{1,9},{9,1},{2,10},{10,2},{3,11},{11,3},{4,12},{12,4},... | collective-permute-start | bytes 1572872 | tf_op jit(solution)/shard_map/ppermute | solution.py:226
  44.7 16.8 %collective-permute-start.13 = (f32[2,2,2,4,4,8,128]{6,5,4,3,2,1,0:T(8,128)S(1)}, f32[2,2,2,4,4,8,128]{6,5,4,3,2,1,0:T(8,128)S(1)}, u32[]{:S(2)}, u32[]{:S(2)}) collective-permute-start(f32[2,2,2,4,4,8,128]{6,5,4,3,2,1,0:T(8,128)S(1)} %get-tuple-element.38), channel_id=1, source_target_pairs={{0,4},{4,0},{1,5},{5,1},{2,6},{6,2},{3,7},{7,3},{8,12},{12,8},{9,1... | collective-permute-start | bytes 1572872 | tf_op jit(solution)/shard_map/ppermute | solution.py:226
  49.1 9.2 %collective-permute-start.6 = (f32[2,2,4,5,8,128]{5,4,3,2,1,0:T(8,128)S(1)}, f32[2,2,4,5,8,128]{5,4,3,2,1,0:T(8,128)S(1)}, u32[]{:S(2)}, u32[]{:S(2)}) collective-permute-start(f32[2,2,4,5,8,128]{5,4,3,2,1,0:T(8,128)S(1)} %get-tuple-element.25), channel_id=1, source_target_pairs={{0,64},{64,0},{1,65},{65,1},{2,66},{66,2},{3,67},{67,3},{4,68},{68... | collective-permute-start | bytes 983048 | tf_op jit(solution)/shard_map/ppermute | solution.py:226
  49.1 10.4 %collective-permute-start.7 = (f32[2,2,4,5,8,128]{5,4,3,2,1,0:T(8,128)S(1)}, f32[2,2,4,5,8,128]{5,4,3,2,1,0:T(8,128)S(1)}, u32[]{:S(2)}, u32[]{:S(2)}) collective-permute-start(f32[2,2,4,5,8,128]{5,4,3,2,1,0:T(8,128)S(1)} %get-tuple-element.26), channel_id=1, source_target_pairs={{0,192},{64,128},{128,64},{192,0},{1,193},{65,129},{129,65},{193,1... | collective-permute-start | bytes 983048 | tf_op jit(solution)/shard_map/ppermute | solution.py:222
  59.6 8.6 %collective-permute-start.8 = (f32[2,2,4,5,8,128]{5,4,3,2,1,0:T(8,128)S(1)}, f32[2,2,4,5,8,128]{5,4,3,2,1,0:T(8,128)S(1)}, u32[]{:S(2)}, u32[]{:S(2)}) collective-permute-start(f32[2,2,4,5,8,128]{5,4,3,2,1,0:T(8,128)S(1)} %get-tuple-element.28), channel_id=1, source_target_pairs={{0,8},{8,0},{1,9},{9,1},{2,10},{10,2},{3,11},{11,3},{4,12},{12,4},... | collective-permute-start | bytes 983048 | tf_op jit(solution)/shard_map/ppermute | solution.py:226
  60.4 9.1 %collective-permute-start.11 = (f32[2,2,4,4,8,128]{5,4,3,2,1,0:T(8,128)S(1)}, f32[2,2,4,4,8,128]{5,4,3,2,1,0:T(8,128)S(1)}, u32[]{:S(2)}, u32[]{:S(2)}) collective-permute-start(f32[2,2,4,4,8,128]{5,4,3,2,1,0:T(8,128)S(1)} %get-tuple-element.34), channel_id=1, source_target_pairs={{0,4},{4,0},{1,5},{5,1},{2,6},{6,2},{3,7},{7,3},{8,12},{12,8},{9,1... | collective-permute-start | bytes 786440 | tf_op jit(solution)/shard_map/ppermute | solution.py:226
  61.7 8.5 %collective-permute-start.14 = (f32[2,2,4,4,8,128]{5,4,3,2,1,0:T(8,128)S(1)}, f32[2,2,4,4,8,128]{5,4,3,2,1,0:T(8,128)S(1)}, u32[]{:S(2)}, u32[]{:S(2)}) collective-permute-start(f32[2,2,4,4,8,128]{5,4,3,2,1,0:T(8,128)S(1)} %get-tuple-element.40), channel_id=1, source_target_pairs={{0,64},{64,0},{1,65},{65,1},{2,66},{66,2},{3,67},{67,3},{4,68},{68... | collective-permute-start | bytes 786440 | tf_op jit(solution)/shard_map/ppermute | solution.py:226
  68.3 5.4 %collective-permute-start.9 = (f32[2,4,5,8,128]{4,3,2,1,0:T(8,128)S(1)}, f32[2,4,5,8,128]{4,3,2,1,0:T(8,128)S(1)}, u32[]{:S(2)}, u32[]{:S(2)}) collective-permute-start(f32[2,4,5,8,128]{4,3,2,1,0:T(8,128)S(1)} %get-tuple-element.30), channel_id=1, source_target_pairs={{0,4},{4,0},{1,5},{5,1},{2,6},{6,2},{3,7},{7,3},{8,12},{12,8},{9,1... | collective-permute-start | bytes 491528 | tf_op jit(solution)/shard_map/ppermute | solution.py:226
  69.5 5.1 %collective-permute-start.12 = (f32[2,4,4,8,128]{4,3,2,1,0:T(8,128)S(1)}, f32[2,4,4,8,128]{4,3,2,1,0:T(8,128)S(1)}, u32[]{:S(2)}, u32[]{:S(2)}) collective-permute-start(f32[2,4,4,8,128]{4,3,2,1,0:T(8,128)S(1)} %get-tuple-element.36), channel_id=1, source_target_pairs={{0,64},{64,0},{1,65},{65,1},{2,66},{66,2},{3,67},{67,3},{4,68},{68... | collective-permute-start | bytes 393224 | tf_op jit(solution)/shard_map/ppermute | solution.py:226
  70.2 5.1 %collective-permute-start.15 = (f32[2,4,4,8,128]{4,3,2,1,0:T(8,128)S(1)}, f32[2,4,4,8,128]{4,3,2,1,0:T(8,128)S(1)}, u32[]{:S(2)}, u32[]{:S(2)}) collective-permute-start(f32[2,4,4,8,128]{4,3,2,1,0:T(8,128)S(1)} %get-tuple-element.42), channel_id=1, source_target_pairs={{0,8},{8,0},{1,9},{9,1},{2,10},{10,2},{3,11},{11,3},{4,12},{12,4},... | collective-permute-start | bytes 393224 | tf_op jit(solution)/shard_map/ppermute | solution.py:226

commit v5 on v4

--- a/solution.py
+++ b/solution.py
@@ -1,3 +1,5 @@
+import itertools
+
 import jax
 import jax.numpy as jnp
 from jax import lax
@@ -11,8 +13,15 @@
 HALF = SLOTS // 2
 CHUNK = 4
 GT = 4
-NXH, NXL, NZH, NZL, NYL = 2, 2, 4, 2, 2
-GROUPS = (("xl", "zl", "yl", GT + 1), ("zl", "yl", "xl", GT), ("yl", "xl", "zl", GT))
+NXH, NXL, NZA, NZB, NZL, NYL = 2, 2, 2, 2, 2, 2
+TILES = (GT + 1, GT, GT)
+AXES = (
+    ("xl", "zl", "yl", "xh", "zb", "za"),
+    ("zl", "yl", "xl", "zb", "za", "xh"),
+    ("yl", "xl", "zl", "za", "xh", "zb"),
+)
+PHASES = 6
+ROWS = ("xh", "xl", "za", "zb", "zl", "yl")
 F32 = jnp.float32
 BF16 = jnp.bfloat16
 ANY = pl.BlockSpec(memory_space=pl.ANY)
@@ -31,8 +40,10 @@
 
 
 def cluster_device():
-    xh, xl, zh, zl, yl = (lax.axis_index(name) for name in ("xh", "xl", "zh", "zl", "yl"))
-    return (((xh * NXL + xl) * NZH + zh) * NZL + zl) * NYL + yl
+    index = 0
+    for name in ROWS:
+        index = index * 2 + lax.axis_index(name)
+    return index
 
 
 def coupling_kernel(mine, pts_hbm, inv_ref, out_ref, pts_buf, sems):
@@ -112,14 +123,12 @@
                 rows = jnp.dot(left, right, preferred_element_type=F32)
                 row_tile = tiles_ref[cam, device * SLOTS + slot]
                 for rel in range(4):
-                    block = rows[:, rel * W : (rel + 1) * W].reshape(NZH, NZL, NYL, 8, W)
+                    block = rows[:, rel * W : (rel + 1) * W].reshape(NZA, NZB, NZL, NYL, 8, W)
 
                     def add(group, tile, block=block):
-                        for zl in range(NZL):
-                            for yl in range(NYL):
-                                at = {"xl": lax.rem(row_tile, NXL), "zl": zl, "yl": yl}
-                                lead = tuple(at[name] for name in GROUPS[group][:3])
-                                accs[group][lead + (row_tile // NXL, slice(None), tile)] += block[:, zl, yl]
+                        for za, zb, zl, yl in itertools.product(range(2), repeat=4):
+                            at = {"xl": lax.rem(row_tile, NXL), "xh": row_tile // NXL, "za": za, "zb": zb, "zl": zl, "yl": yl}
+                            accs[group][tuple(at[name] for name in AXES[group]) + (tile,)] += block[za, zb, zl, yl]
 
                     if rel == 0:
                         add(0, GT)
@@ -128,7 +137,7 @@
                     add(rel - 1, tile)
 
     copies = []
-    for group, names in enumerate(GROUPS):
+    for group, names in enumerate(AXES):
         bit = lax.axis_index(names[0])
         away = accs[group].at[1 - bit]
         copies += [away.at[0], away.at[1]] if group == 0 else [away]
@@ -144,7 +153,8 @@
     return pl.pallas_call(
         schur_kernel,
         out_shape=[
-            jax.ShapeDtypeStruct(lead + (2, NXH, NZH, names[3], 8, W), F32) for k, names in enumerate(GROUPS)
+            jax.ShapeDtypeStruct(lead + (2,) * (PHASES - 2) + (count, 8, W), F32)
+            for k, count in enumerate(TILES)
             for lead in (((), (), (2,)) if k == 0 else ((2,), (2,)))
         ],
         in_specs=[SMEM, SMEM] + [VMEM] * 6,
@@ -152,40 +162,35 @@
         scratch_shapes=[
             pltpu.SemaphoreType.DMA((7,)),
         ]
-        + [pltpu.VMEM((2, 2, 2, NXH, NZH, names[3], 8, W), F32) for names in GROUPS],
+        + [pltpu.VMEM((2,) * PHASES + (count, 8, W), F32) for count in TILES],
         cost_estimate=pl.CostEstimate(flops=SLOTS * 6 * 5 * W * W * W, bytes_accessed=SLOTS * 5 * W * W * 4, transcendentals=0),
         compiler_params=pltpu.CompilerParams(vmem_limit_bytes=12 << 20),
         name="schur",
     )(counts, tiles, *[pltpu.with_memory_space_constraint(v, pltpu.VMEM) for v in (own, oth, *panels)])
 
 
-def place_kernel(in_ref, out_ref):
+def place_kernel(*refs):
+    out_ref = refs[-1]
     cam = camera_index()
     x = lax.axis_index("xh") * NXL + lax.axis_index("xl")
     out_ref[...] = jnp.zeros_like(out_ref)
-
-    def total(tile):
-        value = in_ref[0, tile]
-        for source in range(1, NXH * NZH):
-            value = value + in_ref[source, tile]
-        return value
-
-    row = 0
-    for rel, t in [(1, t) for t in range(GT)] + [(0, x)] + [(rel, t) for rel in (2, 3) for t in range(GT)]:
-        column = lax.bitwise_xor(cam, rel) * GT + t
-        out_ref[0, :, pl.ds(pl.multiple_of(column * W, W), W)] = total(row)
-        row += 1
+    for rel in range(4):
+        for t in [x] if rel == 0 else range(GT):
+            group, tile = (0, GT) if rel == 0 else (rel - 1, t)
+            column = lax.bitwise_xor(cam, rel) * GT + t
+            value = refs[group * 2][tile] + refs[group * 2 + 1][tile]
+            out_ref[0, :, pl.ds(pl.multiple_of(column * W, W), W)] = value
 
 
 def place(pieces):
     return pl.pallas_call(
         place_kernel,
         out_shape=jax.ShapeDtypeStruct((1, 8, 4 * GT * W), F32),
-        in_specs=[VMEM],
+        in_specs=[VMEM] * len(pieces),
         out_specs=VMEM,
         compiler_params=pltpu.CompilerParams(vmem_limit_bytes=4 << 20),
         name="place",
-    )(pieces)
+    )(*[pltpu.with_memory_space_constraint(v, pltpu.VMEM) for v in pieces])
 
 
 def halve_kernel(axis, keep_ref, *refs):
@@ -248,24 +253,19 @@
     low_x = swap(outs[0], "xl")
     high_x = swap_x_other(outs[1])
     groups = [(outs[2], (low_x, high_x)), (outs[4], (near_z,)), (outs[6], (near_y,))]
-    for phase in (1, 2):
+    for phase in range(1, PHASES):
         halves = []
         for k, (keep, parts) in enumerate(groups):
-            halves.append(halve(GROUPS[k][phase], keep, parts))
+            halves.append(halve(AXES[k][phase], keep, parts))
         groups = []
         for k, (send, keep) in enumerate(halves):
-            groups.append((keep, (swap(send, GROUPS[k][phase]),)))
-    groups = [(keep, parts[0]) for keep, parts in groups]
-    received = [got for _, got in groups]
-    part = jnp.concatenate(
-        [(keep + got).reshape(NXH * NZH, -1, 8, W) for (keep, _), got in zip(groups, received)], axis=1
-    )
-    return place(lax.all_to_all(part, ("xh", "zh"), 0, 0, tiled=True))
+            groups.append((keep, (swap(send, AXES[k][phase]),)))
+    return place([piece for keep, parts in groups for piece in (keep, *parts)])
 
 
 def solution(mesh):
-    fine = Mesh(mesh.devices.reshape(NXH, NXL, NZH, NZL, NYL, 2, 2), ("xh", "xl", "zh", "zl", "yl", "yh", "c"))
-    rows = ("xh", "xl", "zh", "zl", "yl")
+    fine = Mesh(mesh.devices.reshape((2,) * 8), ROWS + ("yh", "c"))
+    rows = ROWS
     cams = ("yh", "c")
     in_specs = (
         P(),

time: 99.5 us -> 102 us (1.025)
  starting transfers between devices: 18.2 us -> 42.7 us
  blocking collectives: 23.1 us -> 0 us
  waiting for transfers between devices: 42 us -> 43.3 us
    ppermute x15 -> x24, starting transfers between devices: 15.5 us -> 39.9 us  [swap(): return lax.ppermute(value, axis, [(0, 1), (1, 0)])]
    all_to_all x1 -> x0, blocking collectives: 23.1 us -> none  [on_device(): return place(lax.all_to_all(part, ('xh', 'zh'), 0, 0, tiled=True))]
    ppermute x15 -> x24, waiting for transfers between devices: 40.8 us -> 42.1 us  [swap(): return lax.ppermute(value, axis, [(0, 1), (1, 0)])]
  transfers between devices with their start and end apart: 16 -> 25, of which waited for: 9 -> 9; matrix products, arithmetic and copies ran while one was open for 0% -> 0% of each run, Pallas kernels for 9% -> 9%
where the time goes in v5:
time: 102 us
  waiting for transfers between devices  43.3 us (42%)
  starting transfers between devices  42.7 us (42%)
  Pallas kernels  12.8 us (13%)
  local copies, waits for them, and re-layouts  2.79 us (3%)
    ppermute x24, waiting for transfers between devices, swap(): return lax.ppermute(value, axis, [(0, 1), (1, 0)])  42.1 us
    ppermute x24, starting transfers between devices, swap(): return lax.ppermute(value, axis, [(0, 1), (1, 0)])  39.9 us
    pallas_call x2, Pallas kernels, coupling(): pl.pallas_call(kernel, out_shape=jax.ShapeDtypeStruct((HALF, W, W), F32),...  8.77 us
    pallas_call x1, Pallas kernels, schur(): pl.pallas_call(schur_kernel, out_shape=[jax.ShapeDtypeStruct(lead + (2,)...  2.8 us
    unnamed x10, local copies, waits for them, and re-layouts  2.79 us
    ppermute x1, starting transfers between devices, swap_x_other(): lax.ppermute(value, ('xh', 'xl'), [(i, (i + 1 if i % 2 else i - 1) % size...  2.77 us
  transfers between devices with their start and end apart: 25, of which 9 were waited for; matrix products, arithmetic and copies ran while one was open for 0% of the time, Pallas kernels for 9%

profile of v5, /device:TPU:16, one launch (start us, length us, event | category | flops | bytes accessed | tf_op | source)
XLA Modules:
  0.0 101.9 jit_solution(10945154915339252539)
XLA Ops:
  0.0 2.0 %collective-permute-start.4 = (f32[16,128,128]{2,1,0:T(8,128)}, f32[16,128,128]{2,1,0:T(8,128)S(1)}, u32[]{:S(2)}, u32[]{:S(2)}) collective-permute-start(f32[16,128,128]{2,1,0:T(8,128)} %c0_ref.1), channel_id=1, source_target_pairs={{0,2},{2,0},{1,3},{3,1},{4,6},{6,4},{5,7},{7,5},{8,10},{10,8},{9,1... | collective-permute-start | bytes 3145736 | tf_op jit(solution)/shard_map/ppermute | solution.py:231
  2.0 1.9 %copy-done = f32[16,128,3,128]{3,1,2,0:T(8,128)S(1)} copy-done((f32[16,128,3,128]{3,1,2,0:T(8,128)S(1)}, f32[16,128,3,128]{3,1,2,0:T(8,128)}, u32[]{:S(2)}) %copy-start) | copy-done | bytes 3145752
  3.9 0.9 copy-done.2
  4.8 4.4 %coupling.3 = f32[8,128,128]{2,1,0:T(8,128)S(1)} custom-call(f32[16,3,128,128]{3,2,1,0:T(8,128)S(1)} %bitcast.3, f32[3,3,16,128]{3,2,1,0:T(8,128)S(1)} %bitcast.5), custom_call_target="tpu_custom_call" | custom-call | flops 301989888 | bytes 2097152 | tf_op jit(solution)/shard_map/coupling/pallas_call | solution.py:77
  9.2 0.0 copy-start.1
  9.2 0.0 copy-start.3
  9.2 0.0 copy-start.4
  9.2 0.1 collective-permute-start
  9.3 4.4 %coupling.2 = f32[8,128,128]{2,1,0:T(8,128)S(1)} custom-call(f32[16,3,128,128]{3,2,1,0:T(8,128)S(1)} %bitcast.4, f32[3,3,16,128]{3,2,1,0:T(8,128)S(1)} %bitcast.6), custom_call_target="tpu_custom_call" | custom-call | flops 301989888 | bytes 2097152 | tf_op jit(solution)/shard_map/coupling/pallas_call | solution.py:77
  13.8 0.1 add.6
  13.8 1.6 %collective-permute-start.1 = (f32[8,128,128]{2,1,0:T(8,128)S(1)}, f32[8,128,128]{2,1,0:T(8,128)S(1)}, u32[]{:S(2)}, u32[]{:S(2)}) collective-permute-start(f32[8,128,128]{2,1,0:T(8,128)S(1)} %add.6), channel_id=1, source_target_pairs={{0,2},{2,0},{1,3},{3,1},{4,6},{6,4},{5,7},{7,5},{8,10},{10,8},{9,1... | collective-permute-start | bytes 1572872 | tf_op jit(solution)/shard_map/ppermute | solution.py:231
  15.4 0.2 collective-permute-start.3
  15.6 12.2 %collective-permute-done.4.c2_ref = f32[16,128,128]{2,1,0:T(8,128)S(1)} collective-permute-done((f32[16,128,128]{2,1,0:T(8,128)}, f32[16,128,128]{2,1,0:T(8,128)S(1)}, u32[]{:S(2)}, u32[]{:S(2)}) %collective-permute-start.4) | collective-permute-done | bytes 1048608 | tf_op jit(solution)/shard_map/ppermute | solution.py:231
  27.7 0.0 collective-permute-start.5
  27.7 10.1 %collective-permute-done.1 = f32[8,128,128]{2,1,0:T(8,128)S(1)} collective-permute-done((f32[8,128,128]{2,1,0:T(8,128)S(1)}, f32[8,128,128]{2,1,0:T(8,128)S(1)}, u32[]{:S(2)}, u32[]{:S(2)}) %collective-permute-start.1) | collective-permute-done | bytes 524320 | tf_op jit(solution)/shard_map/ppermute | solution.py:231
  37.9 0.1 add.7.own_ref
  37.9 0.1 collective-permute-start.2
  38.0 0.0 collective-permute-done.3.c1_ref
  38.0 1.9 %collective-permute-done.2.oth_ref = f32[8,128,128]{2,1,0:T(8,128)S(1)} collective-permute-done((f32[8,128,128]{2,1,0:T(8,128)S(1)}, f32[8,128,128]{2,1,0:T(8,128)S(1)}, u32[]{:S(2)}, u32[]{:S(2)}) %collective-permute-start.2) | collective-permute-done | bytes 524320 | tf_op jit(solution)/shard_map/ppermute | solution.py:231
  39.9 2.8 %schur.1 = (f32[2,2,2,2,5,8,128]{6,5,4,3,2,1,0:T(8,128)S(1)}, f32[2,2,2,2,5,8,128]{6,5,4,3,2,1,0:T(8,128)S(1)}, f32[2,2,2,2,2,5,8,128]{7,6,5,4,3,2,1,0:T(8,128)S...) custom-call(s32[64]{0:T(128)S(1)} %copy-done.4, ...), custom_call_target="tpu_custom_call" | custom-call | flops 1006632960 | bytes 5242880 | tf_op jit(solution)/shard_map/schur/pallas_call | solution.py:153
  42.7 2.0 %collective-permute-start.13 = (f32[2,2,2,2,2,4,8,128]{7,6,5,4,3,2,1,0:T(8,128)S(1)}, f32[2,2,2,2,2,4,8,128]{7,6,5,4,3,2,1,0:T(8,128)S(1)}, u32[]{:S(2)}, u32[]{:S(2)}) collective-permute-start(f32[2,2,2,2,2,4,8,128]{7,6,5,4,3,2,1,0:T(8,128)S(1)} %get-tuple-element.56), channel_id=1, source_target_pairs={{0,8},{8,0},{1,9},{9,1},{2,10},{10,2},{3,11},{11,3},{4,12},{12,4},... | collective-permute-start | bytes 1572872 | tf_op jit(solution)/shard_map/ppermute | solution.py:231
  44.7 4.4 %collective-permute-start.19 = (f32[2,2,2,2,2,4,8,128]{7,6,5,4,3,2,1,0:T(8,128)S(1)}, f32[2,2,2,2,2,4,8,128]{7,6,5,4,3,2,1,0:T(8,128)S(1)}, u32[]{:S(2)}, u32[]{:S(2)}) collective-permute-start(f32[2,2,2,2,2,4,8,128]{7,6,5,4,3,2,1,0:T(8,128)S(1)} %get-tuple-element.68), channel_id=1, source_target_pairs={{0,4},{4,0},{1,5},{5,1},{2,6},{6,2},{3,7},{7,3},{8,12},{12,8},{9,1... | collective-permute-start | bytes 1572872 | tf_op jit(solution)/shard_map/ppermute | solution.py:231
  49.1 2.8 %collective-permute-start.7 = (f32[2,2,2,2,5,8,128]{6,5,4,3,2,1,0:T(8,128)S(1)}, f32[2,2,2,2,5,8,128]{6,5,4,3,2,1,0:T(8,128)S(1)}, u32[]{:S(2)}, u32[]{:S(2)}) collective-permute-start(f32[2,2,2,2,5,8,128]{6,5,4,3,2,1,0:T(8,128)S(1)} %get-tuple-element.44), channel_id=1, source_target_pairs={{0,192},{64,128},{128,64},{192,0},{1,193},{65,129},{129,65},{193,1... | collective-permute-start | bytes 983048 | tf_op jit(solution)/shard_map/ppermute | solution.py:227
  51.9 6.4 %collective-permute-done.6.refs_1_ = f32[2,2,2,2,5,8,128]{6,5,4,3,2,1,0:T(8,128)S(1)} collective-permute-done((f32[2,2,2,2,5,8,128]{6,5,4,3,2,1,0:T(8,128)S(1)}, f32[2,2,2,2,5,8,128]{6,5,4,3,2,1,0:T(8,128)S(1)}, u32[]{:S(2)}, u32[]{:S(2)}) %collective-permute-start.6) | collective-permute-done | bytes 327712 | tf_op jit(solution)/shard_map/ppermute | solution.py:231
  58.3 1.2 %collective-permute-done.7.refs_2_ = f32[2,2,2,2,5,8,128]{6,5,4,3,2,1,0:T(8,128)S(1)} collective-permute-done((f32[2,2,2,2,5,8,128]{6,5,4,3,2,1,0:T(8,128)S(1)}, f32[2,2,2,2,5,8,128]{6,5,4,3,2,1,0:T(8,128)S(1)}, u32[]{:S(2)}, u32[]{:S(2)}) %collective-permute-start.7) | collective-permute-done | bytes 327712 | tf_op jit(solution)/shard_map/ppermute | solution.py:227
  59.5 0.1 halve.15
  59.6 0.6 collective-permute-start.8
  60.3 0.1 halve.20
  60.4 1.2 %collective-permute-start.14 = (f32[2,2,2,2,4,8,128]{6,5,4,3,2,1,0:T(8,128)S(1)}, f32[2,2,2,2,4,8,128]{6,5,4,3,2,1,0:T(8,128)S(1)}, u32[]{:S(2)}, u32[]{:S(2)}) collective-permute-start(f32[2,2,2,2,4,8,128]{6,5,4,3,2,1,0:T(8,128)S(1)} %get-tuple-element.58), channel_id=1, source_target_pairs={{0,4},{4,0},{1,5},{5,1},{2,6},{6,2},{3,7},{7,3},{8,12},{12,8},{9,1... | collective-permute-start | bytes 786440 | tf_op jit(solution)/shard_map/ppermute | solution.py:231
  61.6 0.1 halve.25
  61.7 0.7 collective-permute-start.20
  62.3 5.9 %collective-permute-done.8.refs_1_ = f32[2,2,2,2,5,8,128]{6,5,4,3,2,1,0:T(8,128)S(1)} collective-permute-done((f32[2,2,2,2,5,8,128]{6,5,4,3,2,1,0:T(8,128)S(1)}, f32[2,2,2,2,5,8,128]{6,5,4,3,2,1,0:T(8,128)S(1)}, u32[]{:S(2)}, u32[]{:S(2)}) %collective-permute-start.8) | collective-permute-done | bytes 327712 | tf_op jit(solution)/shard_map/ppermute | solution.py:231
  68.3 1.2 %collective-permute-start.9 = (f32[2,2,2,5,8,128]{5,4,3,2,1,0:T(8,128)S(1)}, f32[2,2,2,5,8,128]{5,4,3,2,1,0:T(8,128)S(1)}, u32[]{:S(2)}, u32[]{:S(2)}) collective-permute-start(f32[2,2,2,5,8,128]{5,4,3,2,1,0:T(8,128)S(1)} %get-tuple-element.48), channel_id=1, source_target_pairs={{0,4},{4,0},{1,5},{5,1},{2,6},{6,2},{3,7},{7,3},{8,12},{12,8},{9,1... | collective-permute-start | bytes 491528 | tf_op jit(solution)/shard_map/ppermute | solution.py:231
  69.5 0.6 collective-permute-start.15
  70.2 0.7 collective-permute-start.21
  71.0 2.7 %collective-permute-done.9.refs_1_ = f32[2,2,2,5,8,128]{5,4,3,2,1,0:T(8,128)S(1)} collective-permute-done((f32[2,2,2,5,8,128]{5,4,3,2,1,0:T(8,128)S(1)}, f32[2,2,2,5,8,128]{5,4,3,2,1,0:T(8,128)S(1)}, u32[]{:S(2)}, u32[]{:S(2)}) %collective-permute-start.9) | collective-permute-done | bytes 163872 | tf_op jit(solution)/shard_map/ppermute | solution.py:231
  73.7 2.6 %collective-permute-start.10 = (f32[2,2,5,8,128]{4,3,2,1,0:T(8,128)S(1)}, f32[2,2,5,8,128]{4,3,2,1,0:T(8,128)S(1)}, u32[]{:S(2)}, u32[]{:S(2)}) collective-permute-start(f32[2,2,5,8,128]{4,3,2,1,0:T(8,128)S(1)} %get-tuple-element.50), channel_id=1, source_target_pairs={{0,128},{128,0},{1,129},{129,1},{2,130},{130,2},{3,131},{131,3},{4... | collective-permute-start | bytes 245768 | tf_op jit(solution)/shard_map/ppermute | solution.py:231
  76.3 3.4 %collective-permute-start.16 = (f32[2,2,4,8,128]{4,3,2,1,0:T(8,128)S(1)}, f32[2,2,4,8,128]{4,3,2,1,0:T(8,128)S(1)}, u32[]{:S(2)}, u32[]{:S(2)}) collective-permute-start(f32[2,2,4,8,128]{4,3,2,1,0:T(8,128)S(1)} %get-tuple-element.62), channel_id=1, source_target_pairs={{0,16},{16,0},{1,17},{17,1},{2,18},{18,2},{3,19},{19,3},{4,20},{20... | collective-permute-start | bytes 196616 | tf_op jit(solution)/shard_map/ppermute | solution.py:231
  79.8 4.7 %collective-permute-start.22 = (f32[2,2,4,8,128]{4,3,2,1,0:T(8,128)S(1)}, f32[2,2,4,8,128]{4,3,2,1,0:T(8,128)S(1)}, u32[]{:S(2)}, u32[]{:S(2)}) collective-permute-start(f32[2,2,4,8,128]{4,3,2,1,0:T(8,128)S(1)} %get-tuple-element.74), channel_id=1, source_target_pairs={{0,32},{32,0},{1,33},{33,1},{2,34},{34,2},{3,35},{35,3},{4,36},{36... | collective-permute-start | bytes 196616 | tf_op jit(solution)/shard_map/ppermute | solution.py:231
  84.5 0.8 collective-permute-start.11
  85.3 5.1 %collective-permute-start.17 = (f32[2,4,8,128]{3,2,1,0:T(8,128)S(1)}, f32[2,4,8,128]{3,2,1,0:T(8,128)S(1)}, u32[]{:S(2)}, u32[]{:S(2)}) collective-permute-start(f32[2,4,8,128]{3,2,1,0:T(8,128)S(1)} %get-tuple-element.64), channel_id=1, source_target_pairs={{0,32},{32,0},{1,33},{33,1},{2,34},{34,2},{3,35},{35,3},{4,36},{36... | collective-permute-start | bytes 98312 | tf_op jit(solution)/shard_map/ppermute | solution.py:231
  90.4 2.6 %collective-permute-start.23 = (f32[2,4,8,128]{3,2,1,0:T(8,128)S(1)}, f32[2,4,8,128]{3,2,1,0:T(8,128)S(1)}, u32[]{:S(2)}, u32[]{:S(2)}) collective-permute-start(f32[2,4,8,128]{3,2,1,0:T(8,128)S(1)} %get-tuple-element.76), channel_id=1, source_target_pairs={{0,128},{128,0},{1,129},{129,1},{2,130},{130,2},{3,131},{131,3},{4... | collective-permute-start | bytes 98312 | tf_op jit(solution)/shard_map/ppermute | solution.py:231
  93.1 2.4 %collective-permute-start.12 = (f32[5,8,128]{2,1,0:T(8,128)S(1)}, f32[5,8,128]{2,1,0:T(8,128)S(1)}, u32[]{:S(2)}, u32[]{:S(2)}) collective-permute-start(f32[5,8,128]{2,1,0:T(8,128)S(1)} %get-tuple-element.54), channel_id=1, source_target_pairs={{0,32},{32,0},{1,33},{33,1},{2,34},{34,2},{3,35},{35,3},{4,36},{36... | collective-permute-start | bytes 61448 | tf_op jit(solution)/shard_map/ppermute | solution.py:231
  95.5 1.0 collective-permute-start.18
  96.5 1.9 %collective-permute-start.24 = (f32[4,8,128]{2,1,0:T(8,128)S(1)}, f32[4,8,128]{2,1,0:T(8,128)S(1)}, u32[]{:S(2)}, u32[]{:S(2)}) collective-permute-start(f32[4,8,128]{2,1,0:T(8,128)S(1)} %get-tuple-element.78), channel_id=1, source_target_pairs={{0,16},{16,0},{1,17},{17,1},{2,18},{18,2},{3,19},{19,3},{4,20},{20... | collective-permute-start | bytes 49160 | tf_op jit(solution)/shard_map/ppermute | solution.py:231
  98.4 2.4 %collective-permute-done.12.refs_1_ = f32[5,8,128]{2,1,0:T(8,128)S(1)} collective-permute-done((f32[5,8,128]{2,1,0:T(8,128)S(1)}, f32[5,8,128]{2,1,0:T(8,128)S(1)}, u32[]{:S(2)}, u32[]{:S(2)}) %collective-permute-start.12) | collective-permute-done | bytes 20512 | tf_op jit(solution)/shard_map/ppermute | solution.py:231
  100.8 0.4 collective-permute-done.24.refs_5_
  101.2 0.7 place.1
  (33 shorter events, 0.4 us)
Async XLA Ops:
  0.0 27.7 %collective-permute-start.4 = (f32[16,128,128]{2,1,0:T(8,128)}, f32[16,128,128]{2,1,0:T(8,128)S(1)}, u32[]{:S(2)}, u32[]{:S(2)}) collective-permute-start(f32[16,128,128]{2,1,0:T(8,128)} %c0_ref.1), channel_id=1, source_target_pairs={{0,2},{2,0},{1,3},{3,1},{4,6},{6,4},{5,7},{7,5},{8,10},{10,8},{9,1... | collective-permute-start | bytes 3145736 | tf_op jit(solution)/shard_map/ppermute | solution.py:231
  2.0 1.9 %copy-start = (f32[16,128,3,128]{3,1,2,0:T(8,128)S(1)}, f32[16,128,3,128]{3,1,2,0:T(8,128)}, u32[]{:S(2)}) copy-start(f32[16,128,3,128]{3,1,2,0:T(8,128)} %param.8) | copy-start | bytes 9437188
  3.9 0.9 copy-start.2
  9.2 6.2 %copy-start.1 = (f32[16,128,128]{2,1,0:T(8,128)S(1)}, f32[16,128,128]{2,1,0:T(8,128)}, u32[]{:S(2)}) copy-start(f32[16,128,128]{2,1,0:T(8,128)} %c0_ref.1) | copy-start | bytes 3145732
  9.2 30.7 %copy-start.3 = (s32[1024,4]{0,1:T(4,128)S(1)}, s32[1024,4]{0,1:T(4,128)}, u32[]{:S(2)}) copy-start(s32[1024,4]{0,1:T(4,128)} %param.6) | copy-start | bytes 49156
  9.2 30.7 %copy-start.4 = (s32[64]{0:T(128)S(1)}, s32[64]{0:T(128)}, u32[]{:S(2)}) copy-start(s32[64]{0:T(128)} %counts_ref.1) | copy-start | bytes 772
  9.2 4.5 %collective-permute-start = (f32[8,128,128]{2,1,0:T(8,128)S(1)}, f32[8,128,128]{2,1,0:T(8,128)S(1)}, u32[]{:S(2)}, u32[]{:S(2)}) collective-permute-start(f32[8,128,128]{2,1,0:T(8,128)S(1)} %coupling.3), channel_id=1, source_target_pairs={{0,1},{1,0},{2,3},{3,2},{4,5},{5,4},{6,7},{7,6},{8,9},{9,8},{10,11... | collective-permute-start | bytes 1572872 | tf_op jit(solution)/shard_map/ppermute | solution.py:231
  13.8 24.0 %collective-permute-start.1 = (f32[8,128,128]{2,1,0:T(8,128)S(1)}, f32[8,128,128]{2,1,0:T(8,128)S(1)}, u32[]{:S(2)}, u32[]{:S(2)}) collective-permute-start(f32[8,128,128]{2,1,0:T(8,128)S(1)} %add.6), channel_id=1, source_target_pairs={{0,2},{2,0},{1,3},{3,1},{4,6},{6,4},{5,7},{7,5},{8,10},{10,8},{9,1... | collective-permute-start | bytes 1572872 | tf_op jit(solution)/shard_map/ppermute | solution.py:231
  15.4 22.6 %collective-permute-start.3 = (f32[16,128,128]{2,1,0:T(8,128)S(1)}, f32[16,128,128]{2,1,0:T(8,128)S(1)}, u32[]{:S(2)}, u32[]{:S(2)}) collective-permute-start(f32[16,128,128]{2,1,0:T(8,128)S(1)} %copy-done.1), channel_id=1, source_target_pairs={{0,1},{1,0},{2,3},{3,2},{4,5},{5,4},{6,7},{7,6},{8,9},{9,8},{10,11... | collective-permute-start | bytes 3145736 | tf_op jit(solution)/shard_map/ppermute | solution.py:231
  27.7 12.2 %collective-permute-start.5 = (f32[16,128,128]{2,1,0:T(8,128)S(1)}, f32[16,128,128]{2,1,0:T(8,128)S(1)}, u32[]{:S(2)}, u32[]{:S(2)}) collective-permute-start(f32[16,128,128]{2,1,0:T(8,128)S(1)} %collective-permute-done.4.c2_ref), channel_id=1, source_target_pairs={{0,1},{1,0},{2,3},{3,2},{4,5},{5,4},{6,7},{7,6},{8,9},{9,8},{10,11... | collective-permute-start | bytes 3145736 | tf_op jit(solution)/shard_map/ppermute | solution.py:231
  37.9 2.0 %collective-permute-start.2 = (f32[8,128,128]{2,1,0:T(8,128)S(1)}, f32[8,128,128]{2,1,0:T(8,128)S(1)}, u32[]{:S(2)}, u32[]{:S(2)}) collective-permute-start(f32[8,128,128]{2,1,0:T(8,128)S(1)} %add.7.own_ref), channel_id=1, source_target_pairs={{0,1},{1,0},{2,3},{3,2},{4,5},{5,4},{6,7},{7,6},{8,9},{9,8},{10,11... | collective-permute-start | bytes 1572872 | tf_op jit(solution)/shard_map/ppermute | solution.py:231
  42.7 17.6 %collective-permute-start.13 = (f32[2,2,2,2,2,4,8,128]{7,6,5,4,3,2,1,0:T(8,128)S(1)}, f32[2,2,2,2,2,4,8,128]{7,6,5,4,3,2,1,0:T(8,128)S(1)}, u32[]{:S(2)}, u32[]{:S(2)}) collective-permute-start(f32[2,2,2,2,2,4,8,128]{7,6,5,4,3,2,1,0:T(8,128)S(1)} %get-tuple-element.56), channel_id=1, source_target_pairs={{0,8},{8,0},{1,9},{9,1},{2,10},{10,2},{3,11},{11,3},{4,12},{12,4},... | collective-permute-start | bytes 1572872 | tf_op jit(solution)/shard_map/ppermute | solution.py:231
  44.7 16.8 %collective-permute-start.19 = (f32[2,2,2,2,2,4,8,128]{7,6,5,4,3,2,1,0:T(8,128)S(1)}, f32[2,2,2,2,2,4,8,128]{7,6,5,4,3,2,1,0:T(8,128)S(1)}, u32[]{:S(2)}, u32[]{:S(2)}) collective-permute-start(f32[2,2,2,2,2,4,8,128]{7,6,5,4,3,2,1,0:T(8,128)S(1)} %get-tuple-element.68), channel_id=1, source_target_pairs={{0,4},{4,0},{1,5},{5,1},{2,6},{6,2},{3,7},{7,3},{8,12},{12,8},{9,1... | collective-permute-start | bytes 1572872 | tf_op jit(solution)/shard_map/ppermute | solution.py:231
  49.1 9.2 %collective-permute-start.6 = (f32[2,2,2,2,5,8,128]{6,5,4,3,2,1,0:T(8,128)S(1)}, f32[2,2,2,2,5,8,128]{6,5,4,3,2,1,0:T(8,128)S(1)}, u32[]{:S(2)}, u32[]{:S(2)}) collective-permute-start(f32[2,2,2,2,5,8,128]{6,5,4,3,2,1,0:T(8,128)S(1)} %get-tuple-element.43), channel_id=1, source_target_pairs={{0,64},{64,0},{1,65},{65,1},{2,66},{66,2},{3,67},{67,3},{4,68},{68... | collective-permute-start | bytes 983048 | tf_op jit(solution)/shard_map/ppermute | solution.py:231
  49.1 10.4 %collective-permute-start.7 = (f32[2,2,2,2,5,8,128]{6,5,4,3,2,1,0:T(8,128)S(1)}, f32[2,2,2,2,5,8,128]{6,5,4,3,2,1,0:T(8,128)S(1)}, u32[]{:S(2)}, u32[]{:S(2)}) collective-permute-start(f32[2,2,2,2,5,8,128]{6,5,4,3,2,1,0:T(8,128)S(1)} %get-tuple-element.44), channel_id=1, source_target_pairs={{0,192},{64,128},{128,64},{192,0},{1,193},{65,129},{129,65},{193,1... | collective-permute-start | bytes 983048 | tf_op jit(solution)/shard_map/ppermute | solution.py:227
  59.6 8.6 %collective-permute-start.8 = (f32[2,2,2,2,5,8,128]{6,5,4,3,2,1,0:T(8,128)S(1)}, f32[2,2,2,2,5,8,128]{6,5,4,3,2,1,0:T(8,128)S(1)}, u32[]{:S(2)}, u32[]{:S(2)}) collective-permute-start(f32[2,2,2,2,5,8,128]{6,5,4,3,2,1,0:T(8,128)S(1)} %get-tuple-element.46), channel_id=1, source_target_pairs={{0,8},{8,0},{1,9},{9,1},{2,10},{10,2},{3,11},{11,3},{4,12},{12,4},... | collective-permute-start | bytes 983048 | tf_op jit(solution)/shard_map/ppermute | solution.py:231
  60.4 9.1 %collective-permute-start.14 = (f32[2,2,2,2,4,8,128]{6,5,4,3,2,1,0:T(8,128)S(1)}, f32[2,2,2,2,4,8,128]{6,5,4,3,2,1,0:T(8,128)S(1)}, u32[]{:S(2)}, u32[]{:S(2)}) collective-permute-start(f32[2,2,2,2,4,8,128]{6,5,4,3,2,1,0:T(8,128)S(1)} %get-tuple-element.58), channel_id=1, source_target_pairs={{0,4},{4,0},{1,5},{5,1},{2,6},{6,2},{3,7},{7,3},{8,12},{12,8},{9,1... | collective-permute-start | bytes 786440 | tf_op jit(solution)/shard_map/ppermute | solution.py:231
  61.7 8.5 %collective-permute-start.20 = (f32[2,2,2,2,4,8,128]{6,5,4,3,2,1,0:T(8,128)S(1)}, f32[2,2,2,2,4,8,128]{6,5,4,3,2,1,0:T(8,128)S(1)}, u32[]{:S(2)}, u32[]{:S(2)}) collective-permute-start(f32[2,2,2,2,4,8,128]{6,5,4,3,2,1,0:T(8,128)S(1)} %get-tuple-element.70), channel_id=1, source_target_pairs={{0,64},{64,0},{1,65},{65,1},{2,66},{66,2},{3,67},{67,3},{4,68},{68... | collective-permute-start | bytes 786440 | tf_op jit(solution)/shard_map/ppermute | solution.py:231
  68.3 5.4 %collective-permute-start.9 = (f32[2,2,2,5,8,128]{5,4,3,2,1,0:T(8,128)S(1)}, f32[2,2,2,5,8,128]{5,4,3,2,1,0:T(8,128)S(1)}, u32[]{:S(2)}, u32[]{:S(2)}) collective-permute-start(f32[2,2,2,5,8,128]{5,4,3,2,1,0:T(8,128)S(1)} %get-tuple-element.48), channel_id=1, source_target_pairs={{0,4},{4,0},{1,5},{5,1},{2,6},{6,2},{3,7},{7,3},{8,12},{12,8},{9,1... | collective-permute-start | bytes 491528 | tf_op jit(solution)/shard_map/ppermute | solution.py:231
  69.5 6.8 %collective-permute-start.15 = (f32[2,2,2,4,8,128]{5,4,3,2,1,0:T(8,128)S(1)}, f32[2,2,2,4,8,128]{5,4,3,2,1,0:T(8,128)S(1)}, u32[]{:S(2)}, u32[]{:S(2)}) collective-permute-start(f32[2,2,2,4,8,128]{5,4,3,2,1,0:T(8,128)S(1)} %get-tuple-element.60), channel_id=1, source_target_pairs={{0,64},{64,0},{1,65},{65,1},{2,66},{66,2},{3,67},{67,3},{4,68},{68... | collective-permute-start | bytes 393224 | tf_op jit(solution)/shard_map/ppermute | solution.py:231
  70.2 9.5 %collective-permute-start.21 = (f32[2,2,2,4,8,128]{5,4,3,2,1,0:T(8,128)S(1)}, f32[2,2,2,4,8,128]{5,4,3,2,1,0:T(8,128)S(1)}, u32[]{:S(2)}, u32[]{:S(2)}) collective-permute-start(f32[2,2,2,4,8,128]{5,4,3,2,1,0:T(8,128)S(1)} %get-tuple-element.72), channel_id=1, source_target_pairs={{0,8},{8,0},{1,9},{9,1},{2,10},{10,2},{3,11},{11,3},{4,12},{12,4},... | collective-permute-start | bytes 393224 | tf_op jit(solution)/shard_map/ppermute | solution.py:231
  73.7 10.7 %collective-permute-start.10 = (f32[2,2,5,8,128]{4,3,2,1,0:T(8,128)S(1)}, f32[2,2,5,8,128]{4,3,2,1,0:T(8,128)S(1)}, u32[]{:S(2)}, u32[]{:S(2)}) collective-permute-start(f32[2,2,5,8,128]{4,3,2,1,0:T(8,128)S(1)} %get-tuple-element.50), channel_id=1, source_target_pairs={{0,128},{128,0},{1,129},{129,1},{2,130},{130,2},{3,131},{131,3},{4... | collective-permute-start | bytes 245768 | tf_op jit(solution)/shard_map/ppermute | solution.py:231
  76.3 9.0 %collective-permute-start.16 = (f32[2,2,4,8,128]{4,3,2,1,0:T(8,128)S(1)}, f32[2,2,4,8,128]{4,3,2,1,0:T(8,128)S(1)}, u32[]{:S(2)}, u32[]{:S(2)}) collective-permute-start(f32[2,2,4,8,128]{4,3,2,1,0:T(8,128)S(1)} %get-tuple-element.62), channel_id=1, source_target_pairs={{0,16},{16,0},{1,17},{17,1},{2,18},{18,2},{3,19},{19,3},{4,20},{20... | collective-permute-start | bytes 196616 | tf_op jit(solution)/shard_map/ppermute | solution.py:231
  79.8 10.6 %collective-permute-start.22 = (f32[2,2,4,8,128]{4,3,2,1,0:T(8,128)S(1)}, f32[2,2,4,8,128]{4,3,2,1,0:T(8,128)S(1)}, u32[]{:S(2)}, u32[]{:S(2)}) collective-permute-start(f32[2,2,4,8,128]{4,3,2,1,0:T(8,128)S(1)} %get-tuple-element.74), channel_id=1, source_target_pairs={{0,32},{32,0},{1,33},{33,1},{2,34},{34,2},{3,35},{35,3},{4,36},{36... | collective-permute-start | bytes 196616 | tf_op jit(solution)/shard_map/ppermute | solution.py:231
  84.5 8.6 %collective-permute-start.11 = (f32[2,5,8,128]{3,2,1,0:T(8,128)S(1)}, f32[2,5,8,128]{3,2,1,0:T(8,128)S(1)}, u32[]{:S(2)}, u32[]{:S(2)}) collective-permute-start(f32[2,5,8,128]{3,2,1,0:T(8,128)S(1)} %get-tuple-element.52), channel_id=1, source_target_pairs={{0,16},{16,0},{1,17},{17,1},{2,18},{18,2},{3,19},{19,3},{4,20},{20... | collective-permute-start | bytes 122888 | tf_op jit(solution)/shard_map/ppermute | solution.py:231
  85.3 10.1 %collective-permute-start.17 = (f32[2,4,8,128]{3,2,1,0:T(8,128)S(1)}, f32[2,4,8,128]{3,2,1,0:T(8,128)S(1)}, u32[]{:S(2)}, u32[]{:S(2)}) collective-permute-start(f32[2,4,8,128]{3,2,1,0:T(8,128)S(1)} %get-tuple-element.64), channel_id=1, source_target_pairs={{0,32},{32,0},{1,33},{33,1},{2,34},{34,2},{3,35},{35,3},{4,36},{36... | collective-permute-start | bytes 98312 | tf_op jit(solution)/shard_map/ppermute | solution.py:231
  90.4 6.0 %collective-permute-start.23 = (f32[2,4,8,128]{3,2,1,0:T(8,128)S(1)}, f32[2,4,8,128]{3,2,1,0:T(8,128)S(1)}, u32[]{:S(2)}, u32[]{:S(2)}) collective-permute-start(f32[2,4,8,128]{3,2,1,0:T(8,128)S(1)} %get-tuple-element.76), channel_id=1, source_target_pairs={{0,128},{128,0},{1,129},{129,1},{2,130},{130,2},{3,131},{131,3},{4... | collective-permute-start | bytes 98312 | tf_op jit(solution)/shard_map/ppermute | solution.py:231
  93.1 7.8 %collective-permute-start.12 = (f32[5,8,128]{2,1,0:T(8,128)S(1)}, f32[5,8,128]{2,1,0:T(8,128)S(1)}, u32[]{:S(2)}, u32[]{:S(2)}) collective-permute-start(f32[5,8,128]{2,1,0:T(8,128)S(1)} %get-tuple-element.54), channel_id=1, source_target_pairs={{0,32},{32,0},{1,33},{33,1},{2,34},{34,2},{3,35},{35,3},{4,36},{36... | collective-permute-start | bytes 61448 | tf_op jit(solution)/shard_map/ppermute | solution.py:231
  95.5 5.3 %collective-permute-start.18 = (f32[4,8,128]{2,1,0:T(8,128)S(1)}, f32[4,8,128]{2,1,0:T(8,128)S(1)}, u32[]{:S(2)}, u32[]{:S(2)}) collective-permute-start(f32[4,8,128]{2,1,0:T(8,128)S(1)} %get-tuple-element.66), channel_id=1, source_target_pairs={{0,128},{128,0},{1,129},{129,1},{2,130},{130,2},{3,131},{131,3},{4... | collective-permute-start | bytes 49160 | tf_op jit(solution)/shard_map/ppermute | solution.py:231
  96.5 4.7 %collective-permute-start.24 = (f32[4,8,128]{2,1,0:T(8,128)S(1)}, f32[4,8,128]{2,1,0:T(8,128)S(1)}, u32[]{:S(2)}, u32[]{:S(2)}) collective-permute-start(f32[4,8,128]{2,1,0:T(8,128)S(1)} %get-tuple-element.78), channel_id=1, source_target_pairs={{0,16},{16,0},{1,17},{17,1},{2,18},{18,2},{3,19},{19,3},{4,20},{20... | collective-permute-start | bytes 49160 | tf_op jit(solution)/shard_map/ppermute | solution.py:231

commit v6 on v4

--- a/solution.py
+++ b/solution.py
@@ -8,9 +8,13 @@
 
 W = 128
 SLOTS = 16
-HALF = SLOTS // 2
+BASE = 8
+MOVED = 4
+CAP = BASE + MOVED
+HALF = CAP // 2
 CHUNK = 4
 GT = 4
+PARTNER = 32
 NXH, NXL, NZH, NZL, NYL = 2, 2, 4, 2, 2
 GROUPS = (("xl", "zl", "yl", GT + 1), ("zl", "yl", "xl", GT), ("yl", "xl", "zl", GT))
 F32 = jnp.float32
@@ -21,6 +25,9 @@
 HBM = pl.BlockSpec(memory_space=pltpu.HBM)
 
 
+COUPLING_MIB = 8
+
+
 def split(value):
     high = value.astype(BF16)
     return high, (value - high.astype(F32)).astype(BF16)
@@ -35,23 +42,28 @@
     return (((xh * NXL + xl) * NZH + zh) * NZL + zl) * NYL + yl
 
 
-def coupling_kernel(mine, pts_hbm, inv_ref, out_ref, pts_buf, sems):
+def half_slots(half):
+    return [half * (BASE // 2) + i for i in range(BASE // 2)] + [BASE + half * (MOVED // 2) + i for i in range(MOVED // 2)]
+
+
+def coupling_kernel(which, pts_hbm, inv_ref, out_ref, pts_buf, sems):
     core = lax.axis_index("c")
-    base = (core if mine else 1 - core) * HALF
-
-    def fetch(i):
-        return pltpu.make_async_copy(pts_hbm.at[base + i], pts_buf.at[i], sems.at[i])
-
-    for i in range(HALF):
-        fetch(i).start()
-    for i in range(HALF):
-        fetch(i).wait()
+    if which == "moved":
+        slots = [CAP + i for i in range(MOVED)]
+    else:
+        slots = half_slots(core if which == "keep" else 1 - core)
+
+    copies = [pltpu.make_async_copy(pts_hbm.at[slot], pts_buf.at[i], sems.at[i]) for i, slot in enumerate(slots)]
+    for copy in copies:
+        copy.start()
+    for i, slot in enumerate(slots):
+        copies[i].wait()
         pts = [pts_buf[i, j] for j in range(3)]
         pairs = []
         for k in range(3):
             weighted = None
             for j in range(3):
-                term = pts[j] * inv_ref[j, k, pl.ds(base + i, 1), :]
+                term = pts[j] * inv_ref[j, k, pl.ds(slot, 1), :]
                 weighted = term if weighted is None else weighted + term
             pairs.append((split(weighted), split(pts[k])))
         left = jnp.concatenate([w[0] for w, _ in pairs] + [w[0] for w, _ in pairs] + [w[1] for w, _ in pairs], axis=1)
@@ -59,41 +71,95 @@
         out_ref[i] = lax.dot_general(left, right, (((1,), (1,)), ((), ())), preferred_element_type=F32)
 
 
-def coupling(mine, pts, inv):
+def coupling(which, pts, inv):
+    count = MOVED if which == "moved" else HALF
+
     def kernel(*refs):
-        coupling_kernel(mine, *refs)
+        coupling_kernel(which, *refs)
 
     return pl.pallas_call(
         kernel,
-        out_shape=jax.ShapeDtypeStruct((HALF, W, W), F32),
+        out_shape=jax.ShapeDtypeStruct((count, W, W), F32),
         in_specs=[HBM, VMEM],
         out_specs=VMEM,
-        scratch_shapes=[pltpu.VMEM((HALF, 3, W, W), F32), pltpu.SemaphoreType.DMA((HALF,))],
-        cost_estimate=pl.CostEstimate(flops=HALF * 2 * 9 * W * W * W, bytes_accessed=HALF * 4 * W * W * 4, transcendentals=0),
-        compiler_params=pltpu.CompilerParams(vmem_limit_bytes=8 << 20),
+        scratch_shapes=[pltpu.VMEM((count, 3, W, W), F32), pltpu.SemaphoreType.DMA((count,))],
+        cost_estimate=pl.CostEstimate(flops=count * 2 * 9 * W * W * W, bytes_accessed=count * 4 * W * W * 4, transcendentals=0),
+        compiler_params=pltpu.CompilerParams(vmem_limit_bytes=COUPLING_MIB << 20),
         name="coupling",
     )(pts, inv)
 
 
-def schur_kernel(counts_ref, tiles_ref, own_ref, oth_ref, c0_ref, c1_ref, c2_ref, c3_ref, *refs):
-    outs, o_sems, accs = refs[:7], refs[7], refs[8:]
+def combine_kernel(counts_ref, keep_ref, recv_ref, mine_ref, other_ref, out_ref):
+    core = lax.axis_index("c")
+    heavy = counts_ref[cluster_device()] > CAP
+    for i in range(HALF):
+        value = keep_ref[i] + recv_ref[i]
+        if i >= BASE // 2:
+            at = core * (MOVED // 2) + i - BASE // 2
+            value = jnp.where(heavy, value, mine_ref[at] + other_ref[at])
+        out_ref[i] = value
+
+
+def in_vmem(values):
+    return [pltpu.with_memory_space_constraint(v, pltpu.VMEM) for v in values]
+
+
+def combine(counts, *values):
+    return pl.pallas_call(
+        combine_kernel,
+        out_shape=jax.ShapeDtypeStruct((HALF, W, W), F32),
+        in_specs=[SMEM] + [VMEM] * 4,
+        out_specs=VMEM,
+        compiler_params=pltpu.CompilerParams(vmem_limit_bytes=4 << 20),
+        name="combine",
+    )(counts, *in_vmem(values))
+
+
+def choose_kernel(counts_ref, own_ref, recv_ref, out_ref):
+    heavy = counts_ref[cluster_device()] > CAP
+    out_ref[...] = jnp.where(heavy, own_ref[...], recv_ref[...])
+
+
+def choose(counts, own, recv):
+    return pl.pallas_call(
+        choose_kernel,
+        out_shape=jax.ShapeDtypeStruct(own.shape, F32),
+        in_specs=[SMEM] + [VMEM] * 2,
+        out_specs=VMEM,
+        compiler_params=pltpu.CompilerParams(vmem_limit_bytes=4 << 20),
+        name="choose",
+    )(counts, *in_vmem((own, recv)))
+
+
+def schur_kernel(counts_ref, tiles_ref, own_ref, oth_ref, *refs):
+    base_panels, moved_panels, outs, o_sems, accs = refs[:4], refs[4:8], refs[8:15], refs[15], refs[16:]
     core = lax.axis_index("c")
     cam = camera_index()
     device = cluster_device()
-    live = counts_ref[device]
-    panels = (c0_ref, c1_ref, c2_ref, c3_ref)
-
-    steps = SLOTS // CHUNK
+    count = counts_ref[device]
+    partner = lax.bitwise_xor(device, PARTNER)
+    heavy = count > CAP
+    moved_live = jnp.where(heavy, count - BASE, counts_ref[partner] - CAP)
+    moved_first = jnp.where(heavy, device * SLOTS + BASE, partner * SLOTS + CAP)
+
     for acc in accs:
         acc[...] = jnp.zeros_like(acc)
 
-    for k in range(steps):
-        @pl.when(k * CHUNK < live)
+    for k in range(CAP // CHUNK):
+        moved = k * CHUNK >= BASE
+        panels = moved_panels if moved else base_panels
+        start = k * CHUNK - (BASE if moved else 0)
+        live = moved_live if moved else count
+
+        @pl.when(start < live)
         def _():
             for i in range(CHUNK):
-                slot = k * CHUNK + i
-                m_high, m_low = split(jnp.where(core == k // 2, own_ref[slot % HALF], oth_ref[slot % HALF]))
-                panel_t = c0_ref[slot].T
+                slot = start + i
+                table = (moved_first if moved else device * SLOTS) + slot
+                per_half = (MOVED if moved else BASE) // 2
+                m_at = slot % per_half + (BASE // 2 if moved else 0)
+                m_high, m_low = split(jnp.where(core == slot // per_half, own_ref[m_at], oth_ref[m_at]))
+                panel_t = panels[0][slot].T
                 t_high, t_low = split(panel_t)
                 prod = jnp.dot(
                     jnp.concatenate([t_high, t_high, t_low], axis=1),
@@ -110,7 +176,7 @@
                 lows = jnp.concatenate([l for _, l in parts], axis=1)
                 right = jnp.concatenate([highs, lows, highs], axis=0)
                 rows = jnp.dot(left, right, preferred_element_type=F32)
-                row_tile = tiles_ref[cam, device * SLOTS + slot]
+                row_tile = tiles_ref[cam, table]
                 for rel in range(4):
                     block = rows[:, rel * W : (rel + 1) * W].reshape(NZH, NZL, NYL, 8, W)
 
@@ -124,7 +190,7 @@
                     if rel == 0:
                         add(0, GT)
                         continue
-                    tile = tiles_ref[lax.bitwise_xor(cam, rel), device * SLOTS + slot]
+                    tile = tiles_ref[lax.bitwise_xor(cam, rel), table]
                     add(rel - 1, tile)
 
     copies = []
@@ -140,14 +206,14 @@
         copy.wait()
 
 
-def schur(counts, tiles, own, oth, panels):
+def schur(counts, tiles, own, oth, base_panels, moved_panels):
     return pl.pallas_call(
         schur_kernel,
         out_shape=[
             jax.ShapeDtypeStruct(lead + (2, NXH, NZH, names[3], 8, W), F32) for k, names in enumerate(GROUPS)
             for lead in (((), (), (2,)) if k == 0 else ((2,), (2,)))
         ],
-        in_specs=[SMEM, SMEM] + [VMEM] * 6,
+        in_specs=[SMEM, SMEM] + [VMEM] * 10,
         out_specs=[ANY] * 7,
         scratch_shapes=[
             pltpu.SemaphoreType.DMA((7,)),
@@ -156,7 +222,7 @@
         cost_estimate=pl.CostEstimate(flops=SLOTS * 6 * 5 * W * W * W, bytes_accessed=SLOTS * 5 * W * W * 4, transcendentals=0),
         compiler_params=pltpu.CompilerParams(vmem_limit_bytes=12 << 20),
         name="schur",
-    )(counts, tiles, *[pltpu.with_memory_space_constraint(v, pltpu.VMEM) for v in (own, oth, *panels)])
+    )(counts, tiles, *in_vmem((own, oth, *base_panels, *moved_panels)))
 
 
 def place_kernel(in_ref, out_ref):
@@ -230,19 +296,22 @@
     pts = point_jac.transpose(0, 2, 1, 3)
     inv = point_inv.transpose(1, 2, 0, 3)
 
-    c0 = cam_jac
-    c2 = swap(c0, "yh")
-    c1 = swap(c0, "c")
-
-    m_send = coupling(False, pts, inv)
-    m_recv = swap(m_send, "c")
-    m_keep = coupling(True, pts, inv)
-    m_chip = m_keep + m_recv
+    a0 = cam_jac[:BASE]
+    a2 = swap(a0, "yh")
+    b_recv = swap(cam_jac[CAP:], "xh")
+    m_moved = coupling("moved", pts, inv)
+    m_moved = swap(m_moved, "xh")
+    m_recv = coupling("send", pts, inv)
+    m_recv = swap(m_recv, "c")
+    b0 = choose(counts, cam_jac[BASE:CAP], b_recv)
+    b2 = swap(b0, "yh")
+    m_keep = coupling("keep", pts, inv)
+    m_chip = combine(counts, m_keep, m_recv, m_moved, swap(m_moved, "c"))
     m_own = m_chip + swap(m_chip, "yh")
     m_oth = swap(m_own, "c")
-    c3 = swap(c2, "c")
-
-    outs = schur(counts, tiles.T, m_own, m_oth, (c0, c1, c2, c3))
+    base = (a0, swap(a0, "c"), a2, swap(a2, "c"))
+    moved = (b0, swap(b0, "c"), b2, swap(b2, "c"))
+    outs = schur(counts, tiles.T, m_own, m_oth, base, moved)
     near_z = swap(outs[3], "zl")
     near_y = swap(outs[5], "yl")
     low_x = swap(outs[0], "xl")

time: 99.5 us -> 100 us (level)
  Pallas kernels: 12.6 us -> 15 us
  waiting for transfers between devices: 42 us -> 40.2 us
    ppermute x15 -> x21, starting transfers between devices: 15.5 us -> 17.7 us  [swap(): return lax.ppermute(value, axis, [(0, 1), (1, 0)])]
    ppermute x15 -> x21, waiting for transfers between devices: 40.8 us -> 38.9 us  [swap(): return lax.ppermute(value, axis, [(0, 1), (1, 0)])]
    ppermute x1, starting transfers between devices: 2.78 us -> 1.15 us  [swap_x_other(): lax.ppermute(value, ('xh', 'xl'), [(i, (i + 1 if i % 2 else i - 1) % size...]
    pallas_call x1, Pallas kernels: 2.8 us -> 4.04 us  [schur(): pl.pallas_call(schur_kernel, out_shape=[jax.ShapeDtypeStruct(lead + (2, N...]
    pallas_call x2 -> x5, Pallas kernels: 8.77 us -> 9.93 us  [the longest x3 8.72 us: coupling(): pl.pallas_call(kernel, out_shape=jax.ShapeDtypeStruct((count, W, W), F32)...]
    unnamed x10 -> x14, local copies, waits for them, and re-layouts: 2.79 us -> 2.8 us
  transfers between devices with their start and end apart: 16 -> 22, of which waited for: 9 -> 12; matrix products, arithmetic and copies ran while one was open for 0% -> 0% of each run, Pallas kernels for 9% -> 8%
where the time goes in v6:
time: 100 us
  waiting for transfers between devices  40.2 us (40%)
  blocking collectives  22.7 us (23%)
  starting transfers between devices  18.9 us (19%)
  Pallas kernels  15 us (15%)
  local copies, waits for them, and re-layouts  2.87 us (3%)
    ppermute x21, waiting for transfers between devices, swap(): return lax.ppermute(value, axis, [(0, 1), (1, 0)])  38.9 us
    all_to_all x1, blocking collectives, on_device(): return place(lax.all_to_all(part, ('xh', 'zh'), 0, 0, tiled=True))  22.7 us
    ppermute x21, starting transfers between devices, swap(): return lax.ppermute(value, axis, [(0, 1), (1, 0)])  17.7 us
    pallas_call x3, Pallas kernels, coupling(): pl.pallas_call(kernel, out_shape=jax.ShapeDtypeStruct((count, W, W), F32)...  8.72 us
    pallas_call x1, Pallas kernels, schur(): pl.pallas_call(schur_kernel, out_shape=[jax.ShapeDtypeStruct(lead + (2, N...  4.04 us
    unnamed x14, local copies, waits for them, and re-layouts  2.8 us
  transfers between devices with their start and end apart: 22, of which 12 were waited for; matrix products, arithmetic and copies ran while one was open for 0% of the time, Pallas kernels for 8%

profile of v6, /device:TPU:16, one launch (start us, length us, event | category | flops | bytes accessed | tf_op | source)
XLA Modules:
  0.0 100.0 jit_solution(1733649980849962823)
XLA Ops:
  0.0 1.9 %copy-done = f32[16,128,3,128]{3,1,2,0:T(8,128)S(1)} copy-done((f32[16,128,3,128]{3,1,2,0:T(8,128)S(1)}, f32[16,128,3,128]{3,1,2,0:T(8,128)}, u32[]{:S(2)}) %copy-start) | copy-done | bytes 3145752
  1.9 0.9 copy-done.2
  2.8 2.2 %coupling.5 = f32[4,128,128]{2,1,0:T(8,128)S(1)} custom-call(f32[16,3,128,128]{3,2,1,0:T(8,128)S(1)} %bitcast.6, f32[3,3,16,128]{3,2,1,0:T(8,128)S(1)} %bitcast.9), custom_call_target="tpu_custom_call" | custom-call | flops 150994944 | bytes 1048576 | tf_op jit(solution)/shard_map/coupling/pallas_call | solution.py:80
  5.0 0.0 copy-start.1
  5.0 0.0 copy-start.3
  5.0 3.1 %collective-permute-start.1 = (f32[4,128,128]{2,1,0:T(8,128)S(1)}, f32[4,128,128]{2,1,0:T(8,128)S(1)}, u32[]{:S(2)}, u32[]{:S(2)}) collective-permute-start(f32[4,128,128]{2,1,0:T(8,128)S(1)} %coupling.5), channel_id=1, source_target_pairs={{0,128},{128,0},{1,129},{129,1},{2,130},{130,2},{3,131},{131,3},{4... | collective-permute-start | bytes 786440 | tf_op jit(solution)/shard_map/ppermute | solution.py:292
  8.1 3.3 %coupling.4 = f32[6,128,128]{2,1,0:T(8,128)S(1)} custom-call(f32[16,3,128,128]{3,2,1,0:T(8,128)S(1)} %bitcast.7, f32[3,3,16,128]{3,2,1,0:T(8,128)S(1)} %bitcast.10), custom_call_target="tpu_custom_call" | custom-call | flops 226492416 | bytes 1572864 | tf_op jit(solution)/shard_map/coupling/pallas_call | solution.py:80
  11.4 0.0 copy-start.5
  11.4 0.1 collective-permute-start
  11.5 0.4 collective-permute-start.6
  11.9 2.7 %collective-permute-done.1.mine_ref = f32[4,128,128]{2,1,0:T(8,128)S(1)} collective-permute-done((f32[4,128,128]{2,1,0:T(8,128)S(1)}, f32[4,128,128]{2,1,0:T(8,128)S(1)}, u32[]{:S(2)}, u32[]{:S(2)}) %collective-permute-start.1) | collective-permute-done | bytes 262176 | tf_op jit(solution)/shard_map/ppermute | solution.py:292
  14.7 0.0 copy-start.4
  14.7 3.1 %collective-permute-start.8 = (f32[4,128,128]{2,1,0:T(8,128)S(1)}, f32[4,128,128]{2,1,0:T(8,128)S(1)}, u32[]{:S(2)}, u32[]{:S(2)}) collective-permute-start(f32[4,128,128]{2,1,0:T(8,128)S(1)} %get-tuple-element.43), channel_id=1, source_target_pairs={{0,128},{128,0},{1,129},{129,1},{2,130},{130,2},{3,131},{131,3},{4... | collective-permute-start | bytes 786440 | tf_op jit(solution)/shard_map/ppermute | solution.py:292
  17.8 3.3 %coupling.3.keep_ref = f32[6,128,128]{2,1,0:T(8,128)S(1)} custom-call(f32[16,3,128,128]{3,2,1,0:T(8,128)S(1)} %bitcast.8, f32[3,3,16,128]{3,2,1,0:T(8,128)S(1)} %bitcast.11), custom_call_target="tpu_custom_call" | custom-call | flops 226492416 | bytes 1572864 | tf_op jit(solution)/shard_map/coupling/pallas_call | solution.py:80
  21.1 0.6 combine.1
  21.7 0.4 collective-permute-start.3
  22.2 2.8 %collective-permute-done.8.recv_ref = f32[4,128,128]{2,1,0:T(8,128)S(1)} collective-permute-done((f32[4,128,128]{2,1,0:T(8,128)S(1)}, f32[4,128,128]{2,1,0:T(8,128)S(1)}, u32[]{:S(2)}, u32[]{:S(2)}) %collective-permute-start.8) | collective-permute-done | bytes 262176 | tf_op jit(solution)/shard_map/ppermute | solution.py:292
  25.0 0.6 choose.1.refs_4_
  25.6 0.6 collective-permute-start.10
  26.2 1.7 %collective-permute-done.6.refs_2_ = f32[8,128,128]{2,1,0:T(8,128)S(1)} collective-permute-done((f32[8,128,128]{2,1,0:T(8,128)S(1)}, f32[8,128,128]{2,1,0:T(8,128)S(1)}, u32[]{:S(2)}, u32[]{:S(2)}) %collective-permute-start.6) | collective-permute-done | bytes 524320 | tf_op jit(solution)/shard_map/ppermute | solution.py:292
  27.9 8.4 %collective-permute-done.3 = f32[6,128,128]{2,1,0:T(8,128)S(1)} collective-permute-done((f32[6,128,128]{2,1,0:T(8,128)S(1)}, f32[6,128,128]{2,1,0:T(8,128)S(1)}, u32[]{:S(2)}, u32[]{:S(2)}) %collective-permute-start.3) | collective-permute-done | bytes 393248 | tf_op jit(solution)/shard_map/ppermute | solution.py:292
  36.3 0.1 add.12.own_ref
  36.4 0.1 collective-permute-start.4
  36.5 0.5 collective-permute-start.9
  37.0 4.5 %collective-permute-done.10.refs_6_ = f32[4,128,128]{2,1,0:T(8,128)S(1)} collective-permute-done((f32[4,128,128]{2,1,0:T(8,128)S(1)}, f32[4,128,128]{2,1,0:T(8,128)S(1)}, u32[]{:S(2)}, u32[]{:S(2)}) %collective-permute-start.10) | collective-permute-done | bytes 262176 | tf_op jit(solution)/shard_map/ppermute | solution.py:292
  41.5 1.5 %collective-permute-done.11.refs_7_ = f32[4,128,128]{2,1,0:T(8,128)S(1)} collective-permute-done((f32[4,128,128]{2,1,0:T(8,128)S(1)}, f32[4,128,128]{2,1,0:T(8,128)S(1)}, u32[]{:S(2)}, u32[]{:S(2)}) %collective-permute-start.11) | collective-permute-done | bytes 262176 | tf_op jit(solution)/shard_map/ppermute | solution.py:292
  43.0 4.0 %schur.1 = (f32[2,2,4,5,8,128]{5,4,3,2,1,0:T(8,128)S(1)}, f32[2,2,4,5,8,128]{5,4,3,2,1,0:T(8,128)S(1)}, f32[2,2,2,4,5,8,128]{6,5,4,3,2,1,0:T(8,128)S(1)}, f32[2,...) custom-call(s32[64]{0:T(128)S(1)} %copy-done.5, ...), custom_call_target="tpu_custom_call" | custom-call | flops 1006632960 | bytes 5242880 | tf_op jit(solution)/shard_map/schur/pallas_call | solution.py:210
  47.1 2.0 %collective-permute-start.16 = (f32[2,2,2,4,4,8,128]{6,5,4,3,2,1,0:T(8,128)S(1)}, f32[2,2,2,4,4,8,128]{6,5,4,3,2,1,0:T(8,128)S(1)}, u32[]{:S(2)}, u32[]{:S(2)}) collective-permute-start(f32[2,2,2,4,4,8,128]{6,5,4,3,2,1,0:T(8,128)S(1)} %get-tuple-element.32), channel_id=1, source_target_pairs={{0,8},{8,0},{1,9},{9,1},{2,10},{10,2},{3,11},{11,3},{4,12},{12,4},... | collective-permute-start | bytes 1572872 | tf_op jit(solution)/shard_map/ppermute | solution.py:292
  49.1 2.3 %collective-permute-start.19 = (f32[2,2,2,4,4,8,128]{6,5,4,3,2,1,0:T(8,128)S(1)}, f32[2,2,2,4,4,8,128]{6,5,4,3,2,1,0:T(8,128)S(1)}, u32[]{:S(2)}, u32[]{:S(2)}) collective-permute-start(f32[2,2,2,4,4,8,128]{6,5,4,3,2,1,0:T(8,128)S(1)} %get-tuple-element.38), channel_id=1, source_target_pairs={{0,4},{4,0},{1,5},{5,1},{2,6},{6,2},{3,7},{7,3},{8,12},{12,8},{9,1... | collective-permute-start | bytes 1572872 | tf_op jit(solution)/shard_map/ppermute | solution.py:292
  51.4 1.1 %collective-permute-start.13 = (f32[2,2,4,5,8,128]{5,4,3,2,1,0:T(8,128)S(1)}, f32[2,2,4,5,8,128]{5,4,3,2,1,0:T(8,128)S(1)}, u32[]{:S(2)}, u32[]{:S(2)}) collective-permute-start(f32[2,2,4,5,8,128]{5,4,3,2,1,0:T(8,128)S(1)} %get-tuple-element.26), channel_id=1, source_target_pairs={{0,192},{64,128},{128,64},{192,0},{1,193},{65,129},{129,65},{193,1... | collective-permute-start | bytes 983048 | tf_op jit(solution)/shard_map/ppermute | solution.py:288
  52.5 8.0 %collective-permute-done.12.refs_1_ = f32[2,2,4,5,8,128]{5,4,3,2,1,0:T(8,128)S(1)} collective-permute-done((f32[2,2,4,5,8,128]{5,4,3,2,1,0:T(8,128)S(1)}, f32[2,2,4,5,8,128]{5,4,3,2,1,0:T(8,128)S(1)}, u32[]{:S(2)}, u32[]{:S(2)}) %collective-permute-start.12) | collective-permute-done | bytes 327712 | tf_op jit(solution)/shard_map/ppermute | solution.py:292
  60.6 1.2 %collective-permute-done.13.refs_2_ = f32[2,2,4,5,8,128]{5,4,3,2,1,0:T(8,128)S(1)} collective-permute-done((f32[2,2,4,5,8,128]{5,4,3,2,1,0:T(8,128)S(1)}, f32[2,2,4,5,8,128]{5,4,3,2,1,0:T(8,128)S(1)}, u32[]{:S(2)}, u32[]{:S(2)}) %collective-permute-start.13) | collective-permute-done | bytes 327712 | tf_op jit(solution)/shard_map/ppermute | solution.py:288
  61.8 0.1 halve.6
  61.9 0.5 collective-permute-start.14
  62.4 0.1 halve.8
  62.5 1.3 %collective-permute-start.17 = (f32[2,2,4,4,8,128]{5,4,3,2,1,0:T(8,128)S(1)}, f32[2,2,4,4,8,128]{5,4,3,2,1,0:T(8,128)S(1)}, u32[]{:S(2)}, u32[]{:S(2)}) collective-permute-start(f32[2,2,4,4,8,128]{5,4,3,2,1,0:T(8,128)S(1)} %get-tuple-element.34), channel_id=1, source_target_pairs={{0,4},{4,0},{1,5},{5,1},{2,6},{6,2},{3,7},{7,3},{8,12},{12,8},{9,1... | collective-permute-start | bytes 786440 | tf_op jit(solution)/shard_map/ppermute | solution.py:292
  63.8 0.1 halve.10
  63.9 0.7 collective-permute-start.20
  64.5 5.8 %collective-permute-done.14.refs_1_ = f32[2,2,4,5,8,128]{5,4,3,2,1,0:T(8,128)S(1)} collective-permute-done((f32[2,2,4,5,8,128]{5,4,3,2,1,0:T(8,128)S(1)}, f32[2,2,4,5,8,128]{5,4,3,2,1,0:T(8,128)S(1)}, u32[]{:S(2)}, u32[]{:S(2)}) %collective-permute-start.14) | collective-permute-done | bytes 327712 | tf_op jit(solution)/shard_map/ppermute | solution.py:292
  70.4 0.8 collective-permute-start.15
  71.3 0.1 collective-permute-start.18
  71.4 0.0 collective-permute-done.20.refs_1_
  71.5 1.6 %collective-permute-start.21 = (f32[2,4,4,8,128]{4,3,2,1,0:T(8,128)S(1)}, f32[2,4,4,8,128]{4,3,2,1,0:T(8,128)S(1)}, u32[]{:S(2)}, u32[]{:S(2)}) collective-permute-start(f32[2,4,4,8,128]{4,3,2,1,0:T(8,128)S(1)} %get-tuple-element.42), channel_id=1, source_target_pairs={{0,8},{8,0},{1,9},{9,1},{2,10},{10,2},{3,11},{11,3},{4,12},{12,4},... | collective-permute-start | bytes 393224 | tf_op jit(solution)/shard_map/ppermute | solution.py:292
  73.1 2.7 %collective-permute-done.15 = f32[2,4,5,8,128]{4,3,2,1,0:T(8,128)S(1)} collective-permute-done((f32[2,4,5,8,128]{4,3,2,1,0:T(8,128)S(1)}, f32[2,4,5,8,128]{4,3,2,1,0:T(8,128)S(1)}, u32[]{:S(2)}, u32[]{:S(2)}) %collective-permute-start.15) | collective-permute-done | bytes 163872 | tf_op jit(solution)/shard_map/ppermute | solution.py:292
  75.8 0.5 collective-permute-done.18
  76.4 0.2 collective-permute-done.21
  76.6 22.7 %all_to_all.5.in_ref = f32[8,13,8,128]{3,2,1,0:T(8,128)S(1)} all-to-all(f32[8,13,8,128]{3,2,1,0:T(8,128)S(1)} %pad_maximum_fusion), channel_id=1, replica_groups=mesh['xh'=2,'xl'=2,'zh'=4,'zl'=2,'yl'=2,'yh'=2,'c'=2] {'xh','zh'}, dimensions={0} | all-to-all | bytes 851968 | tf_op jit(solution)/shard_map/all_to_all | solution.py:332
  99.4 0.7 place.1
  (31 shorter events, 0.3 us)
Async XLA Ops:
  0.0 1.9 %copy-start = (f32[16,128,3,128]{3,1,2,0:T(8,128)S(1)}, f32[16,128,3,128]{3,1,2,0:T(8,128)}, u32[]{:S(2)}) copy-start(f32[16,128,3,128]{3,1,2,0:T(8,128)} %param.8) | copy-start | bytes 9437188
  1.9 0.9 copy-start.2
  2.8 8.7 %copy-start.6 = (f32[16,128,128]{2,1,0:T(8,128)S(1)}, f32[16,128,128]{2,1,0:T(8,128)}, u32[]{:S(2)}) copy-start(f32[16,128,128]{2,1,0:T(8,128)} %param.7) | copy-start | bytes 3145732
  5.0 12.8 %copy-start.1 = (f32[16,128,3,128]{3,1,2,0:T(8,128)S(1)}, f32[16,128,3,128]{3,1,2,0:T(8,128)}, u32[]{:S(2)}) copy-start(f32[16,128,3,128]{3,1,2,0:T(8,128)} %param.8) | copy-start | bytes 9437188
  5.0 12.8 %copy-start.3 = (f32[16,3,3,128]{3,0,2,1:T(8,128)S(1)}, f32[16,3,3,128]{3,0,2,1:T(8,128)}, u32[]{:S(2)}) copy-start(f32[16,3,3,128]{3,0,2,1:T(8,128)} %param.9) | copy-start | bytes 221188
  5.0 9.6 %collective-permute-start.1 = (f32[4,128,128]{2,1,0:T(8,128)S(1)}, f32[4,128,128]{2,1,0:T(8,128)S(1)}, u32[]{:S(2)}, u32[]{:S(2)}) collective-permute-start(f32[4,128,128]{2,1,0:T(8,128)S(1)} %coupling.5), channel_id=1, source_target_pairs={{0,128},{128,0},{1,129},{129,1},{2,130},{130,2},{3,131},{131,3},{4... | collective-permute-start | bytes 786440 | tf_op jit(solution)/shard_map/ppermute | solution.py:292
  11.4 9.8 %copy-start.5 = (s32[64]{0:T(128)S(1)}, s32[64]{0:T(128)}, u32[]{:S(2)}) copy-start(s32[64]{0:T(128)} %counts_ref.5) | copy-start | bytes 772
  11.4 9.7 %collective-permute-start = (f32[6,128,128]{2,1,0:T(8,128)S(1)}, f32[6,128,128]{2,1,0:T(8,128)S(1)}, u32[]{:S(2)}, u32[]{:S(2)}) collective-permute-start(f32[6,128,128]{2,1,0:T(8,128)S(1)} %coupling.4), channel_id=1, source_target_pairs={{0,1},{1,0},{2,3},{3,2},{4,5},{5,4},{6,7},{7,6},{8,9},{9,8},{10,11... | collective-permute-start | bytes 1179656 | tf_op jit(solution)/shard_map/ppermute | solution.py:292
  11.5 16.4 %collective-permute-start.6 = (f32[8,128,128]{2,1,0:T(8,128)S(1)}, f32[8,128,128]{2,1,0:T(8,128)S(1)}, u32[]{:S(2)}, u32[]{:S(2)}) collective-permute-start(f32[8,128,128]{2,1,0:T(8,128)S(1)} %slice.9.refs_0_), channel_id=1, source_target_pairs={{0,2},{2,0},{1,3},{3,1},{4,6},{6,4},{5,7},{7,5},{8,10},{10,8},{9,1... | collective-permute-start | bytes 1572872 | tf_op jit(solution)/shard_map/ppermute | solution.py:292
  14.6 6.5 %collective-permute-start.2 = (f32[4,128,128]{2,1,0:T(8,128)S(1)}, f32[4,128,128]{2,1,0:T(8,128)S(1)}, u32[]{:S(2)}, u32[]{:S(2)}) collective-permute-start(f32[4,128,128]{2,1,0:T(8,128)S(1)} %collective-permute-done.1.mine_ref), channel_id=1, source_target_pairs={{0,1},{1,0},{2,3},{3,2},{4,5},{5,4},{6,7},{7,6},{8,9},{9,8},{10,11... | collective-permute-start | bytes 786440 | tf_op jit(solution)/shard_map/ppermute | solution.py:292
  14.7 28.4 %copy-start.4 = (s32[1024,4]{0,1:T(4,128)S(1)}, s32[1024,4]{0,1:T(4,128)}, u32[]{:S(2)}) copy-start(s32[1024,4]{0,1:T(4,128)} %param.6) | copy-start | bytes 49156
  14.7 10.3 %collective-permute-start.8 = (f32[4,128,128]{2,1,0:T(8,128)S(1)}, f32[4,128,128]{2,1,0:T(8,128)S(1)}, u32[]{:S(2)}, u32[]{:S(2)}) collective-permute-start(f32[4,128,128]{2,1,0:T(8,128)S(1)} %get-tuple-element.43), channel_id=1, source_target_pairs={{0,128},{128,0},{1,129},{129,1},{2,130},{130,2},{3,131},{131,3},{4... | collective-permute-start | bytes 786440 | tf_op jit(solution)/shard_map/ppermute | solution.py:292
  21.7 14.6 %collective-permute-start.3 = (f32[6,128,128]{2,1,0:T(8,128)S(1)}, f32[6,128,128]{2,1,0:T(8,128)S(1)}, u32[]{:S(2)}, u32[]{:S(2)}) collective-permute-start(f32[6,128,128]{2,1,0:T(8,128)S(1)} %combine.1), channel_id=1, source_target_pairs={{0,2},{2,0},{1,3},{3,1},{4,6},{6,4},{5,7},{7,5},{8,10},{10,8},{9,1... | collective-permute-start | bytes 1179656 | tf_op jit(solution)/shard_map/ppermute | solution.py:292
  22.2 19.3 %collective-permute-start.5 = (f32[8,128,128]{2,1,0:T(8,128)S(1)}, f32[8,128,128]{2,1,0:T(8,128)S(1)}, u32[]{:S(2)}, u32[]{:S(2)}) collective-permute-start(f32[8,128,128]{2,1,0:T(8,128)S(1)} %slice.9.refs_0_), channel_id=1, source_target_pairs={{0,1},{1,0},{2,3},{3,2},{4,5},{5,4},{6,7},{7,6},{8,9},{9,8},{10,11... | collective-permute-start | bytes 1572872 | tf_op jit(solution)/shard_map/ppermute | solution.py:292
  25.6 15.9 %collective-permute-start.10 = (f32[4,128,128]{2,1,0:T(8,128)S(1)}, f32[4,128,128]{2,1,0:T(8,128)S(1)}, u32[]{:S(2)}, u32[]{:S(2)}) collective-permute-start(f32[4,128,128]{2,1,0:T(8,128)S(1)} %choose.1.refs_4_), channel_id=1, source_target_pairs={{0,2},{2,0},{1,3},{3,1},{4,6},{6,4},{5,7},{7,5},{8,10},{10,8},{9,1... | collective-permute-start | bytes 786440 | tf_op jit(solution)/shard_map/ppermute | solution.py:292
  27.9 15.1 %collective-permute-start.7 = (f32[8,128,128]{2,1,0:T(8,128)S(1)}, f32[8,128,128]{2,1,0:T(8,128)S(1)}, u32[]{:S(2)}, u32[]{:S(2)}) collective-permute-start(f32[8,128,128]{2,1,0:T(8,128)S(1)} %collective-permute-done.6.refs_2_), channel_id=1, source_target_pairs={{0,1},{1,0},{2,3},{3,2},{4,5},{5,4},{6,7},{7,6},{8,9},{9,8},{10,11... | collective-permute-start | bytes 1572872 | tf_op jit(solution)/shard_map/ppermute | solution.py:292
  36.4 6.6 %collective-permute-start.4 = (f32[6,128,128]{2,1,0:T(8,128)S(1)}, f32[6,128,128]{2,1,0:T(8,128)S(1)}, u32[]{:S(2)}, u32[]{:S(2)}) collective-permute-start(f32[6,128,128]{2,1,0:T(8,128)S(1)} %add.12.own_ref), channel_id=1, source_target_pairs={{0,1},{1,0},{2,3},{3,2},{4,5},{5,4},{6,7},{7,6},{8,9},{9,8},{10,11... | collective-permute-start | bytes 1179656 | tf_op jit(solution)/shard_map/ppermute | solution.py:292
  36.5 5.0 %collective-permute-start.9 = (f32[4,128,128]{2,1,0:T(8,128)S(1)}, f32[4,128,128]{2,1,0:T(8,128)S(1)}, u32[]{:S(2)}, u32[]{:S(2)}) collective-permute-start(f32[4,128,128]{2,1,0:T(8,128)S(1)} %choose.1.refs_4_), channel_id=1, source_target_pairs={{0,1},{1,0},{2,3},{3,2},{4,5},{5,4},{6,7},{7,6},{8,9},{9,8},{10,11... | collective-permute-start | bytes 786440 | tf_op jit(solution)/shard_map/ppermute | solution.py:292
  41.5 1.5 %collective-permute-start.11 = (f32[4,128,128]{2,1,0:T(8,128)S(1)}, f32[4,128,128]{2,1,0:T(8,128)S(1)}, u32[]{:S(2)}, u32[]{:S(2)}) collective-permute-start(f32[4,128,128]{2,1,0:T(8,128)S(1)} %collective-permute-done.10.refs_6_), channel_id=1, source_target_pairs={{0,1},{1,0},{2,3},{3,2},{4,5},{5,4},{6,7},{7,6},{8,9},{9,8},{10,11... | collective-permute-start | bytes 786440 | tf_op jit(solution)/shard_map/ppermute | solution.py:292
  47.1 15.3 %collective-permute-start.16 = (f32[2,2,2,4,4,8,128]{6,5,4,3,2,1,0:T(8,128)S(1)}, f32[2,2,2,4,4,8,128]{6,5,4,3,2,1,0:T(8,128)S(1)}, u32[]{:S(2)}, u32[]{:S(2)}) collective-permute-start(f32[2,2,2,4,4,8,128]{6,5,4,3,2,1,0:T(8,128)S(1)} %get-tuple-element.32), channel_id=1, source_target_pairs={{0,8},{8,0},{1,9},{9,1},{2,10},{10,2},{3,11},{11,3},{4,12},{12,4},... | collective-permute-start | bytes 1572872 | tf_op jit(solution)/shard_map/ppermute | solution.py:292
  49.1 14.7 %collective-permute-start.19 = (f32[2,2,2,4,4,8,128]{6,5,4,3,2,1,0:T(8,128)S(1)}, f32[2,2,2,4,4,8,128]{6,5,4,3,2,1,0:T(8,128)S(1)}, u32[]{:S(2)}, u32[]{:S(2)}) collective-permute-start(f32[2,2,2,4,4,8,128]{6,5,4,3,2,1,0:T(8,128)S(1)} %get-tuple-element.38), channel_id=1, source_target_pairs={{0,4},{4,0},{1,5},{5,1},{2,6},{6,2},{3,7},{7,3},{8,12},{12,8},{9,1... | collective-permute-start | bytes 1572872 | tf_op jit(solution)/shard_map/ppermute | solution.py:292
  51.4 9.2 %collective-permute-start.12 = (f32[2,2,4,5,8,128]{5,4,3,2,1,0:T(8,128)S(1)}, f32[2,2,4,5,8,128]{5,4,3,2,1,0:T(8,128)S(1)}, u32[]{:S(2)}, u32[]{:S(2)}) collective-permute-start(f32[2,2,4,5,8,128]{5,4,3,2,1,0:T(8,128)S(1)} %get-tuple-element.25), channel_id=1, source_target_pairs={{0,64},{64,0},{1,65},{65,1},{2,66},{66,2},{3,67},{67,3},{4,68},{68... | collective-permute-start | bytes 983048 | tf_op jit(solution)/shard_map/ppermute | solution.py:292
  51.4 10.4 %collective-permute-start.13 = (f32[2,2,4,5,8,128]{5,4,3,2,1,0:T(8,128)S(1)}, f32[2,2,4,5,8,128]{5,4,3,2,1,0:T(8,128)S(1)}, u32[]{:S(2)}, u32[]{:S(2)}) collective-permute-start(f32[2,2,4,5,8,128]{5,4,3,2,1,0:T(8,128)S(1)} %get-tuple-element.26), channel_id=1, source_target_pairs={{0,192},{64,128},{128,64},{192,0},{1,193},{65,129},{129,65},{193,1... | collective-permute-start | bytes 983048 | tf_op jit(solution)/shard_map/ppermute | solution.py:288
  61.9 8.4 %collective-permute-start.14 = (f32[2,2,4,5,8,128]{5,4,3,2,1,0:T(8,128)S(1)}, f32[2,2,4,5,8,128]{5,4,3,2,1,0:T(8,128)S(1)}, u32[]{:S(2)}, u32[]{:S(2)}) collective-permute-start(f32[2,2,4,5,8,128]{5,4,3,2,1,0:T(8,128)S(1)} %get-tuple-element.28), channel_id=1, source_target_pairs={{0,8},{8,0},{1,9},{9,1},{2,10},{10,2},{3,11},{11,3},{4,12},{12,4},... | collective-permute-start | bytes 983048 | tf_op jit(solution)/shard_map/ppermute | solution.py:292
  62.5 8.7 %collective-permute-start.17 = (f32[2,2,4,4,8,128]{5,4,3,2,1,0:T(8,128)S(1)}, f32[2,2,4,4,8,128]{5,4,3,2,1,0:T(8,128)S(1)}, u32[]{:S(2)}, u32[]{:S(2)}) collective-permute-start(f32[2,2,4,4,8,128]{5,4,3,2,1,0:T(8,128)S(1)} %get-tuple-element.34), channel_id=1, source_target_pairs={{0,4},{4,0},{1,5},{5,1},{2,6},{6,2},{3,7},{7,3},{8,12},{12,8},{9,1... | collective-permute-start | bytes 786440 | tf_op jit(solution)/shard_map/ppermute | solution.py:292
  63.9 7.6 %collective-permute-start.20 = (f32[2,2,4,4,8,128]{5,4,3,2,1,0:T(8,128)S(1)}, f32[2,2,4,4,8,128]{5,4,3,2,1,0:T(8,128)S(1)}, u32[]{:S(2)}, u32[]{:S(2)}) collective-permute-start(f32[2,2,4,4,8,128]{5,4,3,2,1,0:T(8,128)S(1)} %get-tuple-element.40), channel_id=1, source_target_pairs={{0,64},{64,0},{1,65},{65,1},{2,66},{66,2},{3,67},{67,3},{4,68},{68... | collective-permute-start | bytes 786440 | tf_op jit(solution)/shard_map/ppermute | solution.py:292
  70.4 5.4 %collective-permute-start.15 = (f32[2,4,5,8,128]{4,3,2,1,0:T(8,128)S(1)}, f32[2,4,5,8,128]{4,3,2,1,0:T(8,128)S(1)}, u32[]{:S(2)}, u32[]{:S(2)}) collective-permute-start(f32[2,4,5,8,128]{4,3,2,1,0:T(8,128)S(1)} %get-tuple-element.30), channel_id=1, source_target_pairs={{0,4},{4,0},{1,5},{5,1},{2,6},{6,2},{3,7},{7,3},{8,12},{12,8},{9,1... | collective-permute-start | bytes 491528 | tf_op jit(solution)/shard_map/ppermute | solution.py:292
  71.3 5.1 %collective-permute-start.18 = (f32[2,4,4,8,128]{4,3,2,1,0:T(8,128)S(1)}, f32[2,4,4,8,128]{4,3,2,1,0:T(8,128)S(1)}, u32[]{:S(2)}, u32[]{:S(2)}) collective-permute-start(f32[2,4,4,8,128]{4,3,2,1,0:T(8,128)S(1)} %get-tuple-element.36), channel_id=1, source_target_pairs={{0,64},{64,0},{1,65},{65,1},{2,66},{66,2},{3,67},{67,3},{4,68},{68... | collective-permute-start | bytes 393224 | tf_op jit(solution)/shard_map/ppermute | solution.py:292
  71.5 5.1 %collective-permute-start.21 = (f32[2,4,4,8,128]{4,3,2,1,0:T(8,128)S(1)}, f32[2,4,4,8,128]{4,3,2,1,0:T(8,128)S(1)}, u32[]{:S(2)}, u32[]{:S(2)}) collective-permute-start(f32[2,4,4,8,128]{4,3,2,1,0:T(8,128)S(1)} %get-tuple-element.42), channel_id=1, source_target_pairs={{0,8},{8,0},{1,9},{9,1},{2,10},{10,2},{3,11},{11,3},{4,12},{12,4},... | collective-permute-start | bytes 393224 | tf_op jit(solution)/shard_map/ppermute | solution.py:292

commit v7 on v4

--- a/solution.py
+++ b/solution.py
@@ -75,14 +75,48 @@
     )(pts, inv)
 
 
-def schur_kernel(counts_ref, tiles_ref, own_ref, oth_ref, c0_ref, c1_ref, c2_ref, c3_ref, *refs):
+def prepare_kernel(counts_ref, c0_ref, c1_ref, c2_ref, c3_ref, high_ref, low_ref, t_ref, t_high_ref, t_low_ref):
+    live = counts_ref[cluster_device()]
+    for k in range(SLOTS // CHUNK):
+
+        @pl.when(k * CHUNK < live)
+        def _():
+            for slot in range(k * CHUNK, (k + 1) * CHUNK):
+                for rel, ref in enumerate((c0_ref, c1_ref, c2_ref, c3_ref)):
+                    high, low = split(ref[slot])
+                    high_ref[slot, :, rel * W : (rel + 1) * W] = high
+                    low_ref[slot, :, rel * W : (rel + 1) * W] = low
+                panel_t = c0_ref[slot].T
+                t_ref[slot] = panel_t
+                t_high_ref[slot], t_low_ref[slot] = split(panel_t)
+
+
+def in_vmem(values):
+    return [pltpu.with_memory_space_constraint(v, pltpu.VMEM) for v in values]
+
+
+def prepare(counts, panels):
+    wide, square = (SLOTS, W, 4 * W), (SLOTS, W, W)
+    return pl.pallas_call(
+        prepare_kernel,
+        out_shape=[
+            jax.ShapeDtypeStruct(shape, kind)
+            for shape, kind in ((wide, BF16), (wide, BF16), (square, F32), (square, BF16), (square, BF16))
+        ],
+        in_specs=[SMEM] + [VMEM] * 4,
+        out_specs=[VMEM] * 5,
+        cost_estimate=pl.CostEstimate(flops=SLOTS * 20 * W * W, bytes_accessed=SLOTS * 12 * W * W * 4, transcendentals=0),
+        compiler_params=pltpu.CompilerParams(vmem_limit_bytes=8 << 20),
+        name="prepare",
+    )(counts, *in_vmem(panels))
+
+
+def schur_kernel(counts_ref, tiles_ref, own_ref, oth_ref, high_ref, low_ref, t_ref, t_high_ref, t_low_ref, *refs):
     outs, o_sems, accs = refs[:7], refs[7], refs[8:]
     core = lax.axis_index("c")
     cam = camera_index()
     device = cluster_device()
     live = counts_ref[device]
-    panels = (c0_ref, c1_ref, c2_ref, c3_ref)
-
     steps = SLOTS // CHUNK
     for acc in accs:
         acc[...] = jnp.zeros_like(acc)
@@ -93,22 +127,19 @@
             for i in range(CHUNK):
                 slot = k * CHUNK + i
                 m_high, m_low = split(jnp.where(core == k // 2, own_ref[slot % HALF], oth_ref[slot % HALF]))
-                panel_t = c0_ref[slot].T
-                t_high, t_low = split(panel_t)
+                t_high, t_low = t_high_ref[slot], t_low_ref[slot]
                 prod = jnp.dot(
                     jnp.concatenate([t_high, t_high, t_low], axis=1),
                     jnp.concatenate([m_high, m_low, m_high], axis=0),
                     preferred_element_type=F32,
                 )
-                rest = panel_t - prod
+                rest = t_ref[slot] - prod
                 if i:
                     rest = jnp.where(slot < live, rest, 0.0)
                 r_high, r_low = split(rest)
                 left = jnp.concatenate([r_high, r_high, r_low], axis=1)
-                parts = [split(panels[rel][slot]) for rel in range(4)]
-                highs = jnp.concatenate([h for h, _ in parts], axis=1)
-                lows = jnp.concatenate([l for _, l in parts], axis=1)
-                right = jnp.concatenate([highs, lows, highs], axis=0)
+                highs = high_ref[slot]
+                right = jnp.concatenate([highs, low_ref[slot], highs], axis=0)
                 rows = jnp.dot(left, right, preferred_element_type=F32)
                 row_tile = tiles_ref[cam, device * SLOTS + slot]
                 for rel in range(4):
@@ -140,14 +171,14 @@
         copy.wait()
 
 
-def schur(counts, tiles, own, oth, panels):
+def schur(counts, tiles, own, oth, ready):
     return pl.pallas_call(
         schur_kernel,
         out_shape=[
             jax.ShapeDtypeStruct(lead + (2, NXH, NZH, names[3], 8, W), F32) for k, names in enumerate(GROUPS)
             for lead in (((), (), (2,)) if k == 0 else ((2,), (2,)))
         ],
-        in_specs=[SMEM, SMEM] + [VMEM] * 6,
+        in_specs=[SMEM, SMEM] + [VMEM] * 7,
         out_specs=[ANY] * 7,
         scratch_shapes=[
             pltpu.SemaphoreType.DMA((7,)),
@@ -156,7 +187,7 @@
         cost_estimate=pl.CostEstimate(flops=SLOTS * 6 * 5 * W * W * W, bytes_accessed=SLOTS * 5 * W * W * 4, transcendentals=0),
         compiler_params=pltpu.CompilerParams(vmem_limit_bytes=12 << 20),
         name="schur",
-    )(counts, tiles, *[pltpu.with_memory_space_constraint(v, pltpu.VMEM) for v in (own, oth, *panels)])
+    )(counts, tiles, *in_vmem((own, oth, *ready)))
 
 
 def place_kernel(in_ref, out_ref):
@@ -233,16 +264,16 @@
     c0 = cam_jac
     c2 = swap(c0, "yh")
     c1 = swap(c0, "c")
-
     m_send = coupling(False, pts, inv)
     m_recv = swap(m_send, "c")
     m_keep = coupling(True, pts, inv)
     m_chip = m_keep + m_recv
-    m_own = m_chip + swap(m_chip, "yh")
+    m_recv = swap(m_chip, "yh")
+    c3 = swap(c2, "c")
+    ready = prepare(counts, (c0, c1, c2, c3))
+    m_own = m_chip + m_recv
     m_oth = swap(m_own, "c")
-    c3 = swap(c2, "c")
-
-    outs = schur(counts, tiles.T, m_own, m_oth, (c0, c1, c2, c3))
+    outs = schur(counts, tiles.T, m_own, m_oth, ready)
     near_z = swap(outs[3], "zl")
     near_y = swap(outs[5], "yl")
     low_x = swap(outs[0], "xl")

time: 99.5 us -> 109 us (1.095)
  waiting for transfers between devices: 42 us -> 51.5 us
  starting transfers between devices: 18.2 us -> 17 us
    ppermute x15, waiting for transfers between devices: 40.8 us -> 50.3 us  [swap(): return lax.ppermute(value, axis, [(0, 1), (1, 0)])]
    ppermute x15, starting transfers between devices: 15.5 us -> 14.3 us  [swap(): return lax.ppermute(value, axis, [(0, 1), (1, 0)])]
where the time goes in v7:
time: 109 us; the launch traced here: 108 us
  waiting for transfers between devices  51.5 us (47%)
  blocking collectives  23.1 us (21%)
  starting transfers between devices  17 us (16%)
  Pallas kernels  13.4 us (12%)
  local copies, waits for them, and re-layouts  2.79 us (3%)
    ppermute x15, waiting for transfers between devices, swap(): return lax.ppermute(value, axis, [(0, 1), (1, 0)])  50.3 us
    all_to_all x1, blocking collectives, on_device(): return place(lax.all_to_all(part, ('xh', 'zh'), 0, 0, tiled=True))  23.1 us
    ppermute x15, starting transfers between devices, swap(): return lax.ppermute(value, axis, [(0, 1), (1, 0)])  14.3 us
    pallas_call x2, Pallas kernels, coupling(): pl.pallas_call(kernel, out_shape=jax.ShapeDtypeStruct((HALF, W, W), F32),...  8.75 us
    unnamed x10, local copies, waits for them, and re-layouts  2.79 us
    ppermute x1, starting transfers between devices, swap_x_other(): lax.ppermute(value, ('xh', 'xl'), [(i, (i + 1 if i % 2 else i - 1) % size...  2.76 us
    pallas_call x1, Pallas kernels, schur(): pl.pallas_call(schur_kernel, out_shape=[jax.ShapeDtypeStruct(lead + (2, N...  2.75 us
  transfers between devices with their start and end apart: 16, of which 9 were waited for; matrix products, arithmetic and copies ran while one was open for 0% of the time, Pallas kernels for 9%

profile of v7, /device:TPU:16, one launch (start us, length us, event | category | flops | bytes accessed | tf_op | source)
XLA Modules:
  0.0 108.3 jit_solution(9341403526371277375)
XLA Ops:
  0.0 2.0 %collective-permute-start.4 = (f32[16,128,128]{2,1,0:T(8,128)}, f32[16,128,128]{2,1,0:T(8,128)S(1)}, u32[]{:S(2)}, u32[]{:S(2)}) collective-permute-start(f32[16,128,128]{2,1,0:T(8,128)} %c0_ref.1), channel_id=1, source_target_pairs={{0,2},{2,0},{1,3},{3,1},{4,6},{6,4},{5,7},{7,5},{8,10},{10,8},{9,1... | collective-permute-start | bytes 3145736 | tf_op jit(solution)/shard_map/ppermute | solution.py:257
  2.0 1.9 %copy-done = f32[16,128,3,128]{3,1,2,0:T(8,128)S(1)} copy-done((f32[16,128,3,128]{3,1,2,0:T(8,128)S(1)}, f32[16,128,3,128]{3,1,2,0:T(8,128)}, u32[]{:S(2)}) %copy-start) | copy-done | bytes 3145752
  3.9 0.9 copy-done.2
  4.8 4.4 %coupling.3 = f32[8,128,128]{2,1,0:T(8,128)S(1)} custom-call(f32[16,3,128,128]{3,2,1,0:T(8,128)S(1)} %bitcast.6, f32[3,3,16,128]{3,2,1,0:T(8,128)S(1)} %bitcast.8), custom_call_target="tpu_custom_call" | custom-call | flops 301989888 | bytes 2097152 | tf_op jit(solution)/shard_map/coupling/pallas_call | solution.py:66
  9.2 0.1 collective-permute-start
  9.3 0.5 collective-permute-start.3
  9.8 16.8 %collective-permute-done.4.c2_ref = f32[16,128,128]{2,1,0:T(8,128)S(1)} collective-permute-done((f32[16,128,128]{2,1,0:T(8,128)}, f32[16,128,128]{2,1,0:T(8,128)S(1)}, u32[]{:S(2)}, u32[]{:S(2)}) %collective-permute-start.4) | collective-permute-done | bytes 1048608 | tf_op jit(solution)/shard_map/ppermute | solution.py:257
  26.6 0.0 collective-permute-start.5
  26.6 4.4 %coupling.2 = f32[8,128,128]{2,1,0:T(8,128)S(1)} custom-call(f32[16,3,128,128]{3,2,1,0:T(8,128)S(1)} %bitcast.7, f32[3,3,16,128]{3,2,1,0:T(8,128)S(1)} %bitcast.9), custom_call_target="tpu_custom_call" | custom-call | flops 301989888 | bytes 2097152 | tf_op jit(solution)/shard_map/coupling/pallas_call | solution.py:66
  31.0 0.0 copy-start.4
  31.0 0.0 collective-permute-done
  31.0 0.1 add.15
  31.1 0.4 collective-permute-start.1
  31.5 15.6 %collective-permute-done.1 = f32[8,128,128]{2,1,0:T(8,128)S(1)} collective-permute-done((f32[8,128,128]{2,1,0:T(8,128)S(1)}, f32[8,128,128]{2,1,0:T(8,128)S(1)}, u32[]{:S(2)}, u32[]{:S(2)}) %collective-permute-start.1) | collective-permute-done | bytes 524320 | tf_op jit(solution)/shard_map/ppermute | solution.py:257
  47.0 0.1 add.16.own_ref
  47.1 0.0 copy-start.3
  47.1 0.1 collective-permute-start.2
  47.2 0.0 collective-permute-done.3.c1_ref
  47.2 0.0 collective-permute-done.5.c3_ref
  47.2 0.8 prepare.1
  48.1 1.0 collective-permute-done.2.oth_ref
  49.1 0.0 copy-done.3
  49.1 2.7 %schur.1 = (f32[2,2,4,5,8,128]{5,4,3,2,1,0:T(8,128)S(1)}, f32[2,2,4,5,8,128]{5,4,3,2,1,0:T(8,128)S(1)}, f32[2,2,2,4,5,8,128]{6,5,4,3,2,1,0:T(8,128)S(1)}, f32[2,...) custom-call(s32[64]{0:T(128)S(1)} %copy-done.4, ...), custom_call_target="tpu_custom_call" | custom-call | flops 1006632960 | bytes 5242880 | tf_op jit(solution)/shard_map/schur/pallas_call | solution.py:175
  51.8 2.0 %collective-permute-start.10 = (f32[2,2,2,4,4,8,128]{6,5,4,3,2,1,0:T(8,128)S(1)}, f32[2,2,2,4,4,8,128]{6,5,4,3,2,1,0:T(8,128)S(1)}, u32[]{:S(2)}, u32[]{:S(2)}) collective-permute-start(f32[2,2,2,4,4,8,128]{6,5,4,3,2,1,0:T(8,128)S(1)} %get-tuple-element.42), channel_id=1, source_target_pairs={{0,8},{8,0},{1,9},{9,1},{2,10},{10,2},{3,11},{11,3},{4,12},{12,4},... | collective-permute-start | bytes 1572872 | tf_op jit(solution)/shard_map/ppermute | solution.py:257
  53.8 4.3 %collective-permute-start.13 = (f32[2,2,2,4,4,8,128]{6,5,4,3,2,1,0:T(8,128)S(1)}, f32[2,2,2,4,4,8,128]{6,5,4,3,2,1,0:T(8,128)S(1)}, u32[]{:S(2)}, u32[]{:S(2)}) collective-permute-start(f32[2,2,2,4,4,8,128]{6,5,4,3,2,1,0:T(8,128)S(1)} %get-tuple-element.48), channel_id=1, source_target_pairs={{0,4},{4,0},{1,5},{5,1},{2,6},{6,2},{3,7},{7,3},{8,12},{12,8},{9,1... | collective-permute-start | bytes 1572872 | tf_op jit(solution)/shard_map/ppermute | solution.py:257
  58.1 0.0 collective-permute-start.6
  58.1 2.8 %collective-permute-start.7 = (f32[2,2,4,5,8,128]{5,4,3,2,1,0:T(8,128)S(1)}, f32[2,2,4,5,8,128]{5,4,3,2,1,0:T(8,128)S(1)}, u32[]{:S(2)}, u32[]{:S(2)}) collective-permute-start(f32[2,2,4,5,8,128]{5,4,3,2,1,0:T(8,128)S(1)} %get-tuple-element.36), channel_id=1, source_target_pairs={{0,192},{64,128},{128,64},{192,0},{1,193},{65,129},{129,65},{193,1... | collective-permute-start | bytes 983048 | tf_op jit(solution)/shard_map/ppermute | solution.py:253
  60.9 6.6 %collective-permute-done.6.refs_1_ = f32[2,2,4,5,8,128]{5,4,3,2,1,0:T(8,128)S(1)} collective-permute-done((f32[2,2,4,5,8,128]{5,4,3,2,1,0:T(8,128)S(1)}, f32[2,2,4,5,8,128]{5,4,3,2,1,0:T(8,128)S(1)}, u32[]{:S(2)}, u32[]{:S(2)}) %collective-permute-start.6) | collective-permute-done | bytes 327712 | tf_op jit(solution)/shard_map/ppermute | solution.py:257
  67.4 1.2 %collective-permute-done.7.refs_2_ = f32[2,2,4,5,8,128]{5,4,3,2,1,0:T(8,128)S(1)} collective-permute-done((f32[2,2,4,5,8,128]{5,4,3,2,1,0:T(8,128)S(1)}, f32[2,2,4,5,8,128]{5,4,3,2,1,0:T(8,128)S(1)}, u32[]{:S(2)}, u32[]{:S(2)}) %collective-permute-start.7) | collective-permute-done | bytes 327712 | tf_op jit(solution)/shard_map/ppermute | solution.py:253
  68.7 0.1 halve.6
  68.8 0.5 collective-permute-start.8
  69.2 0.0 collective-permute-done.10.refs_1_
  69.2 0.1 halve.8
  69.3 1.3 %collective-permute-start.11 = (f32[2,2,4,4,8,128]{5,4,3,2,1,0:T(8,128)S(1)}, f32[2,2,4,4,8,128]{5,4,3,2,1,0:T(8,128)S(1)}, u32[]{:S(2)}, u32[]{:S(2)}) collective-permute-start(f32[2,2,4,4,8,128]{5,4,3,2,1,0:T(8,128)S(1)} %get-tuple-element.44), channel_id=1, source_target_pairs={{0,4},{4,0},{1,5},{5,1},{2,6},{6,2},{3,7},{7,3},{8,12},{12,8},{9,1... | collective-permute-start | bytes 786440 | tf_op jit(solution)/shard_map/ppermute | solution.py:257
  70.7 0.0 collective-permute-done.13.refs_1_
  70.7 0.1 halve.10
  70.7 0.5 collective-permute-start.14
  71.3 6.1 %collective-permute-done.8.refs_1_ = f32[2,2,4,5,8,128]{5,4,3,2,1,0:T(8,128)S(1)} collective-permute-done((f32[2,2,4,5,8,128]{5,4,3,2,1,0:T(8,128)S(1)}, f32[2,2,4,5,8,128]{5,4,3,2,1,0:T(8,128)S(1)}, u32[]{:S(2)}, u32[]{:S(2)}) %collective-permute-start.8) | collective-permute-done | bytes 327712 | tf_op jit(solution)/shard_map/ppermute | solution.py:257
  77.4 1.2 %collective-permute-start.9 = (f32[2,4,5,8,128]{4,3,2,1,0:T(8,128)S(1)}, f32[2,4,5,8,128]{4,3,2,1,0:T(8,128)S(1)}, u32[]{:S(2)}, u32[]{:S(2)}) collective-permute-start(f32[2,4,5,8,128]{4,3,2,1,0:T(8,128)S(1)} %get-tuple-element.40), channel_id=1, source_target_pairs={{0,4},{4,0},{1,5},{5,1},{2,6},{6,2},{3,7},{7,3},{8,12},{12,8},{9,1... | collective-permute-start | bytes 491528 | tf_op jit(solution)/shard_map/ppermute | solution.py:257
  78.6 0.0 collective-permute-done.11.refs_1_
  78.6 0.7 collective-permute-start.12
  79.3 0.0 collective-permute-done.14.refs_1_
  79.4 0.7 collective-permute-start.15
  80.1 2.7 %collective-permute-done.9 = f32[2,4,5,8,128]{4,3,2,1,0:T(8,128)S(1)} collective-permute-done((f32[2,4,5,8,128]{4,3,2,1,0:T(8,128)S(1)}, f32[2,4,5,8,128]{4,3,2,1,0:T(8,128)S(1)}, u32[]{:S(2)}, u32[]{:S(2)}) %collective-permute-start.9) | collective-permute-done | bytes 163872 | tf_op jit(solution)/shard_map/ppermute | solution.py:257
  82.8 0.9 collective-permute-done.12
  83.7 0.7 collective-permute-done.15
  84.5 23.1 %all_to_all.5.in_ref = f32[8,13,8,128]{3,2,1,0:T(8,128)S(1)} all-to-all(f32[8,13,8,128]{3,2,1,0:T(8,128)S(1)} %pad_maximum_fusion), channel_id=1, replica_groups=mesh['xh'=2,'xl'=2,'zh'=4,'zl'=2,'yl'=2,'yh'=2,'c'=2] {'xh','zh'}, dimensions={0} | all-to-all | bytes 851968 | tf_op jit(solution)/shard_map/all_to_all | solution.py:294
  107.6 0.7 place.1
  (12 shorter events, 0.2 us)
Async XLA Ops:
  0.0 26.6 %collective-permute-start.4 = (f32[16,128,128]{2,1,0:T(8,128)}, f32[16,128,128]{2,1,0:T(8,128)S(1)}, u32[]{:S(2)}, u32[]{:S(2)}) collective-permute-start(f32[16,128,128]{2,1,0:T(8,128)} %c0_ref.1), channel_id=1, source_target_pairs={{0,2},{2,0},{1,3},{3,1},{4,6},{6,4},{5,7},{7,5},{8,10},{10,8},{9,1... | collective-permute-start | bytes 3145736 | tf_op jit(solution)/shard_map/ppermute | solution.py:257
  2.0 1.9 %copy-start = (f32[16,128,3,128]{3,1,2,0:T(8,128)S(1)}, f32[16,128,3,128]{3,1,2,0:T(8,128)}, u32[]{:S(2)}) copy-start(f32[16,128,3,128]{3,1,2,0:T(8,128)} %param.8) | copy-start | bytes 9437188
  3.9 0.9 copy-start.2
  4.8 4.5 %copy-start.1 = (f32[16,128,128]{2,1,0:T(8,128)S(1)}, f32[16,128,128]{2,1,0:T(8,128)}, u32[]{:S(2)}) copy-start(f32[16,128,128]{2,1,0:T(8,128)} %c0_ref.1) | copy-start | bytes 3145732
  9.2 21.8 %collective-permute-start = (f32[8,128,128]{2,1,0:T(8,128)S(1)}, f32[8,128,128]{2,1,0:T(8,128)S(1)}, u32[]{:S(2)}, u32[]{:S(2)}) collective-permute-start(f32[8,128,128]{2,1,0:T(8,128)S(1)} %coupling.3), channel_id=1, source_target_pairs={{0,1},{1,0},{2,3},{3,2},{4,5},{5,4},{6,7},{7,6},{8,9},{9,8},{10,11... | collective-permute-start | bytes 1572872 | tf_op jit(solution)/shard_map/ppermute | solution.py:257
  9.3 37.9 %collective-permute-start.3 = (f32[16,128,128]{2,1,0:T(8,128)S(1)}, f32[16,128,128]{2,1,0:T(8,128)S(1)}, u32[]{:S(2)}, u32[]{:S(2)}) collective-permute-start(f32[16,128,128]{2,1,0:T(8,128)S(1)} %copy-done.1), channel_id=1, source_target_pairs={{0,1},{1,0},{2,3},{3,2},{4,5},{5,4},{6,7},{7,6},{8,9},{9,8},{10,11... | collective-permute-start | bytes 3145736 | tf_op jit(solution)/shard_map/ppermute | solution.py:257
  26.6 20.6 %collective-permute-start.5 = (f32[16,128,128]{2,1,0:T(8,128)S(1)}, f32[16,128,128]{2,1,0:T(8,128)S(1)}, u32[]{:S(2)}, u32[]{:S(2)}) collective-permute-start(f32[16,128,128]{2,1,0:T(8,128)S(1)} %collective-permute-done.4.c2_ref), channel_id=1, source_target_pairs={{0,1},{1,0},{2,3},{3,2},{4,5},{5,4},{6,7},{7,6},{8,9},{9,8},{10,11... | collective-permute-start | bytes 3145736 | tf_op jit(solution)/shard_map/ppermute | solution.py:257
  31.0 16.2 %copy-start.4 = (s32[64]{0:T(128)S(1)}, s32[64]{0:T(128)}, u32[]{:S(2)}) copy-start(s32[64]{0:T(128)} %counts_ref.3) | copy-start | bytes 772
  31.1 15.9 %collective-permute-start.1 = (f32[8,128,128]{2,1,0:T(8,128)S(1)}, f32[8,128,128]{2,1,0:T(8,128)S(1)}, u32[]{:S(2)}, u32[]{:S(2)}) collective-permute-start(f32[8,128,128]{2,1,0:T(8,128)S(1)} %add.15), channel_id=1, source_target_pairs={{0,2},{2,0},{1,3},{3,1},{4,6},{6,4},{5,7},{7,5},{8,10},{10,8},{9,1... | collective-permute-start | bytes 1572872 | tf_op jit(solution)/shard_map/ppermute | solution.py:257
  47.1 2.0 %copy-start.3 = (s32[1024,4]{0,1:T(4,128)S(1)}, s32[1024,4]{0,1:T(4,128)}, u32[]{:S(2)}) copy-start(s32[1024,4]{0,1:T(4,128)} %param.6) | copy-start | bytes 49156
  47.1 2.0 %collective-permute-start.2 = (f32[8,128,128]{2,1,0:T(8,128)S(1)}, f32[8,128,128]{2,1,0:T(8,128)S(1)}, u32[]{:S(2)}, u32[]{:S(2)}) collective-permute-start(f32[8,128,128]{2,1,0:T(8,128)S(1)} %add.16.own_ref), channel_id=1, source_target_pairs={{0,1},{1,0},{2,3},{3,2},{4,5},{5,4},{6,7},{7,6},{8,9},{9,8},{10,11... | collective-permute-start | bytes 1572872 | tf_op jit(solution)/shard_map/ppermute | solution.py:257
  51.8 17.4 %collective-permute-start.10 = (f32[2,2,2,4,4,8,128]{6,5,4,3,2,1,0:T(8,128)S(1)}, f32[2,2,2,4,4,8,128]{6,5,4,3,2,1,0:T(8,128)S(1)}, u32[]{:S(2)}, u32[]{:S(2)}) collective-permute-start(f32[2,2,2,4,4,8,128]{6,5,4,3,2,1,0:T(8,128)S(1)} %get-tuple-element.42), channel_id=1, source_target_pairs={{0,8},{8,0},{1,9},{9,1},{2,10},{10,2},{3,11},{11,3},{4,12},{12,4},... | collective-permute-start | bytes 1572872 | tf_op jit(solution)/shard_map/ppermute | solution.py:257
  53.8 16.8 %collective-permute-start.13 = (f32[2,2,2,4,4,8,128]{6,5,4,3,2,1,0:T(8,128)S(1)}, f32[2,2,2,4,4,8,128]{6,5,4,3,2,1,0:T(8,128)S(1)}, u32[]{:S(2)}, u32[]{:S(2)}) collective-permute-start(f32[2,2,2,4,4,8,128]{6,5,4,3,2,1,0:T(8,128)S(1)} %get-tuple-element.48), channel_id=1, source_target_pairs={{0,4},{4,0},{1,5},{5,1},{2,6},{6,2},{3,7},{7,3},{8,12},{12,8},{9,1... | collective-permute-start | bytes 1572872 | tf_op jit(solution)/shard_map/ppermute | solution.py:257
  58.1 9.3 %collective-permute-start.6 = (f32[2,2,4,5,8,128]{5,4,3,2,1,0:T(8,128)S(1)}, f32[2,2,4,5,8,128]{5,4,3,2,1,0:T(8,128)S(1)}, u32[]{:S(2)}, u32[]{:S(2)}) collective-permute-start(f32[2,2,4,5,8,128]{5,4,3,2,1,0:T(8,128)S(1)} %get-tuple-element.35), channel_id=1, source_target_pairs={{0,64},{64,0},{1,65},{65,1},{2,66},{66,2},{3,67},{67,3},{4,68},{68... | collective-permute-start | bytes 983048 | tf_op jit(solution)/shard_map/ppermute | solution.py:257
  58.1 10.5 %collective-permute-start.7 = (f32[2,2,4,5,8,128]{5,4,3,2,1,0:T(8,128)S(1)}, f32[2,2,4,5,8,128]{5,4,3,2,1,0:T(8,128)S(1)}, u32[]{:S(2)}, u32[]{:S(2)}) collective-permute-start(f32[2,2,4,5,8,128]{5,4,3,2,1,0:T(8,128)S(1)} %get-tuple-element.36), channel_id=1, source_target_pairs={{0,192},{64,128},{128,64},{192,0},{1,193},{65,129},{129,65},{193,1... | collective-permute-start | bytes 983048 | tf_op jit(solution)/shard_map/ppermute | solution.py:253
  68.8 8.6 %collective-permute-start.8 = (f32[2,2,4,5,8,128]{5,4,3,2,1,0:T(8,128)S(1)}, f32[2,2,4,5,8,128]{5,4,3,2,1,0:T(8,128)S(1)}, u32[]{:S(2)}, u32[]{:S(2)}) collective-permute-start(f32[2,2,4,5,8,128]{5,4,3,2,1,0:T(8,128)S(1)} %get-tuple-element.38), channel_id=1, source_target_pairs={{0,8},{8,0},{1,9},{9,1},{2,10},{10,2},{3,11},{11,3},{4,12},{12,4},... | collective-permute-start | bytes 983048 | tf_op jit(solution)/shard_map/ppermute | solution.py:257
  69.3 9.3 %collective-permute-start.11 = (f32[2,2,4,4,8,128]{5,4,3,2,1,0:T(8,128)S(1)}, f32[2,2,4,4,8,128]{5,4,3,2,1,0:T(8,128)S(1)}, u32[]{:S(2)}, u32[]{:S(2)}) collective-permute-start(f32[2,2,4,4,8,128]{5,4,3,2,1,0:T(8,128)S(1)} %get-tuple-element.44), channel_id=1, source_target_pairs={{0,4},{4,0},{1,5},{5,1},{2,6},{6,2},{3,7},{7,3},{8,12},{12,8},{9,1... | collective-permute-start | bytes 786440 | tf_op jit(solution)/shard_map/ppermute | solution.py:257
  70.7 8.6 %collective-permute-start.14 = (f32[2,2,4,4,8,128]{5,4,3,2,1,0:T(8,128)S(1)}, f32[2,2,4,4,8,128]{5,4,3,2,1,0:T(8,128)S(1)}, u32[]{:S(2)}, u32[]{:S(2)}) collective-permute-start(f32[2,2,4,4,8,128]{5,4,3,2,1,0:T(8,128)S(1)} %get-tuple-element.50), channel_id=1, source_target_pairs={{0,64},{64,0},{1,65},{65,1},{2,66},{66,2},{3,67},{67,3},{4,68},{68... | collective-permute-start | bytes 786440 | tf_op jit(solution)/shard_map/ppermute | solution.py:257
  77.4 5.4 %collective-permute-start.9 = (f32[2,4,5,8,128]{4,3,2,1,0:T(8,128)S(1)}, f32[2,4,5,8,128]{4,3,2,1,0:T(8,128)S(1)}, u32[]{:S(2)}, u32[]{:S(2)}) collective-permute-start(f32[2,4,5,8,128]{4,3,2,1,0:T(8,128)S(1)} %get-tuple-element.40), channel_id=1, source_target_pairs={{0,4},{4,0},{1,5},{5,1},{2,6},{6,2},{3,7},{7,3},{8,12},{12,8},{9,1... | collective-permute-start | bytes 491528 | tf_op jit(solution)/shard_map/ppermute | solution.py:257
  78.6 5.1 %collective-permute-start.12 = (f32[2,4,4,8,128]{4,3,2,1,0:T(8,128)S(1)}, f32[2,4,4,8,128]{4,3,2,1,0:T(8,128)S(1)}, u32[]{:S(2)}, u32[]{:S(2)}) collective-permute-start(f32[2,4,4,8,128]{4,3,2,1,0:T(8,128)S(1)} %get-tuple-element.46), channel_id=1, source_target_pairs={{0,64},{64,0},{1,65},{65,1},{2,66},{66,2},{3,67},{67,3},{4,68},{68... | collective-permute-start | bytes 393224 | tf_op jit(solution)/shard_map/ppermute | solution.py:257
  79.4 5.1 %collective-permute-start.15 = (f32[2,4,4,8,128]{4,3,2,1,0:T(8,128)S(1)}, f32[2,4,4,8,128]{4,3,2,1,0:T(8,128)S(1)}, u32[]{:S(2)}, u32[]{:S(2)}) collective-permute-start(f32[2,4,4,8,128]{4,3,2,1,0:T(8,128)S(1)} %get-tuple-element.52), channel_id=1, source_target_pairs={{0,8},{8,0},{1,9},{9,1},{2,10},{10,2},{3,11},{11,3},{4,12},{12,4},... | collective-permute-start | bytes 393224 | tf_op jit(solution)/shard_map/ppermute | solution.py:257

commit v8 on v7

--- a/solution.py
+++ b/solution.py
@@ -10,9 +10,10 @@
 SLOTS = 16
 HALF = SLOTS // 2
 CHUNK = 4
+PACKED = 3 * W // 4
 GT = 4
 NXH, NXL, NZH, NZL, NYL = 2, 2, 4, 2, 2
-GROUPS = (("xl", "zl", "yl", GT + 1), ("zl", "yl", "xl", GT), ("yl", "xl", "zl", GT))
+GROUPS = (("xl", "zl", "yl", GT + 1), ("zl", "yl", "xl", GT + 1), ("yl", "xl", "zl", GT - 1))
 F32 = jnp.float32
 BF16 = jnp.bfloat16
 ANY = pl.BlockSpec(memory_space=pl.ANY)
@@ -56,7 +57,10 @@
             pairs.append((split(weighted), split(pts[k])))
         left = jnp.concatenate([w[0] for w, _ in pairs] + [w[0] for w, _ in pairs] + [w[1] for w, _ in pairs], axis=1)
         right = jnp.concatenate([p[0] for _, p in pairs] + [p[1] for _, p in pairs] + [p[0] for _, p in pairs], axis=1)
-        out_ref[i] = lax.dot_general(left, right, (((1,), (1,)), ((), ())), preferred_element_type=F32)
+        full = lax.dot_general(left, right, (((1,), (1,)), ((), ())), preferred_element_type=F32)
+        out_ref[i, : W // 2] = full[: W // 2]
+        out_ref[i, W // 2 :, : W // 2] = full[W // 2 : PACKED, W // 2 :]
+        out_ref[i, W // 2 :, W // 2 :] = full[PACKED:, W // 2 :]
 
 
 def coupling(mine, pts, inv):
@@ -65,7 +69,7 @@
 
     return pl.pallas_call(
         kernel,
-        out_shape=jax.ShapeDtypeStruct((HALF, W, W), F32),
+        out_shape=jax.ShapeDtypeStruct((HALF, PACKED, W), F32),
         in_specs=[HBM, VMEM],
         out_specs=VMEM,
         scratch_shapes=[pltpu.VMEM((HALF, 3, W, W), F32), pltpu.SemaphoreType.DMA((HALF,))],
@@ -112,7 +116,7 @@
 
 
 def schur_kernel(counts_ref, tiles_ref, own_ref, oth_ref, high_ref, low_ref, t_ref, t_high_ref, t_low_ref, *refs):
-    outs, o_sems, accs = refs[:7], refs[7], refs[8:]
+    outs, o_sems, accs = refs[:8], refs[8], refs[9:]
     core = lax.axis_index("c")
     cam = camera_index()
     device = cluster_device()
@@ -126,7 +130,11 @@
         def _():
             for i in range(CHUNK):
                 slot = k * CHUNK + i
-                m_high, m_low = split(jnp.where(core == k // 2, own_ref[slot % HALF], oth_ref[slot % HALF]))
+                packed = jnp.where(core == k // 2, own_ref[slot % HALF], oth_ref[slot % HALF])
+                top, rest = packed[: W // 2], packed[W // 2 :]
+                corner = jnp.concatenate([rest[:, : W // 2], rest[:, W // 2 :]], axis=0)
+                bottom = jnp.concatenate([top[:, W // 2 :].T, corner], axis=1)
+                m_high, m_low = split(jnp.concatenate([top, bottom], axis=0))
                 t_high, t_low = t_high_ref[slot], t_low_ref[slot]
                 prod = jnp.dot(
                     jnp.concatenate([t_high, t_high, t_low], axis=1),
@@ -156,13 +164,18 @@
                         add(0, GT)
                         continue
                     tile = tiles_ref[lax.bitwise_xor(cam, rel), device * SLOTS + slot]
-                    add(rel - 1, tile)
+                    if rel < 3:
+                        add(rel - 1, tile)
+                        continue
+                    last = tile == GT - 1
+                    add(1, GT, jnp.where(last, block, 0.0))
+                    add(2, jnp.minimum(tile, GT - 2), jnp.where(last, 0.0, block))
 
     copies = []
     for group, names in enumerate(GROUPS):
         bit = lax.axis_index(names[0])
         away = accs[group].at[1 - bit]
-        copies += [away.at[0], away.at[1]] if group == 0 else [away]
+        copies += [away.at[0], away.at[1]] if group < 2 else [away]
         copies.append(accs[group].at[bit])
     copies = [pltpu.make_async_copy(source, outs[k], o_sems.at[k]) for k, source in enumerate(copies)]
     for copy in copies:
@@ -176,12 +189,12 @@
         schur_kernel,
         out_shape=[
             jax.ShapeDtypeStruct(lead + (2, NXH, NZH, names[3], 8, W), F32) for k, names in enumerate(GROUPS)
-            for lead in (((), (), (2,)) if k == 0 else ((2,), (2,)))
+            for lead in (((), (), (2,)) if k < 2 else ((2,), (2,)))
         ],
         in_specs=[SMEM, SMEM] + [VMEM] * 7,
-        out_specs=[ANY] * 7,
+        out_specs=[ANY] * 8,
         scratch_shapes=[
-            pltpu.SemaphoreType.DMA((7,)),
+            pltpu.SemaphoreType.DMA((8,)),
         ]
         + [pltpu.VMEM((2, 2, 2, NXH, NZH, names[3], 8, W), F32) for names in GROUPS],
         cost_estimate=pl.CostEstimate(flops=SLOTS * 6 * 5 * W * W * W, bytes_accessed=SLOTS * 5 * W * W * 4, transcendentals=0),
@@ -202,7 +215,7 @@
         return value
 
     row = 0
-    for rel, t in [(1, t) for t in range(GT)] + [(0, x)] + [(rel, t) for rel in (2, 3) for t in range(GT)]:
+    for rel, t in [(1, t) for t in range(GT)] + [(0, x)] + [(2, t) for t in range(GT)] + [(3, (t - 1) % GT) for t in range(GT)]:
         column = lax.bitwise_xor(cam, rel) * GT + t
         out_ref[0, :, pl.ds(pl.multiple_of(column * W, W), W)] = total(row)
         row += 1
@@ -248,9 +261,8 @@
     )(*[pltpu.with_memory_space_constraint(v, pltpu.VMEM) for v in (keep, *parts)])
 
 
-def swap_x_other(value):
-    size = NXH * NXL
-    return lax.ppermute(value, ("xh", "xl"), [(i, (i + 1 if i % 2 else i - 1) % size) for i in range(size)])
+def swap_other(value, high, low, size):
+    return lax.ppermute(value, (high, low), [(i, (i + 1 if i % 2 else i - 1) % size) for i in range(size)])
 
 
 def swap(value, axis):
@@ -274,11 +286,12 @@
     m_own = m_chip + m_recv
     m_oth = swap(m_own, "c")
     outs = schur(counts, tiles.T, m_own, m_oth, ready)
-    near_z = swap(outs[3], "zl")
-    near_y = swap(outs[5], "yl")
+    near_y = swap(outs[6], "yl")
+    low_z = swap(outs[3], "zl")
     low_x = swap(outs[0], "xl")
-    high_x = swap_x_other(outs[1])
-    groups = [(outs[2], (low_x, high_x)), (outs[4], (near_z,)), (outs[6], (near_y,))]
+    high_z = swap_other(outs[4], "zh", "zl", NZH * NZL)
+    high_x = swap_other(outs[1], "xh", "xl", NXH * NXL)
+    groups = [(outs[2], (low_x, high_x)), (outs[5], (low_z, high_z)), (outs[7], (near_y,))]
     for phase in (1, 2):
         halves = []
         for k, (keep, parts) in enumerate(groups):

time: 109 us -> 108 us (level)
  starting transfers between devices: 17 us -> 23.9 us
  waiting for transfers between devices: 51.5 us -> 46.5 us
  blocking collectives: 23.1 us -> 18.6 us
  Pallas kernels: 13.4 us -> 15.3 us
    ppermute x15, waiting for transfers between devices: 50.3 us -> 42.3 us  [swap(): return lax.ppermute(value, axis, [(0, 1), (1, 0)])]
    ppermute x1 -> x2, starting transfers between devices: 2.76 us -> 10.6 us  [swap_other(): lax.ppermute(value, (high, low), [(i, (i + 1 if i % 2 else i - 1) % size)...]
    all_to_all x1, blocking collectives: 23.1 us -> 18.6 us  [on_device(): return place(lax.all_to_all(part, ('xh', 'zh'), 0, 0, tiled=True))]
    ppermute x1 -> x2, waiting for transfers between devices: 1.21 us -> 4.17 us  [swap_other(): lax.ppermute(value, (high, low), [(i, (i + 1 if i % 2 else i - 1) % size)...]
  transfers between devices with their start and end apart: 16 -> 17, of which waited for: 9 -> 7; matrix products, arithmetic and copies ran while one was open for 0% -> 0% of each run, Pallas kernels for 9% -> 10%
where the time goes in v8:
time: 108 us
  waiting for transfers between devices  46.5 us (43%)
  starting transfers between devices  23.9 us (22%)
  blocking collectives  18.6 us (17%)
  Pallas kernels  15.3 us (14%)
  local copies, waits for them, and re-layouts  2.79 us (3%)
    ppermute x15, waiting for transfers between devices, swap(): return lax.ppermute(value, axis, [(0, 1), (1, 0)])  42.3 us
    all_to_all x1, blocking collectives, on_device(): return place(lax.all_to_all(part, ('xh', 'zh'), 0, 0, tiled=True))  18.6 us
    ppermute x15, starting transfers between devices, swap(): return lax.ppermute(value, axis, [(0, 1), (1, 0)])  13.4 us
    ppermute x2, starting transfers between devices, swap_other(): lax.ppermute(value, (high, low), [(i, (i + 1 if i % 2 else i - 1) % size)...  10.6 us
    pallas_call x2, Pallas kernels, coupling(): pl.pallas_call(kernel, out_shape=jax.ShapeDtypeStruct((HALF, PACKED, W),...  9.72 us
    ppermute x2, waiting for transfers between devices, swap_other(): lax.ppermute(value, (high, low), [(i, (i + 1 if i % 2 else i - 1) % size)...  4.17 us
    pallas_call x1, Pallas kernels, schur(): pl.pallas_call(schur_kernel, out_shape=[jax.ShapeDtypeStruct(lead + (2, N...  3.7 us
    unnamed x10, local copies, waits for them, and re-layouts  2.79 us
  transfers between devices with their start and end apart: 17, of which 7 were waited for; matrix products, arithmetic and copies ran while one was open for 0% of the time, Pallas kernels for 10%

profile of v8, /device:TPU:16, one launch (start us, length us, event | category | flops | bytes accessed | tf_op | source)
XLA Modules:
  0.0 107.6 jit_solution(16488637915162193799)
XLA Ops:
  0.0 2.0 %collective-permute-start.4 = (f32[16,128,128]{2,1,0:T(8,128)}, f32[16,128,128]{2,1,0:T(8,128)S(1)}, u32[]{:S(2)}, u32[]{:S(2)}) collective-permute-start(f32[16,128,128]{2,1,0:T(8,128)} %c0_ref.1), channel_id=1, source_target_pairs={{0,2},{2,0},{1,3},{3,1},{4,6},{6,4},{5,7},{7,5},{8,10},{10,8},{9,1... | collective-permute-start | bytes 3145736 | tf_op jit(solution)/shard_map/ppermute | solution.py:269
  2.0 1.9 %copy-done = f32[16,128,3,128]{3,1,2,0:T(8,128)S(1)} copy-done((f32[16,128,3,128]{3,1,2,0:T(8,128)S(1)}, f32[16,128,3,128]{3,1,2,0:T(8,128)}, u32[]{:S(2)}) %copy-start) | copy-done | bytes 3145752
  3.9 0.9 copy-done.2
  4.8 4.9 %coupling.3 = f32[8,96,128]{2,1,0:T(8,128)S(1)} custom-call(f32[16,3,128,128]{3,2,1,0:T(8,128)S(1)} %bitcast.6, f32[3,3,16,128]{3,2,1,0:T(8,128)S(1)} %bitcast.8), custom_call_target="tpu_custom_call" | custom-call | flops 301989888 | bytes 2097152 | tf_op jit(solution)/shard_map/coupling/pallas_call | solution.py:70
  9.7 0.0 copy-start.4
  9.7 0.1 collective-permute-start
  9.8 0.5 collective-permute-start.3
  10.3 16.3 %collective-permute-done.4.c2_ref = f32[16,128,128]{2,1,0:T(8,128)S(1)} collective-permute-done((f32[16,128,128]{2,1,0:T(8,128)}, f32[16,128,128]{2,1,0:T(8,128)S(1)}, u32[]{:S(2)}, u32[]{:S(2)}) %collective-permute-start.4) | collective-permute-done | bytes 1048608 | tf_op jit(solution)/shard_map/ppermute | solution.py:269
  26.6 0.0 collective-permute-start.5
  26.6 4.9 %coupling.2 = f32[8,96,128]{2,1,0:T(8,128)S(1)} custom-call(f32[16,3,128,128]{3,2,1,0:T(8,128)S(1)} %bitcast.7, f32[3,3,16,128]{3,2,1,0:T(8,128)S(1)} %bitcast.9), custom_call_target="tpu_custom_call" | custom-call | flops 301989888 | bytes 2097152 | tf_op jit(solution)/shard_map/coupling/pallas_call | solution.py:70
  31.5 0.0 collective-permute-done
  31.5 0.4 collective-permute-start.1
  31.9 12.7 %collective-permute-done.1 = f32[8,96,128]{2,1,0:T(8,128)S(1)} collective-permute-done((f32[8,96,128]{2,1,0:T(8,128)S(1)}, f32[8,96,128]{2,1,0:T(8,128)S(1)}, u32[]{:S(2)}, u32[]{:S(2)}) %collective-permute-start.1) | collective-permute-done | bytes 393248 | tf_op jit(solution)/shard_map/ppermute | solution.py:269
  44.7 0.0 copy-start.3
  44.7 0.1 collective-permute-start.2
  44.8 0.0 collective-permute-done.3.c1_ref
  44.8 0.0 collective-permute-done.5.c3_ref
  44.9 0.8 prepare.1
  45.7 0.8 collective-permute-done.2.oth_ref
  46.5 3.7 %schur.1 = (f32[2,2,4,5,8,128]{5,4,3,2,1,0:T(8,128)S(1)}, f32[2,2,4,5,8,128]{5,4,3,2,1,0:T(8,128)S(1)}, f32[2,2,2,4,5,8,128]{6,5,4,3,2,1,0:T(8,128)S(1)}, f32[2,...) custom-call(s32[64]{0:T(128)S(1)} %copy-done.4, ...), custom_call_target="tpu_custom_call" | custom-call | flops 1006632960 | bytes 5242880 | tf_op jit(solution)/shard_map/schur/pallas_call | solution.py:188
  50.2 1.6 %collective-permute-start.6 = (f32[2,2,4,5,8,128]{5,4,3,2,1,0:T(8,128)S(1)}, f32[2,2,4,5,8,128]{5,4,3,2,1,0:T(8,128)S(1)}, u32[]{:S(2)}, u32[]{:S(2)}) collective-permute-start(f32[2,2,4,5,8,128]{5,4,3,2,1,0:T(8,128)S(1)} %get-tuple-element.36), channel_id=1, source_target_pairs={{0,64},{64,0},{1,65},{65,1},{2,66},{66,2},{3,67},{67,3},{4,68},{68... | collective-permute-start | bytes 983048 | tf_op jit(solution)/shard_map/ppermute | solution.py:269
  51.8 5.6 %collective-permute-start.7 = (f32[2,2,4,5,8,128]{5,4,3,2,1,0:T(8,128)S(1)}, f32[2,2,4,5,8,128]{5,4,3,2,1,0:T(8,128)S(1)}, u32[]{:S(2)}, u32[]{:S(2)}) collective-permute-start(f32[2,2,4,5,8,128]{5,4,3,2,1,0:T(8,128)S(1)} %get-tuple-element.37), channel_id=1, source_target_pairs={{0,192},{64,128},{128,64},{192,0},{1,193},{65,129},{129,65},{193,1... | collective-permute-start | bytes 983048 | tf_op jit(solution)/shard_map/ppermute | solution.py:265
  57.4 1.9 %collective-permute-start.10 = (f32[2,2,4,5,8,128]{5,4,3,2,1,0:T(8,128)S(1)}, f32[2,2,4,5,8,128]{5,4,3,2,1,0:T(8,128)S(1)}, u32[]{:S(2)}, u32[]{:S(2)}) collective-permute-start(f32[2,2,4,5,8,128]{5,4,3,2,1,0:T(8,128)S(1)} %get-tuple-element.43), channel_id=1, source_target_pairs={{0,8},{8,0},{1,9},{9,1},{2,10},{10,2},{3,11},{11,3},{4,12},{12,4},... | collective-permute-start | bytes 983048 | tf_op jit(solution)/shard_map/ppermute | solution.py:269
  59.3 5.0 %collective-permute-start.11 = (f32[2,2,4,5,8,128]{5,4,3,2,1,0:T(8,128)S(1)}, f32[2,2,4,5,8,128]{5,4,3,2,1,0:T(8,128)S(1)}, u32[]{:S(2)}, u32[]{:S(2)}) collective-permute-start(f32[2,2,4,5,8,128]{5,4,3,2,1,0:T(8,128)S(1)} %get-tuple-element.44), channel_id=1, source_target_pairs={{0,56},{8,16},{16,8},{24,32},{32,24},{40,48},{48,40},{56,0},{1,57}... | collective-permute-start | bytes 983048 | tf_op jit(solution)/shard_map/ppermute | solution.py:265
  64.3 1.3 %collective-permute-start.14 = (f32[2,2,2,4,3,8,128]{6,5,4,3,2,1,0:T(8,128)S(1)}, f32[2,2,2,4,3,8,128]{6,5,4,3,2,1,0:T(8,128)S(1)}, u32[]{:S(2)}, u32[]{:S(2)}) collective-permute-start(f32[2,2,2,4,3,8,128]{6,5,4,3,2,1,0:T(8,128)S(1)} %get-tuple-element.50), channel_id=1, source_target_pairs={{0,4},{4,0},{1,5},{5,1},{2,6},{6,2},{3,7},{7,3},{8,12},{12,8},{9,1... | collective-permute-start | bytes 1179656 | tf_op jit(solution)/shard_map/ppermute | solution.py:269
  65.6 0.0 collective-permute-done.6.refs_1_
  65.6 0.0 collective-permute-done.7.refs_2_
  65.6 0.1 halve.6
  65.7 1.9 %collective-permute-start.8 = (f32[2,2,4,5,8,128]{5,4,3,2,1,0:T(8,128)S(1)}, f32[2,2,4,5,8,128]{5,4,3,2,1,0:T(8,128)S(1)}, u32[]{:S(2)}, u32[]{:S(2)}) collective-permute-start(f32[2,2,4,5,8,128]{5,4,3,2,1,0:T(8,128)S(1)} %get-tuple-element.39), channel_id=1, source_target_pairs={{0,8},{8,0},{1,9},{9,1},{2,10},{10,2},{3,11},{11,3},{4,12},{12,4},... | collective-permute-start | bytes 983048 | tf_op jit(solution)/shard_map/ppermute | solution.py:269
  67.6 0.0 collective-permute-done.10.refs_1_
  67.6 4.2 %collective-permute-done.11.refs_2_ = f32[2,2,4,5,8,128]{5,4,3,2,1,0:T(8,128)S(1)} collective-permute-done((f32[2,2,4,5,8,128]{5,4,3,2,1,0:T(8,128)S(1)}, f32[2,2,4,5,8,128]{5,4,3,2,1,0:T(8,128)S(1)}, u32[]{:S(2)}, u32[]{:S(2)}) %collective-permute-start.11) | collective-permute-done | bytes 327712 | tf_op jit(solution)/shard_map/ppermute | solution.py:265
  71.8 0.1 halve.8
  71.9 1.4 %collective-permute-start.12 = (f32[2,2,4,5,8,128]{5,4,3,2,1,0:T(8,128)S(1)}, f32[2,2,4,5,8,128]{5,4,3,2,1,0:T(8,128)S(1)}, u32[]{:S(2)}, u32[]{:S(2)}) collective-permute-start(f32[2,2,4,5,8,128]{5,4,3,2,1,0:T(8,128)S(1)} %get-tuple-element.46), channel_id=1, source_target_pairs={{0,4},{4,0},{1,5},{5,1},{2,6},{6,2},{3,7},{7,3},{8,12},{12,8},{9,1... | collective-permute-start | bytes 983048 | tf_op jit(solution)/shard_map/ppermute | solution.py:269
  73.3 2.4 %collective-permute-done.14.refs_1_ = f32[2,2,2,4,3,8,128]{6,5,4,3,2,1,0:T(8,128)S(1)} collective-permute-done((f32[2,2,2,4,3,8,128]{6,5,4,3,2,1,0:T(8,128)S(1)}, f32[2,2,2,4,3,8,128]{6,5,4,3,2,1,0:T(8,128)S(1)}, u32[]{:S(2)}, u32[]{:S(2)}) %collective-permute-start.14) | collective-permute-done | bytes 393248 | tf_op jit(solution)/shard_map/ppermute | solution.py:269
  75.7 0.1 halve.10
  75.7 0.7 collective-permute-start.15
  76.4 0.0 collective-permute-done.8.refs_1_
  76.4 0.1 halve.7
  76.5 0.8 collective-permute-start.9
  77.3 5.4 %collective-permute-done.12.refs_1_ = f32[2,2,4,5,8,128]{5,4,3,2,1,0:T(8,128)S(1)} collective-permute-done((f32[2,2,4,5,8,128]{5,4,3,2,1,0:T(8,128)S(1)}, f32[2,2,4,5,8,128]{5,4,3,2,1,0:T(8,128)S(1)}, u32[]{:S(2)}, u32[]{:S(2)}) %collective-permute-start.12) | collective-permute-done | bytes 327712 | tf_op jit(solution)/shard_map/ppermute | solution.py:269
  82.8 0.7 collective-permute-start.13
  83.4 0.0 collective-permute-done.15.refs_1_
  83.5 0.1 collective-permute-start.16
  83.6 4.6 %collective-permute-done.16 = f32[2,4,3,8,128]{4,3,2,1,0:T(8,128)S(1)} collective-permute-done((f32[2,4,3,8,128]{4,3,2,1,0:T(8,128)S(1)}, f32[2,4,3,8,128]{4,3,2,1,0:T(8,128)S(1)}, u32[]{:S(2)}, u32[]{:S(2)}) %collective-permute-start.16) | collective-permute-done | bytes 98336 | tf_op jit(solution)/shard_map/ppermute | solution.py:269
  88.2 0.0 collective-permute-done.9
  88.2 0.0 collective-permute-done.13
  88.3 18.6 %all_to_all.5.in_ref = f32[8,13,8,128]{3,2,1,0:T(8,128)S(1)} all-to-all(f32[8,13,8,128]{3,2,1,0:T(8,128)S(1)} %pad_maximum_fusion), channel_id=1, replica_groups=mesh['xh'=2,'xl'=2,'zh'=4,'zl'=2,'yl'=2,'yh'=2,'c'=2] {'xh','zh'}, dimensions={0} | all-to-all | bytes 851968 | tf_op jit(solution)/shard_map/all_to_all | solution.py:307
  106.9 0.7 place.1
  (14 shorter events, 0.3 us)
Async XLA Ops:
  0.0 26.6 %collective-permute-start.4 = (f32[16,128,128]{2,1,0:T(8,128)}, f32[16,128,128]{2,1,0:T(8,128)S(1)}, u32[]{:S(2)}, u32[]{:S(2)}) collective-permute-start(f32[16,128,128]{2,1,0:T(8,128)} %c0_ref.1), channel_id=1, source_target_pairs={{0,2},{2,0},{1,3},{3,1},{4,6},{6,4},{5,7},{7,5},{8,10},{10,8},{9,1... | collective-permute-start | bytes 3145736 | tf_op jit(solution)/shard_map/ppermute | solution.py:269
  2.0 1.9 %copy-start = (f32[16,128,3,128]{3,1,2,0:T(8,128)S(1)}, f32[16,128,3,128]{3,1,2,0:T(8,128)}, u32[]{:S(2)}) copy-start(f32[16,128,3,128]{3,1,2,0:T(8,128)} %param.8) | copy-start | bytes 9437188
  3.9 0.9 copy-start.2
  4.8 5.0 %copy-start.1 = (f32[16,128,128]{2,1,0:T(8,128)S(1)}, f32[16,128,128]{2,1,0:T(8,128)}, u32[]{:S(2)}) copy-start(f32[16,128,128]{2,1,0:T(8,128)} %c0_ref.1) | copy-start | bytes 3145732
  9.7 35.2 %copy-start.4 = (s32[64]{0:T(128)S(1)}, s32[64]{0:T(128)}, u32[]{:S(2)}) copy-start(s32[64]{0:T(128)} %counts_ref.3) | copy-start | bytes 772
  9.7 21.8 %collective-permute-start = (f32[8,96,128]{2,1,0:T(8,128)S(1)}, f32[8,96,128]{2,1,0:T(8,128)S(1)}, u32[]{:S(2)}, u32[]{:S(2)}) collective-permute-start(f32[8,96,128]{2,1,0:T(8,128)S(1)} %coupling.3), channel_id=1, source_target_pairs={{0,1},{1,0},{2,3},{3,2},{4,5},{5,4},{6,7},{7,6},{8,9},{9,8},{10,11... | collective-permute-start | bytes 1179656 | tf_op jit(solution)/shard_map/ppermute | solution.py:269
  9.8 35.0 %collective-permute-start.3 = (f32[16,128,128]{2,1,0:T(8,128)S(1)}, f32[16,128,128]{2,1,0:T(8,128)S(1)}, u32[]{:S(2)}, u32[]{:S(2)}) collective-permute-start(f32[16,128,128]{2,1,0:T(8,128)S(1)} %copy-done.1), channel_id=1, source_target_pairs={{0,1},{1,0},{2,3},{3,2},{4,5},{5,4},{6,7},{7,6},{8,9},{9,8},{10,11... | collective-permute-start | bytes 3145736 | tf_op jit(solution)/shard_map/ppermute | solution.py:269
  26.6 18.2 %collective-permute-start.5 = (f32[16,128,128]{2,1,0:T(8,128)S(1)}, f32[16,128,128]{2,1,0:T(8,128)S(1)}, u32[]{:S(2)}, u32[]{:S(2)}) collective-permute-start(f32[16,128,128]{2,1,0:T(8,128)S(1)} %collective-permute-done.4.c2_ref), channel_id=1, source_target_pairs={{0,1},{1,0},{2,3},{3,2},{4,5},{5,4},{6,7},{7,6},{8,9},{9,8},{10,11... | collective-permute-start | bytes 3145736 | tf_op jit(solution)/shard_map/ppermute | solution.py:269
  31.5 13.1 %collective-permute-start.1 = (f32[8,96,128]{2,1,0:T(8,128)S(1)}, f32[8,96,128]{2,1,0:T(8,128)S(1)}, u32[]{:S(2)}, u32[]{:S(2)}) collective-permute-start(f32[8,96,128]{2,1,0:T(8,128)S(1)} %add.15), channel_id=1, source_target_pairs={{0,2},{2,0},{1,3},{3,1},{4,6},{6,4},{5,7},{7,5},{8,10},{10,8},{9,1... | collective-permute-start | bytes 1179656 | tf_op jit(solution)/shard_map/ppermute | solution.py:269
  44.7 1.8 %copy-start.3 = (s32[1024,4]{0,1:T(4,128)S(1)}, s32[1024,4]{0,1:T(4,128)}, u32[]{:S(2)}) copy-start(s32[1024,4]{0,1:T(4,128)} %param.6) | copy-start | bytes 49156
  44.7 1.8 %collective-permute-start.2 = (f32[8,96,128]{2,1,0:T(8,128)S(1)}, f32[8,96,128]{2,1,0:T(8,128)S(1)}, u32[]{:S(2)}, u32[]{:S(2)}) collective-permute-start(f32[8,96,128]{2,1,0:T(8,128)S(1)} %add.16.own_ref), channel_id=1, source_target_pairs={{0,1},{1,0},{2,3},{3,2},{4,5},{5,4},{6,7},{7,6},{8,9},{9,8},{10,11... | collective-permute-start | bytes 1179656 | tf_op jit(solution)/shard_map/ppermute | solution.py:269
  50.2 15.3 %collective-permute-start.6 = (f32[2,2,4,5,8,128]{5,4,3,2,1,0:T(8,128)S(1)}, f32[2,2,4,5,8,128]{5,4,3,2,1,0:T(8,128)S(1)}, u32[]{:S(2)}, u32[]{:S(2)}) collective-permute-start(f32[2,2,4,5,8,128]{5,4,3,2,1,0:T(8,128)S(1)} %get-tuple-element.36), channel_id=1, source_target_pairs={{0,64},{64,0},{1,65},{65,1},{2,66},{66,2},{3,67},{67,3},{4,68},{68... | collective-permute-start | bytes 983048 | tf_op jit(solution)/shard_map/ppermute | solution.py:269
  51.8 13.8 %collective-permute-start.7 = (f32[2,2,4,5,8,128]{5,4,3,2,1,0:T(8,128)S(1)}, f32[2,2,4,5,8,128]{5,4,3,2,1,0:T(8,128)S(1)}, u32[]{:S(2)}, u32[]{:S(2)}) collective-permute-start(f32[2,2,4,5,8,128]{5,4,3,2,1,0:T(8,128)S(1)} %get-tuple-element.37), channel_id=1, source_target_pairs={{0,192},{64,128},{128,64},{192,0},{1,193},{65,129},{129,65},{193,1... | collective-permute-start | bytes 983048 | tf_op jit(solution)/shard_map/ppermute | solution.py:265
  57.4 10.2 %collective-permute-start.10 = (f32[2,2,4,5,8,128]{5,4,3,2,1,0:T(8,128)S(1)}, f32[2,2,4,5,8,128]{5,4,3,2,1,0:T(8,128)S(1)}, u32[]{:S(2)}, u32[]{:S(2)}) collective-permute-start(f32[2,2,4,5,8,128]{5,4,3,2,1,0:T(8,128)S(1)} %get-tuple-element.43), channel_id=1, source_target_pairs={{0,8},{8,0},{1,9},{9,1},{2,10},{10,2},{3,11},{11,3},{4,12},{12,4},... | collective-permute-start | bytes 983048 | tf_op jit(solution)/shard_map/ppermute | solution.py:269
  59.3 12.4 %collective-permute-start.11 = (f32[2,2,4,5,8,128]{5,4,3,2,1,0:T(8,128)S(1)}, f32[2,2,4,5,8,128]{5,4,3,2,1,0:T(8,128)S(1)}, u32[]{:S(2)}, u32[]{:S(2)}) collective-permute-start(f32[2,2,4,5,8,128]{5,4,3,2,1,0:T(8,128)S(1)} %get-tuple-element.44), channel_id=1, source_target_pairs={{0,56},{8,16},{16,8},{24,32},{32,24},{40,48},{48,40},{56,0},{1,57}... | collective-permute-start | bytes 983048 | tf_op jit(solution)/shard_map/ppermute | solution.py:265
  64.3 11.4 %collective-permute-start.14 = (f32[2,2,2,4,3,8,128]{6,5,4,3,2,1,0:T(8,128)S(1)}, f32[2,2,2,4,3,8,128]{6,5,4,3,2,1,0:T(8,128)S(1)}, u32[]{:S(2)}, u32[]{:S(2)}) collective-permute-start(f32[2,2,2,4,3,8,128]{6,5,4,3,2,1,0:T(8,128)S(1)} %get-tuple-element.50), channel_id=1, source_target_pairs={{0,4},{4,0},{1,5},{5,1},{2,6},{6,2},{3,7},{7,3},{8,12},{12,8},{9,1... | collective-permute-start | bytes 1179656 | tf_op jit(solution)/shard_map/ppermute | solution.py:269
  65.7 10.7 %collective-permute-start.8 = (f32[2,2,4,5,8,128]{5,4,3,2,1,0:T(8,128)S(1)}, f32[2,2,4,5,8,128]{5,4,3,2,1,0:T(8,128)S(1)}, u32[]{:S(2)}, u32[]{:S(2)}) collective-permute-start(f32[2,2,4,5,8,128]{5,4,3,2,1,0:T(8,128)S(1)} %get-tuple-element.39), channel_id=1, source_target_pairs={{0,8},{8,0},{1,9},{9,1},{2,10},{10,2},{3,11},{11,3},{4,12},{12,4},... | collective-permute-start | bytes 983048 | tf_op jit(solution)/shard_map/ppermute | solution.py:269
  71.9 10.8 %collective-permute-start.12 = (f32[2,2,4,5,8,128]{5,4,3,2,1,0:T(8,128)S(1)}, f32[2,2,4,5,8,128]{5,4,3,2,1,0:T(8,128)S(1)}, u32[]{:S(2)}, u32[]{:S(2)}) collective-permute-start(f32[2,2,4,5,8,128]{5,4,3,2,1,0:T(8,128)S(1)} %get-tuple-element.46), channel_id=1, source_target_pairs={{0,4},{4,0},{1,5},{5,1},{2,6},{6,2},{3,7},{7,3},{8,12},{12,8},{9,1... | collective-permute-start | bytes 983048 | tf_op jit(solution)/shard_map/ppermute | solution.py:269
  75.7 7.7 %collective-permute-start.15 = (f32[2,2,4,3,8,128]{5,4,3,2,1,0:T(8,128)S(1)}, f32[2,2,4,3,8,128]{5,4,3,2,1,0:T(8,128)S(1)}, u32[]{:S(2)}, u32[]{:S(2)}) collective-permute-start(f32[2,2,4,3,8,128]{5,4,3,2,1,0:T(8,128)S(1)} %get-tuple-element.52), channel_id=1, source_target_pairs={{0,64},{64,0},{1,65},{65,1},{2,66},{66,2},{3,67},{67,3},{4,68},{68... | collective-permute-start | bytes 589832 | tf_op jit(solution)/shard_map/ppermute | solution.py:269
  76.5 11.7 %collective-permute-start.9 = (f32[2,4,5,8,128]{4,3,2,1,0:T(8,128)S(1)}, f32[2,4,5,8,128]{4,3,2,1,0:T(8,128)S(1)}, u32[]{:S(2)}, u32[]{:S(2)}) collective-permute-start(f32[2,4,5,8,128]{4,3,2,1,0:T(8,128)S(1)} %get-tuple-element.41), channel_id=1, source_target_pairs={{0,4},{4,0},{1,5},{5,1},{2,6},{6,2},{3,7},{7,3},{8,12},{12,8},{9,1... | collective-permute-start | bytes 491528 | tf_op jit(solution)/shard_map/ppermute | solution.py:269
  82.8 5.5 %collective-permute-start.13 = (f32[2,4,5,8,128]{4,3,2,1,0:T(8,128)S(1)}, f32[2,4,5,8,128]{4,3,2,1,0:T(8,128)S(1)}, u32[]{:S(2)}, u32[]{:S(2)}) collective-permute-start(f32[2,4,5,8,128]{4,3,2,1,0:T(8,128)S(1)} %get-tuple-element.48), channel_id=1, source_target_pairs={{0,64},{64,0},{1,65},{65,1},{2,66},{66,2},{3,67},{67,3},{4,68},{68... | collective-permute-start | bytes 491528 | tf_op jit(solution)/shard_map/ppermute | solution.py:269
  83.5 4.7 %collective-permute-start.16 = (f32[2,4,3,8,128]{4,3,2,1,0:T(8,128)S(1)}, f32[2,4,3,8,128]{4,3,2,1,0:T(8,128)S(1)}, u32[]{:S(2)}, u32[]{:S(2)}) collective-permute-start(f32[2,4,3,8,128]{4,3,2,1,0:T(8,128)S(1)} %get-tuple-element.54), channel_id=1, source_target_pairs={{0,8},{8,0},{1,9},{9,1},{2,10},{10,2},{3,11},{11,3},{4,12},{12,4},... | collective-permute-start | bytes 294920 | tf_op jit(solution)/shard_map/ppermute | solution.py:269

commit v9 on v7

--- a/solution.py
+++ b/solution.py
@@ -10,6 +10,7 @@
 SLOTS = 16
 HALF = SLOTS // 2
 CHUNK = 4
+PACKED = 3 * W // 4
 GT = 4
 NXH, NXL, NZH, NZL, NYL = 2, 2, 4, 2, 2
 GROUPS = (("xl", "zl", "yl", GT + 1), ("zl", "yl", "xl", GT), ("yl", "xl", "zl", GT))
@@ -56,7 +57,10 @@
             pairs.append((split(weighted), split(pts[k])))
         left = jnp.concatenate([w[0] for w, _ in pairs] + [w[0] for w, _ in pairs] + [w[1] for w, _ in pairs], axis=1)
         right = jnp.concatenate([p[0] for _, p in pairs] + [p[1] for _, p in pairs] + [p[0] for _, p in pairs], axis=1)
-        out_ref[i] = lax.dot_general(left, right, (((1,), (1,)), ((), ())), preferred_element_type=F32)
+        full = lax.dot_general(left, right, (((1,), (1,)), ((), ())), preferred_element_type=F32)
+        out_ref[i, : W // 2] = full[: W // 2]
+        out_ref[i, W // 2 :, : W // 2] = full[W // 2 : PACKED, W // 2 :]
+        out_ref[i, W // 2 :, W // 2 :] = full[PACKED:, W // 2 :]
 
 
 def coupling(mine, pts, inv):
@@ -65,7 +69,7 @@
 
     return pl.pallas_call(
         kernel,
-        out_shape=jax.ShapeDtypeStruct((HALF, W, W), F32),
+        out_shape=jax.ShapeDtypeStruct((HALF, PACKED, W), F32),
         in_specs=[HBM, VMEM],
         out_specs=VMEM,
         scratch_shapes=[pltpu.VMEM((HALF, 3, W, W), F32), pltpu.SemaphoreType.DMA((HALF,))],
@@ -126,7 +130,11 @@
         def _():
             for i in range(CHUNK):
                 slot = k * CHUNK + i
-                m_high, m_low = split(jnp.where(core == k // 2, own_ref[slot % HALF], oth_ref[slot % HALF]))
+                packed = jnp.where(core == k // 2, own_ref[slot % HALF], oth_ref[slot % HALF])
+                top, rest = packed[: W // 2], packed[W // 2 :]
+                corner = jnp.concatenate([rest[:, : W // 2], rest[:, W // 2 :]], axis=0)
+                bottom = jnp.concatenate([top[:, W // 2 :].T, corner], axis=1)
+                m_high, m_low = split(jnp.concatenate([top, bottom], axis=0))
                 t_high, t_low = t_high_ref[slot], t_low_ref[slot]
                 prod = jnp.dot(
                     jnp.concatenate([t_high, t_high, t_low], axis=1),

time: 109 us -> 107 us (0.982)
  waiting for transfers between devices: 51.5 us -> 48.5 us
  Pallas kernels: 13.4 us -> 14.5 us
    ppermute x15, waiting for transfers between devices: 50.3 us -> 47.2 us  [swap(): return lax.ppermute(value, axis, [(0, 1), (1, 0)])]
  transfers between devices with their start and end apart: 16 -> 16, of which waited for: 9 -> 9; matrix products, arithmetic and copies ran while one was open for 0% -> 0% of each run, Pallas kernels for 9% -> 10%
where the time goes in v9:
time: 107 us
  waiting for transfers between devices  48.5 us (45%)
  blocking collectives  23.1 us (22%)
  starting transfers between devices  17.4 us (16%)
  Pallas kernels  14.5 us (14%)
  local copies, waits for them, and re-layouts  2.79 us (3%)
    ppermute x15, waiting for transfers between devices, swap(): return lax.ppermute(value, axis, [(0, 1), (1, 0)])  47.2 us
    all_to_all x1, blocking collectives, on_device(): return place(lax.all_to_all(part, ('xh', 'zh'), 0, 0, tiled=True))  23.1 us
    ppermute x15, starting transfers between devices, swap(): return lax.ppermute(value, axis, [(0, 1), (1, 0)])  14.7 us
    pallas_call x2, Pallas kernels, coupling(): pl.pallas_call(kernel, out_shape=jax.ShapeDtypeStruct((HALF, PACKED, W),...  9.72 us
    pallas_call x1, Pallas kernels, schur(): pl.pallas_call(schur_kernel, out_shape=[jax.ShapeDtypeStruct(lead + (2, N...  2.91 us
    unnamed x10, local copies, waits for them, and re-layouts  2.79 us
    ppermute x1, starting transfers between devices, swap_x_other(): lax.ppermute(value, ('xh', 'xl'), [(i, (i + 1 if i % 2 else i - 1) % size...  2.76 us
  transfers between devices with their start and end apart: 16, of which 9 were waited for; matrix products, arithmetic and copies ran while one was open for 0% of the time, Pallas kernels for 10%

profile of v9, /device:TPU:16, one launch (start us, length us, event | category | flops | bytes accessed | tf_op | source)
XLA Modules:
  0.0 106.7 jit_solution(11048130942671947824)
XLA Ops:
  0.0 2.0 %collective-permute-start.4 = (f32[16,128,128]{2,1,0:T(8,128)}, f32[16,128,128]{2,1,0:T(8,128)S(1)}, u32[]{:S(2)}, u32[]{:S(2)}) collective-permute-start(f32[16,128,128]{2,1,0:T(8,128)} %c0_ref.1), channel_id=1, source_target_pairs={{0,2},{2,0},{1,3},{3,1},{4,6},{6,4},{5,7},{7,5},{8,10},{10,8},{9,1... | collective-permute-start | bytes 3145736 | tf_op jit(solution)/shard_map/ppermute | solution.py:265
  2.0 1.9 %copy-done = f32[16,128,3,128]{3,1,2,0:T(8,128)S(1)} copy-done((f32[16,128,3,128]{3,1,2,0:T(8,128)S(1)}, f32[16,128,3,128]{3,1,2,0:T(8,128)}, u32[]{:S(2)}) %copy-start) | copy-done | bytes 3145752
  3.9 0.9 copy-done.2
  4.8 4.9 %coupling.3 = f32[8,96,128]{2,1,0:T(8,128)S(1)} custom-call(f32[16,3,128,128]{3,2,1,0:T(8,128)S(1)} %bitcast.6, f32[3,3,16,128]{3,2,1,0:T(8,128)S(1)} %bitcast.8), custom_call_target="tpu_custom_call" | custom-call | flops 301989888 | bytes 2097152 | tf_op jit(solution)/shard_map/coupling/pallas_call | solution.py:70
  9.7 0.0 copy-start.4
  9.7 0.1 collective-permute-start
  9.8 0.0 copy-done.1
  9.8 0.5 collective-permute-start.3
  10.3 16.3 %collective-permute-done.4.c2_ref = f32[16,128,128]{2,1,0:T(8,128)S(1)} collective-permute-done((f32[16,128,128]{2,1,0:T(8,128)}, f32[16,128,128]{2,1,0:T(8,128)S(1)}, u32[]{:S(2)}, u32[]{:S(2)}) %collective-permute-start.4) | collective-permute-done | bytes 1048608 | tf_op jit(solution)/shard_map/ppermute | solution.py:265
  26.6 0.0 collective-permute-start.5
  26.6 4.9 %coupling.2 = f32[8,96,128]{2,1,0:T(8,128)S(1)} custom-call(f32[16,3,128,128]{3,2,1,0:T(8,128)S(1)} %bitcast.7, f32[3,3,16,128]{3,2,1,0:T(8,128)S(1)} %bitcast.9), custom_call_target="tpu_custom_call" | custom-call | flops 301989888 | bytes 2097152 | tf_op jit(solution)/shard_map/coupling/pallas_call | solution.py:70
  31.5 0.0 collective-permute-done
  31.5 0.4 collective-permute-start.1
  31.9 12.7 %collective-permute-done.1 = f32[8,96,128]{2,1,0:T(8,128)S(1)} collective-permute-done((f32[8,96,128]{2,1,0:T(8,128)S(1)}, f32[8,96,128]{2,1,0:T(8,128)S(1)}, u32[]{:S(2)}, u32[]{:S(2)}) %collective-permute-start.1) | collective-permute-done | bytes 393248 | tf_op jit(solution)/shard_map/ppermute | solution.py:265
  44.7 0.0 copy-start.3
  44.7 0.1 collective-permute-start.2
  44.8 0.0 collective-permute-done.3.c1_ref
  44.8 0.0 collective-permute-done.5.c3_ref
  44.8 0.0 copy-done.4
  44.9 0.8 prepare.1
  45.7 0.8 collective-permute-done.2.oth_ref
  46.5 2.9 %schur.1 = (f32[2,2,4,5,8,128]{5,4,3,2,1,0:T(8,128)S(1)}, f32[2,2,4,5,8,128]{5,4,3,2,1,0:T(8,128)S(1)}, f32[2,2,2,4,5,8,128]{6,5,4,3,2,1,0:T(8,128)S(1)}, f32[2,...) custom-call(s32[64]{0:T(128)S(1)} %copy-done.4, ...), custom_call_target="tpu_custom_call" | custom-call | flops 1006632960 | bytes 5242880 | tf_op jit(solution)/shard_map/schur/pallas_call | solution.py:183
  49.5 2.0 %collective-permute-start.10 = (f32[2,2,2,4,4,8,128]{6,5,4,3,2,1,0:T(8,128)S(1)}, f32[2,2,2,4,4,8,128]{6,5,4,3,2,1,0:T(8,128)S(1)}, u32[]{:S(2)}, u32[]{:S(2)}) collective-permute-start(f32[2,2,2,4,4,8,128]{6,5,4,3,2,1,0:T(8,128)S(1)} %get-tuple-element.42), channel_id=1, source_target_pairs={{0,8},{8,0},{1,9},{9,1},{2,10},{10,2},{3,11},{11,3},{4,12},{12,4},... | collective-permute-start | bytes 1572872 | tf_op jit(solution)/shard_map/ppermute | solution.py:265
  51.4 4.7 %collective-permute-start.13 = (f32[2,2,2,4,4,8,128]{6,5,4,3,2,1,0:T(8,128)S(1)}, f32[2,2,2,4,4,8,128]{6,5,4,3,2,1,0:T(8,128)S(1)}, u32[]{:S(2)}, u32[]{:S(2)}) collective-permute-start(f32[2,2,2,4,4,8,128]{6,5,4,3,2,1,0:T(8,128)S(1)} %get-tuple-element.48), channel_id=1, source_target_pairs={{0,4},{4,0},{1,5},{5,1},{2,6},{6,2},{3,7},{7,3},{8,12},{12,8},{9,1... | collective-permute-start | bytes 1572872 | tf_op jit(solution)/shard_map/ppermute | solution.py:265
  56.1 0.0 collective-permute-start.6
  56.1 2.8 %collective-permute-start.7 = (f32[2,2,4,5,8,128]{5,4,3,2,1,0:T(8,128)S(1)}, f32[2,2,4,5,8,128]{5,4,3,2,1,0:T(8,128)S(1)}, u32[]{:S(2)}, u32[]{:S(2)}) collective-permute-start(f32[2,2,4,5,8,128]{5,4,3,2,1,0:T(8,128)S(1)} %get-tuple-element.36), channel_id=1, source_target_pairs={{0,192},{64,128},{128,64},{192,0},{1,193},{65,129},{129,65},{193,1... | collective-permute-start | bytes 983048 | tf_op jit(solution)/shard_map/ppermute | solution.py:261
  58.9 6.8 %collective-permute-done.6.refs_1_ = f32[2,2,4,5,8,128]{5,4,3,2,1,0:T(8,128)S(1)} collective-permute-done((f32[2,2,4,5,8,128]{5,4,3,2,1,0:T(8,128)S(1)}, f32[2,2,4,5,8,128]{5,4,3,2,1,0:T(8,128)S(1)}, u32[]{:S(2)}, u32[]{:S(2)}) %collective-permute-start.6) | collective-permute-done | bytes 327712 | tf_op jit(solution)/shard_map/ppermute | solution.py:265
  65.7 1.2 %collective-permute-done.7.refs_2_ = f32[2,2,4,5,8,128]{5,4,3,2,1,0:T(8,128)S(1)} collective-permute-done((f32[2,2,4,5,8,128]{5,4,3,2,1,0:T(8,128)S(1)}, f32[2,2,4,5,8,128]{5,4,3,2,1,0:T(8,128)S(1)}, u32[]{:S(2)}, u32[]{:S(2)}) %collective-permute-start.7) | collective-permute-done | bytes 327712 | tf_op jit(solution)/shard_map/ppermute | solution.py:261
  66.9 0.1 halve.6
  67.0 0.5 collective-permute-start.8
  67.5 0.0 collective-permute-done.10.refs_1_
  67.5 0.1 halve.8
  67.6 1.3 %collective-permute-start.11 = (f32[2,2,4,4,8,128]{5,4,3,2,1,0:T(8,128)S(1)}, f32[2,2,4,4,8,128]{5,4,3,2,1,0:T(8,128)S(1)}, u32[]{:S(2)}, u32[]{:S(2)}) collective-permute-start(f32[2,2,4,4,8,128]{5,4,3,2,1,0:T(8,128)S(1)} %get-tuple-element.44), channel_id=1, source_target_pairs={{0,4},{4,0},{1,5},{5,1},{2,6},{6,2},{3,7},{7,3},{8,12},{12,8},{9,1... | collective-permute-start | bytes 786440 | tf_op jit(solution)/shard_map/ppermute | solution.py:265
  68.9 0.0 collective-permute-done.13.refs_1_
  68.9 0.1 halve.10
  69.0 0.5 collective-permute-start.14
  69.5 6.3 %collective-permute-done.8.refs_1_ = f32[2,2,4,5,8,128]{5,4,3,2,1,0:T(8,128)S(1)} collective-permute-done((f32[2,2,4,5,8,128]{5,4,3,2,1,0:T(8,128)S(1)}, f32[2,2,4,5,8,128]{5,4,3,2,1,0:T(8,128)S(1)}, u32[]{:S(2)}, u32[]{:S(2)}) %collective-permute-start.8) | collective-permute-done | bytes 327712 | tf_op jit(solution)/shard_map/ppermute | solution.py:265
  75.8 0.1 halve.7
  75.9 1.2 %collective-permute-start.9 = (f32[2,4,5,8,128]{4,3,2,1,0:T(8,128)S(1)}, f32[2,4,5,8,128]{4,3,2,1,0:T(8,128)S(1)}, u32[]{:S(2)}, u32[]{:S(2)}) collective-permute-start(f32[2,4,5,8,128]{4,3,2,1,0:T(8,128)S(1)} %get-tuple-element.40), channel_id=1, source_target_pairs={{0,4},{4,0},{1,5},{5,1},{2,6},{6,2},{3,7},{7,3},{8,12},{12,8},{9,1... | collective-permute-start | bytes 491528 | tf_op jit(solution)/shard_map/ppermute | solution.py:265
  77.0 0.0 collective-permute-done.11.refs_1_
  77.1 0.7 collective-permute-start.12
  77.8 0.0 collective-permute-done.14.refs_1_
  77.8 0.7 collective-permute-start.15
  78.6 2.7 %collective-permute-done.9 = f32[2,4,5,8,128]{4,3,2,1,0:T(8,128)S(1)} collective-permute-done((f32[2,4,5,8,128]{4,3,2,1,0:T(8,128)S(1)}, f32[2,4,5,8,128]{4,3,2,1,0:T(8,128)S(1)}, u32[]{:S(2)}, u32[]{:S(2)}) %collective-permute-start.9) | collective-permute-done | bytes 163872 | tf_op jit(solution)/shard_map/ppermute | solution.py:265
  81.3 0.8 collective-permute-done.12
  82.1 0.8 collective-permute-done.15
  82.9 23.1 %all_to_all.5.in_ref = f32[8,13,8,128]{3,2,1,0:T(8,128)S(1)} all-to-all(f32[8,13,8,128]{3,2,1,0:T(8,128)S(1)} %pad_maximum_fusion), channel_id=1, replica_groups=mesh['xh'=2,'xl'=2,'zh'=4,'zl'=2,'yl'=2,'yh'=2,'c'=2] {'xh','zh'}, dimensions={0} | all-to-all | bytes 851968 | tf_op jit(solution)/shard_map/all_to_all | solution.py:302
  106.0 0.7 place.1
  (12 shorter events, 0.3 us)
Async XLA Ops:
  0.0 26.6 %collective-permute-start.4 = (f32[16,128,128]{2,1,0:T(8,128)}, f32[16,128,128]{2,1,0:T(8,128)S(1)}, u32[]{:S(2)}, u32[]{:S(2)}) collective-permute-start(f32[16,128,128]{2,1,0:T(8,128)} %c0_ref.1), channel_id=1, source_target_pairs={{0,2},{2,0},{1,3},{3,1},{4,6},{6,4},{5,7},{7,5},{8,10},{10,8},{9,1... | collective-permute-start | bytes 3145736 | tf_op jit(solution)/shard_map/ppermute | solution.py:265
  2.0 1.9 %copy-start = (f32[16,128,3,128]{3,1,2,0:T(8,128)S(1)}, f32[16,128,3,128]{3,1,2,0:T(8,128)}, u32[]{:S(2)}) copy-start(f32[16,128,3,128]{3,1,2,0:T(8,128)} %param.8) | copy-start | bytes 9437188
  3.9 0.9 copy-start.2
  4.8 5.0 %copy-start.1 = (f32[16,128,128]{2,1,0:T(8,128)S(1)}, f32[16,128,128]{2,1,0:T(8,128)}, u32[]{:S(2)}) copy-start(f32[16,128,128]{2,1,0:T(8,128)} %c0_ref.1) | copy-start | bytes 3145732
  9.7 35.2 %copy-start.4 = (s32[64]{0:T(128)S(1)}, s32[64]{0:T(128)}, u32[]{:S(2)}) copy-start(s32[64]{0:T(128)} %counts_ref.3) | copy-start | bytes 772
  9.7 21.8 %collective-permute-start = (f32[8,96,128]{2,1,0:T(8,128)S(1)}, f32[8,96,128]{2,1,0:T(8,128)S(1)}, u32[]{:S(2)}, u32[]{:S(2)}) collective-permute-start(f32[8,96,128]{2,1,0:T(8,128)S(1)} %coupling.3), channel_id=1, source_target_pairs={{0,1},{1,0},{2,3},{3,2},{4,5},{5,4},{6,7},{7,6},{8,9},{9,8},{10,11... | collective-permute-start | bytes 1179656 | tf_op jit(solution)/shard_map/ppermute | solution.py:265
  9.8 35.0 %collective-permute-start.3 = (f32[16,128,128]{2,1,0:T(8,128)S(1)}, f32[16,128,128]{2,1,0:T(8,128)S(1)}, u32[]{:S(2)}, u32[]{:S(2)}) collective-permute-start(f32[16,128,128]{2,1,0:T(8,128)S(1)} %copy-done.1), channel_id=1, source_target_pairs={{0,1},{1,0},{2,3},{3,2},{4,5},{5,4},{6,7},{7,6},{8,9},{9,8},{10,11... | collective-permute-start | bytes 3145736 | tf_op jit(solution)/shard_map/ppermute | solution.py:265
  26.6 18.2 %collective-permute-start.5 = (f32[16,128,128]{2,1,0:T(8,128)S(1)}, f32[16,128,128]{2,1,0:T(8,128)S(1)}, u32[]{:S(2)}, u32[]{:S(2)}) collective-permute-start(f32[16,128,128]{2,1,0:T(8,128)S(1)} %collective-permute-done.4.c2_ref), channel_id=1, source_target_pairs={{0,1},{1,0},{2,3},{3,2},{4,5},{5,4},{6,7},{7,6},{8,9},{9,8},{10,11... | collective-permute-start | bytes 3145736 | tf_op jit(solution)/shard_map/ppermute | solution.py:265
  31.5 13.1 %collective-permute-start.1 = (f32[8,96,128]{2,1,0:T(8,128)S(1)}, f32[8,96,128]{2,1,0:T(8,128)S(1)}, u32[]{:S(2)}, u32[]{:S(2)}) collective-permute-start(f32[8,96,128]{2,1,0:T(8,128)S(1)} %add.15), channel_id=1, source_target_pairs={{0,2},{2,0},{1,3},{3,1},{4,6},{6,4},{5,7},{7,5},{8,10},{10,8},{9,1... | collective-permute-start | bytes 1179656 | tf_op jit(solution)/shard_map/ppermute | solution.py:265
  44.7 1.8 %copy-start.3 = (s32[1024,4]{0,1:T(4,128)S(1)}, s32[1024,4]{0,1:T(4,128)}, u32[]{:S(2)}) copy-start(s32[1024,4]{0,1:T(4,128)} %param.6) | copy-start | bytes 49156
  44.7 1.8 %collective-permute-start.2 = (f32[8,96,128]{2,1,0:T(8,128)S(1)}, f32[8,96,128]{2,1,0:T(8,128)S(1)}, u32[]{:S(2)}, u32[]{:S(2)}) collective-permute-start(f32[8,96,128]{2,1,0:T(8,128)S(1)} %add.16.own_ref), channel_id=1, source_target_pairs={{0,1},{1,0},{2,3},{3,2},{4,5},{5,4},{6,7},{7,6},{8,9},{9,8},{10,11... | collective-permute-start | bytes 1179656 | tf_op jit(solution)/shard_map/ppermute | solution.py:265
  49.5 18.0 %collective-permute-start.10 = (f32[2,2,2,4,4,8,128]{6,5,4,3,2,1,0:T(8,128)S(1)}, f32[2,2,2,4,4,8,128]{6,5,4,3,2,1,0:T(8,128)S(1)}, u32[]{:S(2)}, u32[]{:S(2)}) collective-permute-start(f32[2,2,2,4,4,8,128]{6,5,4,3,2,1,0:T(8,128)S(1)} %get-tuple-element.42), channel_id=1, source_target_pairs={{0,8},{8,0},{1,9},{9,1},{2,10},{10,2},{3,11},{11,3},{4,12},{12,4},... | collective-permute-start | bytes 1572872 | tf_op jit(solution)/shard_map/ppermute | solution.py:265
  51.4 17.5 %collective-permute-start.13 = (f32[2,2,2,4,4,8,128]{6,5,4,3,2,1,0:T(8,128)S(1)}, f32[2,2,2,4,4,8,128]{6,5,4,3,2,1,0:T(8,128)S(1)}, u32[]{:S(2)}, u32[]{:S(2)}) collective-permute-start(f32[2,2,2,4,4,8,128]{6,5,4,3,2,1,0:T(8,128)S(1)} %get-tuple-element.48), channel_id=1, source_target_pairs={{0,4},{4,0},{1,5},{5,1},{2,6},{6,2},{3,7},{7,3},{8,12},{12,8},{9,1... | collective-permute-start | bytes 1572872 | tf_op jit(solution)/shard_map/ppermute | solution.py:265
  56.1 9.5 %collective-permute-start.6 = (f32[2,2,4,5,8,128]{5,4,3,2,1,0:T(8,128)S(1)}, f32[2,2,4,5,8,128]{5,4,3,2,1,0:T(8,128)S(1)}, u32[]{:S(2)}, u32[]{:S(2)}) collective-permute-start(f32[2,2,4,5,8,128]{5,4,3,2,1,0:T(8,128)S(1)} %get-tuple-element.35), channel_id=1, source_target_pairs={{0,64},{64,0},{1,65},{65,1},{2,66},{66,2},{3,67},{67,3},{4,68},{68... | collective-permute-start | bytes 983048 | tf_op jit(solution)/shard_map/ppermute | solution.py:265
  56.1 10.8 %collective-permute-start.7 = (f32[2,2,4,5,8,128]{5,4,3,2,1,0:T(8,128)S(1)}, f32[2,2,4,5,8,128]{5,4,3,2,1,0:T(8,128)S(1)}, u32[]{:S(2)}, u32[]{:S(2)}) collective-permute-start(f32[2,2,4,5,8,128]{5,4,3,2,1,0:T(8,128)S(1)} %get-tuple-element.36), channel_id=1, source_target_pairs={{0,192},{64,128},{128,64},{192,0},{1,193},{65,129},{129,65},{193,1... | collective-permute-start | bytes 983048 | tf_op jit(solution)/shard_map/ppermute | solution.py:261
  67.0 8.8 %collective-permute-start.8 = (f32[2,2,4,5,8,128]{5,4,3,2,1,0:T(8,128)S(1)}, f32[2,2,4,5,8,128]{5,4,3,2,1,0:T(8,128)S(1)}, u32[]{:S(2)}, u32[]{:S(2)}) collective-permute-start(f32[2,2,4,5,8,128]{5,4,3,2,1,0:T(8,128)S(1)} %get-tuple-element.38), channel_id=1, source_target_pairs={{0,8},{8,0},{1,9},{9,1},{2,10},{10,2},{3,11},{11,3},{4,12},{12,4},... | collective-permute-start | bytes 983048 | tf_op jit(solution)/shard_map/ppermute | solution.py:265
  67.6 9.4 %collective-permute-start.11 = (f32[2,2,4,4,8,128]{5,4,3,2,1,0:T(8,128)S(1)}, f32[2,2,4,4,8,128]{5,4,3,2,1,0:T(8,128)S(1)}, u32[]{:S(2)}, u32[]{:S(2)}) collective-permute-start(f32[2,2,4,4,8,128]{5,4,3,2,1,0:T(8,128)S(1)} %get-tuple-element.44), channel_id=1, source_target_pairs={{0,4},{4,0},{1,5},{5,1},{2,6},{6,2},{3,7},{7,3},{8,12},{12,8},{9,1... | collective-permute-start | bytes 786440 | tf_op jit(solution)/shard_map/ppermute | solution.py:265
  69.0 8.8 %collective-permute-start.14 = (f32[2,2,4,4,8,128]{5,4,3,2,1,0:T(8,128)S(1)}, f32[2,2,4,4,8,128]{5,4,3,2,1,0:T(8,128)S(1)}, u32[]{:S(2)}, u32[]{:S(2)}) collective-permute-start(f32[2,2,4,4,8,128]{5,4,3,2,1,0:T(8,128)S(1)} %get-tuple-element.50), channel_id=1, source_target_pairs={{0,64},{64,0},{1,65},{65,1},{2,66},{66,2},{3,67},{67,3},{4,68},{68... | collective-permute-start | bytes 786440 | tf_op jit(solution)/shard_map/ppermute | solution.py:265
  75.9 5.4 %collective-permute-start.9 = (f32[2,4,5,8,128]{4,3,2,1,0:T(8,128)S(1)}, f32[2,4,5,8,128]{4,3,2,1,0:T(8,128)S(1)}, u32[]{:S(2)}, u32[]{:S(2)}) collective-permute-start(f32[2,4,5,8,128]{4,3,2,1,0:T(8,128)S(1)} %get-tuple-element.40), channel_id=1, source_target_pairs={{0,4},{4,0},{1,5},{5,1},{2,6},{6,2},{3,7},{7,3},{8,12},{12,8},{9,1... | collective-permute-start | bytes 491528 | tf_op jit(solution)/shard_map/ppermute | solution.py:265
  77.1 5.1 %collective-permute-start.12 = (f32[2,4,4,8,128]{4,3,2,1,0:T(8,128)S(1)}, f32[2,4,4,8,128]{4,3,2,1,0:T(8,128)S(1)}, u32[]{:S(2)}, u32[]{:S(2)}) collective-permute-start(f32[2,4,4,8,128]{4,3,2,1,0:T(8,128)S(1)} %get-tuple-element.46), channel_id=1, source_target_pairs={{0,64},{64,0},{1,65},{65,1},{2,66},{66,2},{3,67},{67,3},{4,68},{68... | collective-permute-start | bytes 393224 | tf_op jit(solution)/shard_map/ppermute | solution.py:265
  77.8 5.1 %collective-permute-start.15 = (f32[2,4,4,8,128]{4,3,2,1,0:T(8,128)S(1)}, f32[2,4,4,8,128]{4,3,2,1,0:T(8,128)S(1)}, u32[]{:S(2)}, u32[]{:S(2)}) collective-permute-start(f32[2,4,4,8,128]{4,3,2,1,0:T(8,128)S(1)} %get-tuple-element.52), channel_id=1, source_target_pairs={{0,8},{8,0},{1,9},{9,1},{2,10},{10,2},{3,11},{11,3},{4,12},{12,4},... | collective-permute-start | bytes 393224 | tf_op jit(solution)/shard_map/ppermute | solution.py:265
